TPU v7x, 32 devices: a whole 2x2x4 slice. The times are simulated.
32 devices in a mesh: groups: 2 (over y), tm: 4 (over z), tile: 2 (over x), chan: 2 (over core).
Axes of the slice: x: 2, y: 2, z: 4, core: 2. Of those that a mesh axis runs over, the one named last changes fastest.
Arguments:
- latent: bfloat16 [16, 24, 32, 512], P(('groups', 'tm'), None, 'tile', 'chan'), parts along dimension 0, may hold values from -110 to 110
- gn_gain: bfloat16 [512], P('chan'), may hold values from 0.099609375 to 1.8984375
- gn_bias: bfloat16 [512], P('chan'), may hold values from -3 to 3
- conv_weight: bfloat16 [27, 512, 512], P(None, 'tm', 'chan'), may hold values from -0.0546875 to 0.0546875
- conv_bias: bfloat16 [512], P('chan'), may hold values from -3 to 3
Outputs:
- decoded: bfloat16 [16, 24, 32, 512], P(('groups', 'tm'), None, 'tile', 'chan'), parts along dimension 0
There are 2 independent parts, one for each index of `groups`. A program takes and returns all parts, laid end to end along the dimension named above; an argument that names none is the same for every part. Nothing has to cross between parts.
All inputs are finite; a program needn't handle non-finite values.
Results may differ from a plain program's by a relative error of at most 0.0043.
Values may be sent and summed in bfloat16 or wider, within the bound.
No kernel may reach another device: no remote copies, remote signals or barrier semaphores. Data moves between devices by JAX's collectives and lax.ppermute only.
A program may use at most 128 MiB of HBM per device.

v0:
```python
import jax
import jax.numpy as jnp
from jax import lax
from jax.sharding import PartitionSpec as P

CH = 512
GROUPS = 32


def shifted(block, axis, distance):
    devices = range(lax.axis_size(axis))
    route = [(i - distance, i) for i in devices if i - distance in devices]
    return lax.ppermute(block, axis, route)


def extended_2(cells, sides, width):
    for axis, dim in sides:
        count = lax.axis_size(axis)
        ends = count - 1
        head = lax.slice_in_dim(cells, 0, width, axis=dim)
        tail = lax.slice_in_dim(cells, cells.shape[dim] - width, cells.shape[dim], axis=dim)
        cells = jnp.concatenate(
            [
                lax.ppermute(tail, axis, [(i, (i + 1) % count) for i in range(ends)]),
                cells,
                lax.ppermute(head, axis, [((i + 1) % count, i) for i in range(ends)]),
            ],
            axis=dim,
        )
    return cells


def normalize(latent, gn_gain, gn_bias):
    values = latent.astype(jnp.float32)
    n_frames, n_rows, n_cols, n_chans = latent.shape
    group_ch = CH // GROUPS
    local_groups = n_chans // group_ch
    shaped = values.reshape(n_frames, n_rows, n_cols, local_groups, group_ch)
    part_sum = jnp.sum(shaped, axis=(0, 1, 2, 4))
    part_square = jnp.sum(shaped * shaped, axis=(0, 1, 2, 4))
    total_sum, total_square = lax.psum((part_sum, part_square), ("tm", "tile"))
    entries = n_frames * n_rows * n_cols * group_ch * lax.axis_size("tm") * lax.axis_size("tile")
    mean_grp = total_sum / entries
    square_grp = total_square / entries
    inv_grp = lax.rsqrt(square_grp - mean_grp * mean_grp + 1e-06)
    mean_ch = jnp.repeat(mean_grp, group_ch)
    inv_ch = jnp.repeat(inv_grp, group_ch)
    scaled = (values - mean_ch) * inv_ch * gn_gain.astype(jnp.float32) + gn_bias.astype(jnp.float32)
    return jax.nn.silu(scaled).astype(jnp.bfloat16)


def conv_term(padded, n_frames, n_rows, n_cols, block_in):
    width_in = block_in.shape[1]
    columns = [
        padded[
            time_off : time_off + n_frames, row_off : row_off + n_rows, col_off : col_off + n_cols
        ]
        for time_off in range(3)
        for row_off in range(3)
        for col_off in range(3)
    ]
    stacked = jnp.stack(columns, axis=3).reshape(n_frames * n_rows * n_cols, 27 * width_in)
    matrix = block_in.reshape(27 * width_in, block_in.shape[2])
    return jnp.dot(stacked, matrix, preferred_element_type=jnp.float32)


def body(latent, gn_gain, gn_bias, conv_weight, conv_bias):
    n_frames, n_rows, n_cols, n_chans = latent.shape
    normed = normalize(latent, gn_gain, gn_bias)
    full_feat = lax.all_gather(normed, "chan", axis=3, tiled=True)
    earlier = shifted(full_feat, "tm", 1)
    extended = jnp.concatenate([earlier, full_feat], axis=0)
    rimmed = extended_2(extended, (("tile", 2),), 1)
    padded = jnp.pad(rimmed, ((0, 0), (1, 1), (0, 0), (0, 0)))
    summed = conv_term(
        padded, n_frames, n_rows, n_cols, lax.all_gather(conv_weight, "tm", axis=1, tiled=True)
    )
    result = (summed + conv_bias.astype(jnp.float32)).astype(jnp.bfloat16)
    return result.reshape(n_frames, n_rows, n_cols, n_chans)


def solution(mesh):
    in_specs = (
        P(("groups", "tm"), None, "tile", "chan"),
        P("chan"),
        P("chan"),
        P(None, "tm", "chan"),
        P("chan"),
    )
    out_specs = P(("groups", "tm"), None, "tile", "chan")
    return jax.shard_map(body, mesh=mesh, in_specs=in_specs, out_specs=out_specs, check_vma=False)
```

profile of v0, /device:TPU:24, one launch (start us, length us, event | category | flops | bytes accessed | tf_op | source)
XLA Modules:
  0.0 189.5 jit_solution(16114364875621279084)
XLA Ops:
  7.3 1.1 convert_reduce_fusion
  8.8 16.9 %all-reduce.1 = (f32[16]{0:T(128)S(1)}, f32[16]{0:T(128)S(1)}) all-reduce(f32[16]{0:T(128)S(1)} %reduce_sum.37, f32[16]{0:T(128)S(1)} %reduce_sum.25), channel_id=1, replica_groups=mesh['groups'=2,'tm'=4,'tile'=2,'chan'=2] {'tm','tile'}, use_global_device_ids=true, to_apply=%region_5.6 | all-reduce | flops 32 | bytes 256 | tf_op jit(solution)/shard_map/psum | solution.py:41
  27.3 1.3 fusion.15
  28.6 2.4 %all_gather.6 = bf16[2,24,16,512]{3,2,1,0:T(8,128)(2,1)S(1)} all-gather(bf16[2,24,16,256]{3,2,1,0:T(8,128)(2,1)S(1)} %fusion.15), channel_id=1, replica_groups=mesh['groups'=2,'tm'=4,'tile'=2,'chan'=2] {'chan'}, dimensions={3}, use_global_device_ids=true | all-gather | bytes 1179648 | tf_op jit(solution)/shard_map/all_gather | solution.py:70
  31.0 1.3 collective-permute-start
  32.3 55.4 %collective-permute-done = bf16[2,24,16,512]{3,2,1,0:T(8,128)(2,1)S(1)} collective-permute-done((bf16[2,24,16,512]{3,2,1,0:T(8,128)(2,1)S(1)}, bf16[2,24,16,512]{3,2,1,0:T(8,128)(2,1)S(1)}, u32[]{:S(2)}, u32[]{:S(2)}) %collective-permute-start) | collective-permute-done | bytes 786464 | tf_op jit(solution)/shard_map/ppermute | solution.py:13
  88.1 4.1 %collective-permute-start.1 = (bf16[4,24,1,512]{3,2,1,0:T(2,128)(2,1)S(1)}, bf16[4,24,1,512]{3,2,1,0:T(2,128)(2,1)S(1)}, u32[]{:S(2)}, u32[]{:S(2)}) collective-permute-start(bf16[4,24,1,512]{3,2,1,0:T(2,128)(2,1)S(1)} %get-tuple-element.9), channel_id=1, source_target_pairs={{0,2},{1,3},{4,6},{5,7},{8,10},{9,11},{12,14},{13,15},{16,18},{17,... | collective-permute-start | bytes 294920 | tf_op jit(solution)/shard_map/ppermute | solution.py:24
  92.3 1.3 collective-permute-start.2
  94.2 2.1 %collective-permute-done.1 = bf16[4,24,1,512]{3,2,1,0:T(2,128)(2,1)S(1)} collective-permute-done((bf16[4,24,1,512]{3,2,1,0:T(2,128)(2,1)S(1)}, bf16[4,24,1,512]{3,2,1,0:T(2,128)(2,1)S(1)}, u32[]{:S(2)}, u32[]{:S(2)}) %collective-permute-start.1) | collective-permute-done | bytes 98336 | tf_op jit(solution)/shard_map/ppermute | solution.py:24
  96.4 4.1 %collective-permute-done.2 = bf16[4,24,1,512]{3,2,1,0:T(2,128)(2,1)S(1)} collective-permute-done((bf16[4,24,1,512]{3,2,1,0:T(2,128)(2,1)S(1)}, bf16[4,24,1,512]{3,2,1,0:T(2,128)(2,1)S(1)}, u32[]{:S(2)}, u32[]{:S(2)}) %collective-permute-start.2) | collective-permute-done | bytes 98336 | tf_op jit(solution)/shard_map/ppermute | solution.py:26
  100.5 1.6 fusion.5
  103.1 1.2 fusion.50
  104.3 1.2 fusion.49
  105.5 1.2 fusion.28
  107.7 1.3 fusion.22
  110.0 1.3 fusion.47
  111.3 1.2 fusion.46
  113.4 1.3 fusion.44
  114.7 1.3 fusion.43
  116.0 1.2 fusion.25
  118.2 1.3 fusion.19
  120.5 1.2 fusion.40
  121.8 1.2 fusion.39
  123.9 1.2 fusion.37
  125.1 1.2 fusion.36
  126.4 1.2 fusion.35
  128.5 1.4 fusion.33
  130.9 1.2 fusion.30
  132.1 1.2 fusion.29
  133.3 20.4 %copy.7 = bf16[2,24,16,27,512]{4,3,2,1,0:T(8,128)(2,1)S(1)} copy(bf16[2,24,16,27,512]{4,2,1,0,3:T(8,128)(2,1)} %fusion.29) | data formatting | bytes 42467328 | tf_op jit(solution)/shard_map/stack | solution.py:62
  153.8 16.2 %copy.8 = bf16[96,8,27,512]{3,1,2,0:T(8,128)(2,1)} copy(bf16[96,8,27,512]{3,2,1,0:T(8,128)(2,1)S(1)} %bitcast.111) | data formatting | bytes 42467328
  170.0 12.7 %fusion.6 = bf16[768,256]{1,0:T(8,128)(2,1)} fusion(bf16[768,13824]{1,0:T(8,128)(2,1)} %bitcast.112, bf16[13824,256]{1,0:T(8,128)(2,1)} %bitcast.113, f32[256]{0:T(256)S(1)} %convert_element_type.24), kind=kOutput, calls=%fused_computation.17 | convolution fusion | flops 5436211200 | bytes 28705792 | tf_op jit(solution)/shard_map/dot_general | solution.py:64
  (27 shorter events, 12.5 us)
Async XLA Ops:
  6.5 163.4 %all-gather.2.cloned.1.call-start = ((), (), s32[]{:S(2)}) async-start(), calls=%async_computation | async-start | bytes 8847360 | tf_op jit(solution)/shard_map/all_gather | solution.py:76
  31.0 56.7 %collective-permute-start = (bf16[2,24,16,512]{3,2,1,0:T(8,128)(2,1)S(1)}, bf16[2,24,16,512]{3,2,1,0:T(8,128)(2,1)S(1)}, u32[]{:S(2)}, u32[]{:S(2)}) collective-permute-start(bf16[2,24,16,512]{3,2,1,0:T(8,128)(2,1)S(1)} %all_gather.6), channel_id=1, source_target_pairs={{0,4},{4,8},{8,12},{1,5},{5,9},{9,13},{2,6},{6,10},{10,14},{3,7},{... | collective-permute-start | bytes 2359304 | tf_op jit(solution)/shard_map/ppermute | solution.py:13
  88.1 8.2 %collective-permute-start.1 = (bf16[4,24,1,512]{3,2,1,0:T(2,128)(2,1)S(1)}, bf16[4,24,1,512]{3,2,1,0:T(2,128)(2,1)S(1)}, u32[]{:S(2)}, u32[]{:S(2)}) collective-permute-start(bf16[4,24,1,512]{3,2,1,0:T(2,128)(2,1)S(1)} %get-tuple-element.9), channel_id=1, source_target_pairs={{0,2},{1,3},{4,6},{5,7},{8,10},{9,11},{12,14},{13,15},{16,18},{17,... | collective-permute-start | bytes 294920 | tf_op jit(solution)/shard_map/ppermute | solution.py:24
  92.3 8.2 %collective-permute-start.2 = (bf16[4,24,1,512]{3,2,1,0:T(2,128)(2,1)S(1)}, bf16[4,24,1,512]{3,2,1,0:T(2,128)(2,1)S(1)}, u32[]{:S(2)}, u32[]{:S(2)}) collective-permute-start(bf16[4,24,1,512]{3,2,1,0:T(2,128)(2,1)S(1)} %get-tuple-element.10), channel_id=1, source_target_pairs={{2,0},{3,1},{6,4},{7,5},{10,8},{11,9},{14,12},{15,13},{18,16},{19,... | collective-permute-start | bytes 294920 | tf_op jit(solution)/shard_map/ppermute | solution.py:26
Sparse Core Ops, SparseCore 0:
  8.9 142.9 all-gather.1
where the time goes:
time: 190 us; the launch traced here: 189 us
  waiting for transfers between devices  62.4 us (33%)
  local copies, waits for them, and re-layouts  60.9 us (32%)
  blocking collectives  19.3 us (10%)
  other arithmetic  14 us (7%)
  between operations  13.5 us (7%)
  matrix products  12.7 us (7%)
  starting transfers between devices  6.7 us (4%)
    ppermute x1, waiting for transfers between devices, shifted(): return lax.ppermute(block, axis, route)  55.4 us
    unnamed x22, local copies, waits for them, and re-layouts  38.5 us
    another operation x2, local copies, waits for them, and re-layouts, conv_term(): jnp.stack(columns, axis=3)  21.6 us
    psum x1, blocking collectives, normalize(): total_sum, total_square = lax.psum((part_sum, part_square), ('tm', 'tile'))  16.9 us
    dot_general x1, matrix products, conv_term(): return jnp.dot(stacked, matrix, preferred_element_type=jnp.float32)  12.7 us
    unnamed x6, other arithmetic  7.75 us
    ppermute x1, starting transfers between devices, extended_2(): lax.ppermute(tail, axis, [(i, (i + 1) % count) for i in range(ends)])  4.13 us
    ppermute x1, waiting for transfers between devices, extended_2(): lax.ppermute(head, axis, [((i + 1) % count, i) for i in range(ends)])  4.12 us
  transfers between devices with their start and end apart: 4, of which 3 were waited for; matrix products, arithmetic and copies ran while one was open for 40% of the time, Pallas kernels for 0%

commit v1 on v0

--- a/solution.py
+++ b/solution.py
@@ -1,10 +1,18 @@
+import functools
+
 import jax
 import jax.numpy as jnp
 from jax import lax
+from jax.experimental import pallas as pl
+from jax.experimental.pallas import tpu as pltpu
 from jax.sharding import PartitionSpec as P
 
 CH = 512
 GROUPS = 32
+EPS = 1e-06
+LANES = 128
+VMEM = 48 << 20
+STAT_ROWS = 16
 
 
 def shifted(block, axis, distance):
@@ -79,6 +87,246 @@
     return result.reshape(n_frames, n_rows, n_cols, n_chans)
 
 
+def near_of(s):
+    return s + 1 - 2 * (s % 2)
+
+
+def mid_of(s):
+    return (s + 2) % 4
+
+
+def far_of(s):
+    return 3 - s
+
+
+def edges_kernel(latent_ref, out_ref, wide_ref, *, cells, cols):
+    wide = latent_ref[...].astype(jnp.float32)
+    edges = cells // cols
+    first = jnp.where(lax.axis_index("tile") == 0, cols - 1, 0)
+    for k in range(wide.shape[1] // LANES):
+        lanes = slice(k * LANES, (k + 1) * LANES)
+        wide_ref[...] = wide[:, lanes]
+        out_ref[:edges, lanes] = wide_ref[pl.ds(first, edges, stride=cols), :]
+    total = jnp.sum(wide, axis=0, keepdims=True)
+    square = jnp.sum(wide * wide, axis=0, keepdims=True)
+    out_ref[edges:] = jnp.concatenate([total, square, jnp.zeros((6, wide.shape[1]), jnp.float32)], axis=0)
+
+
+def three(value):
+    high = value.astype(jnp.bfloat16)
+    rest = value - high.astype(jnp.float32)
+    mid = rest.astype(jnp.bfloat16)
+    low = (rest - mid.astype(jnp.float32)).astype(jnp.bfloat16)
+    return [high, mid, low]
+
+
+def pack_kernel(latent_ref, own_ref, other_ref, gain_ref, bias_ref, same_ref, next_ref, *, cells, edges):
+    sums = own_ref[edges : edges + 2] + other_ref[edges : edges + 2]
+    tail = three(sums[0:1]) + three(sums[1:2]) + [gain_ref[...], bias_ref[...]]
+    tail = jnp.concatenate([row.astype(jnp.float32) for row in tail], axis=0)
+    tail = jnp.concatenate([tail, jnp.zeros_like(tail)], axis=0).astype(jnp.bfloat16)
+    edge = other_ref[:edges].astype(jnp.bfloat16)
+
+    def fill(out_ref, block):
+        lanes = slice(block * LANES, (block + 1) * LANES)
+        out_ref[:cells] = latent_ref[:, lanes]
+        out_ref[cells : cells + edges] = edge[:, lanes]
+        out_ref[cells + edges :] = tail[:, lanes]
+
+    parity = lax.axis_index("tm") % 2
+
+    @pl.when(parity == 0)
+    def _():
+        fill(same_ref, 0)
+        fill(next_ref, 1)
+
+    @pl.when(parity == 1)
+    def _():
+        fill(same_ref, 1)
+        fill(next_ref, 0)
+
+
+def group_total(row, group_ch):
+    lane = lax.broadcasted_iota(jnp.int32, row.shape, 1)
+    step = 1
+    while step < group_ch:
+        up = pltpu.roll(row, LANES - step, 1)
+        down = pltpu.roll(row, step, 1)
+        row = row + jnp.where((lane // step) % 2 == 0, up, down)
+        step *= 2
+    return row
+
+
+def spread_kernel(same_ref, a_ref, b_ref, c_ref, d_ref, out_ref, own_ref, *, frames, rows, cols, entries):
+    s = lax.axis_index("tm")
+    home = lax.axis_index("chan") == s // 2
+    tile = lax.axis_index("tile")
+    cells = frames * rows * cols
+    edges = frames * rows
+    base = cells + edges
+
+    @pl.when(home)
+    def _():
+        own_ref[...] = same_ref[...]
+
+    @pl.when(jnp.logical_not(home))
+    def _():
+        own_ref[...] = d_ref[...]
+
+    near, mid, far = near_of(s), mid_of(s), far_of(s)
+    pieces = (
+        (own_ref, jnp.where(home, s, mid)),
+        (a_ref, jnp.where(home, near, far)),
+        (b_ref, jnp.where(home, mid, s)),
+        (c_ref, jnp.where(home, far, near)),
+    )
+    tails = [ref[base : base + STAT_ROWS].astype(jnp.float32) for ref, _ in pieces]
+    stats = tails[0] + tails[1] + tails[2] + tails[3]
+    total = group_total(stats[0:1] + stats[1:2] + stats[2:3], CH // GROUPS) / entries
+    square = group_total(stats[3:4] + stats[4:5] + stats[5:6], CH // GROUPS) / entries
+    scale = lax.rsqrt(square - total * total + EPS) * tails[0][6:7]
+    shift = tails[0][7:8]
+
+    def normed(raw):
+        value = (raw.astype(jnp.float32) - total) * scale + shift
+        return value / (1.0 + jnp.exp(-value))
+
+    n_all = out_ref.shape[1]
+    zero_row = jnp.zeros((cols, LANES), jnp.bfloat16)
+    for d in range(3):
+        for f in range(n_all):
+            out_ref[d, f, 0] = zero_row
+            out_ref[d, f, rows + 1] = zero_row
+        for f in range(2):
+            out_ref[d, f, 1 : rows + 1] = jnp.zeros((rows, cols, LANES), jnp.bfloat16)
+    col = lax.broadcasted_iota(jnp.int32, (rows, cols, LANES), 1)
+    span = rows * cols
+    for ref, block in pieces:
+        for f in range(frames):
+            value = normed(ref[f * span : (f + 1) * span])
+            edge = normed(ref[cells + f * rows : cells + (f + 1) * rows])
+            edge = jnp.broadcast_to(edge[:, None, :], (rows, cols, LANES))
+            left = pltpu.roll(value, 1, 0).reshape(rows, cols, LANES)
+            left = jnp.where(col == 0, jnp.where(tile == 1, edge, 0.0), left)
+            right = pltpu.roll(value, span - 1, 0).reshape(rows, cols, LANES)
+            right = jnp.where(col == cols - 1, jnp.where(tile == 0, edge, 0.0), right)
+            at = 2 + block * frames + f
+            out_ref[0, at, 1 : rows + 1] = left.astype(jnp.bfloat16)
+            out_ref[1, at, 1 : rows + 1] = value.reshape(rows, cols, LANES).astype(jnp.bfloat16)
+            out_ref[2, at, 1 : rows + 1] = right.astype(jnp.bfloat16)
+
+
+def partial_kernel(spread_ref, weight_ref, *rest, block_of, frame_list, frames, rows, cols, adds, with_bias):
+    out_ref = rest[-1]
+    block = block_of(lax.axis_index("tm"))
+    span = rows * cols
+    for k, f in enumerate(frame_list):
+        at = block * frames + f
+        stacked = jnp.concatenate(
+            [
+                spread_ref[d, at + a, b : b + rows].reshape(span, LANES)
+                for a in range(3)
+                for b in range(3)
+                for d in range(3)
+            ],
+            axis=1,
+        )
+        total = jnp.dot(stacked, weight_ref[...], preferred_element_type=jnp.float32)
+        here = slice(k * span, (k + 1) * span)
+        for ref in rest[:adds]:
+            total = total + ref[here].astype(jnp.float32)
+        if with_bias:
+            total = total + rest[adds][...].astype(jnp.float32)
+        out_ref[here] = total.astype(out_ref.dtype)
+
+
+def params():
+    return pltpu.CompilerParams(vmem_limit_bytes=VMEM)
+
+
+def split_body(latent, gn_gain, gn_bias, conv_weight, conv_bias):
+    frames, rows, cols, chans = latent.shape
+    outs = conv_weight.shape[2]
+    cells = frames * rows * cols
+    edges = frames * rows
+    n_blocks = lax.axis_size("tm")
+    entries = cells * n_blocks * lax.axis_size("tile") * (CH // GROUPS)
+    flat = latent.reshape(cells, chans)
+
+    own = pl.pallas_call(
+        functools.partial(edges_kernel, cells=cells, cols=cols),
+        out_shape=jax.ShapeDtypeStruct((edges + 8, chans), jnp.float32),
+        scratch_shapes=[pltpu.VMEM((cells, LANES), jnp.float32)],
+        compiler_params=params(),
+    )(flat)
+    other = lax.ppermute(own, "tile", [(0, 1), (1, 0)])
+    packed = jax.ShapeDtypeStruct((cells + edges + STAT_ROWS, LANES), jnp.bfloat16)
+    same, following = pl.pallas_call(
+        functools.partial(pack_kernel, cells=cells, edges=edges),
+        out_shape=(packed, packed),
+        compiler_params=params(),
+    )(flat, own, other, gn_gain.reshape(1, chans), gn_bias.reshape(1, chans))
+
+    both = ("tm", "chan")
+    route_a, route_b, route_d = [], [], []
+    for s in range(n_blocks):
+        h = s // 2
+        route_a += [(2 * s + h, 2 * near_of(s) + h), (2 * s + 1 - h, 2 * far_of(s) + h)]
+        route_b += [(2 * s + h, 2 * s + 1 - h), (2 * s + 1 - h, 2 * mid_of(s) + 1 - h)]
+        route_d += [(2 * s + h, 2 * s + 1 - h)]
+    got_a = lax.ppermute(following, both, route_a)
+    got_b = lax.ppermute(same, both, route_b)
+    got_c = lax.ppermute(got_a, "chan", [(0, 1), (1, 0)])
+    got_d = lax.ppermute(got_b, both, route_d)
+    spread = pl.pallas_call(
+        functools.partial(spread_kernel, frames=frames, rows=rows, cols=cols, entries=entries),
+        out_shape=jax.ShapeDtypeStruct((3, n_blocks * frames + 2, rows + 2, cols, LANES), jnp.bfloat16),
+        scratch_shapes=[pltpu.VMEM(packed.shape, jnp.bfloat16)],
+        compiler_params=params(),
+    )(same, got_a, got_b, got_c, got_d)
+
+    weight = conv_weight.reshape(27 * LANES, outs)
+    bias = conv_bias.reshape(1, outs)
+
+    def partial_sum(block_of, frame_list, adds=(), with_bias=False, dtype=jnp.bfloat16):
+        size = len(frame_list) * rows * cols
+        return pl.pallas_call(
+            functools.partial(
+                partial_kernel,
+                block_of=block_of,
+                frame_list=frame_list,
+                frames=frames,
+                rows=rows,
+                cols=cols,
+                adds=len(adds),
+                with_bias=with_bias,
+            ),
+            out_shape=jax.ShapeDtypeStruct((size, outs), dtype),
+            compiler_params=params(),
+            cost_estimate=pl.CostEstimate(
+                flops=2 * size * 27 * LANES * outs, transcendentals=0, bytes_accessed=4 * size * outs
+            ),
+        )(spread, weight, *adds, *([bias] if with_bias else []))
+
+    near_route = [(s, near_of(s)) for s in range(n_blocks)]
+    far_route = [(s, far_of(s)) for s in range(n_blocks)]
+    beyond = [
+        lax.ppermute(partial_sum(lambda s: far_of(near_of(s)), (f,)), "tm", near_route) for f in range(frames)
+    ]
+    arrived = [
+        lax.ppermute(partial_sum(far_of, (f,), (beyond[f],)), "tm", far_route) for f in range(frames)
+    ]
+    beside = lax.ppermute(partial_sum(near_of, tuple(range(frames))), "tm", near_route)
+    home = partial_sum(lambda s: s, tuple(range(frames)), (beside,), True, jnp.float32)
+    result = home + jnp.concatenate(arrived, axis=0).astype(jnp.float32)
+    return result.astype(jnp.bfloat16).reshape(frames, rows, cols, outs)
+
+
+def splits(mesh):
+    size = mesh.shape
+    return size["tm"] == 4 and size["tile"] == 2 and size["chan"] == 2 and CH == size["tm"] * LANES
+
+
 def solution(mesh):
     in_specs = (
         P(("groups", "tm"), None, "tile", "chan"),
@@ -88,4 +336,5 @@
         P("chan"),
     )
     out_specs = P(("groups", "tm"), None, "tile", "chan")
-    return jax.shard_map(body, mesh=mesh, in_specs=in_specs, out_specs=out_specs, check_vma=False)
+    chosen = split_body if splits(mesh) else body
+    return jax.shard_map(chosen, mesh=mesh, in_specs=in_specs, out_specs=out_specs, check_vma=False)

time: 190 us -> 58 us (0.31)
  the two profiles are of different devices: /device:TPU:24 before, /device:TPU:8 now
where the time goes in v1:
time: 58 us; the launch traced here: 57.8 us
  waiting for transfers between devices  30.2 us (52%)
  starting transfers between devices  15.7 us (27%)
  Pallas kernels  8.51 us (15%)
  local copies, waits for them, and re-layouts  2.46 us (4%)
  other arithmetic  0.86 us (1%)
    ppermute x2, waiting for transfers between devices, split_body(): lax.ppermute(partial_sum(lambda s: far_of(near_of(s)), (f,)), 'tm', near_...  13.8 us
    ppermute x2, waiting for transfers between devices, split_body(): lax.ppermute(partial_sum(far_of, (f,), (beyond[f],)), 'tm', far_route)  9.04 us
    pallas_call x6, Pallas kernels, partial_sum(): pl.pallas_call(functools.partial(partial_kernel, block_of=block_of, frame...  6.69 us
    ppermute x1, waiting for transfers between devices, split_body(): got_a = lax.ppermute(following, both, route_a)  4.92 us
    ppermute x2, starting transfers between devices, split_body(): lax.ppermute(partial_sum(lambda s: far_of(near_of(s)), (f,)), 'tm', near_...  3.67 us
    ppermute x1, starting transfers between devices, split_body(): got_d = lax.ppermute(got_b, both, route_d)  3.44 us
    ppermute x1, starting transfers between devices, split_body(): got_c = lax.ppermute(got_a, 'chan', [(0, 1), (1, 0)])  3.17 us
    ppermute x2, starting transfers between devices, split_body(): lax.ppermute(partial_sum(far_of, (f,), (beyond[f],)), 'tm', far_route)  1.83 us
  transfers between devices with their start and end apart: 10, of which 6 were waited for; matrix products, arithmetic and copies ran while one was open for 2% of the time, Pallas kernels for 7%

profile of v1, /device:TPU:8, one launch (start us, length us, event | category | flops | bytes accessed | tf_op | source)
XLA Modules:
  0.0 57.8 jit_solution(3987846238469650111)
XLA Ops:
  0.0 1.1 %copy-done.1 = bf16[2,24,16,256]{3,2,1,0:T(8,128)(2,1)S(1)} copy-done((bf16[2,24,16,256]{3,2,1,0:T(8,128)(2,1)S(1)}, bf16[2,24,16,256]{3,2,1,0:T(8,128)(2,1)}, u32[]{:S(2)}) %copy-start.1) | copy-done | bytes 393240
  1.1 0.2 shard_map.55.own_ref
  1.3 1.6 %collective-permute-start = (f32[56,256]{1,0:T(8,128)S(1)}, f32[56,256]{1,0:T(8,128)S(1)}, u32[]{:S(2)}, u32[]{:S(2)}) collective-permute-start(f32[56,256]{1,0:T(8,128)S(1)} %shard_map.55.own_ref), channel_id=1, source_target_pairs={{0,2},{2,0},{1,3},{3,1},{4,6},{6,4},{5,7},{7,5},{8,10},{10,8},{9,1... | collective-permute-start | bytes 172040 | tf_op jit(solution)/shard_map/ppermute | solution.py:262
  2.9 0.7 %reshape.19.gain_ref = bf16[1,256]{1,0:T(2,128)(2,1)S(1)} reshape(bf16[256]{0:T(256)(128)(2,1)} %param.6) | data formatting | bytes 1024 | tf_op jit(solution)/shard_map/reshape | solution.py:268
  3.5 0.7 %reshape.20.bias_ref = bf16[1,256]{1,0:T(2,128)(2,1)S(1)} reshape(bf16[256]{0:T(256)(128)(2,1)} %param.7) | data formatting | bytes 1024 | tf_op jit(solution)/shard_map/reshape | solution.py:268
  4.2 1.4 %collective-permute-done.other_ref = f32[56,256]{1,0:T(8,128)S(1)} collective-permute-done((f32[56,256]{1,0:T(8,128)S(1)}, f32[56,256]{1,0:T(8,128)S(1)}, u32[]{:S(2)}, u32[]{:S(2)}) %collective-permute-start) | collective-permute-done | bytes 57376 | tf_op jit(solution)/shard_map/ppermute | solution.py:262
  5.6 0.1 shard_map.56
  5.7 0.1 collective-permute-start.1
  5.7 1.7 %collective-permute-start.2 = (bf16[832,128]{1,0:T(8,128)(2,1)S(1)}, bf16[832,128]{1,0:T(8,128)(2,1)S(1)}, u32[]{:S(2)}, u32[]{:S(2)}) collective-permute-start(bf16[832,128]{1,0:T(8,128)(2,1)S(1)} %get-tuple-element.7.same_ref), channel_id=1, source_target_pairs={{0,1},{1,9},{4,5},{5,13},{9,8},{8,0},{13,12},{12,4},{2,3},{3,11},{... | collective-permute-start | bytes 638984 | tf_op jit(solution)/shard_map/ppermute | solution.py:278
  7.4 4.9 %collective-permute-done.1.a_ref = bf16[832,128]{1,0:T(8,128)(2,1)S(1)} collective-permute-done((bf16[832,128]{1,0:T(8,128)(2,1)S(1)}, bf16[832,128]{1,0:T(8,128)(2,1)S(1)}, u32[]{:S(2)}, u32[]{:S(2)}) %collective-permute-start.1) | collective-permute-done | bytes 213024 | tf_op jit(solution)/shard_map/ppermute | solution.py:277
  12.3 3.2 %collective-permute-start.3 = (bf16[832,128]{1,0:T(8,128)(2,1)S(1)}, bf16[832,128]{1,0:T(8,128)(2,1)S(1)}, u32[]{:S(2)}, u32[]{:S(2)}) collective-permute-start(bf16[832,128]{1,0:T(8,128)(2,1)S(1)} %collective-permute-done.1.a_ref), channel_id=1, source_target_pairs={{0,1},{1,0},{2,3},{3,2},{4,5},{5,4},{6,7},{7,6},{8,9},{9,8},{10,11... | collective-permute-start | bytes 638984 | tf_op jit(solution)/shard_map/ppermute | solution.py:279
  15.5 3.4 %collective-permute-start.4 = (bf16[832,128]{1,0:T(8,128)(2,1)S(1)}, bf16[832,128]{1,0:T(8,128)(2,1)S(1)}, u32[]{:S(2)}, u32[]{:S(2)}) collective-permute-start(bf16[832,128]{1,0:T(8,128)(2,1)S(1)} %collective-permute-done.2.b_ref), channel_id=1, source_target_pairs={{0,1},{4,5},{9,8},{13,12},{2,3},{6,7},{11,10},{15,14},{16,17},{20,... | collective-permute-start | bytes 638984 | tf_op jit(solution)/shard_map/ppermute | solution.py:280
  19.0 0.0 collective-permute-done.3.c_ref
  19.0 1.1 %collective-permute-done.4.d_ref = bf16[832,128]{1,0:T(8,128)(2,1)S(1)} collective-permute-done((bf16[832,128]{1,0:T(8,128)(2,1)S(1)}, bf16[832,128]{1,0:T(8,128)(2,1)S(1)}, u32[]{:S(2)}, u32[]{:S(2)}) %collective-permute-start.4) | collective-permute-done | bytes 213024 | tf_op jit(solution)/shard_map/ppermute | solution.py:280
  20.0 1.5 %shard_map.57.spread_ref = bf16[3,10,26,16,128]{4,3,2,1,0:T(8,128)(2,1)S(1)} custom-call(bf16[832,128]{1,0:T(8,128)(2,1)S(1)} %get-tuple-element.7.same_ref, bf16[832,128]{1,0:T(8,128)(2,1)S(1)} %collective-permute-done.1.a_ref, bf16[832,128]{1,0:T(8,128)(2,1)S(1)} %collective-permute-done.2.b_ref, bf16[832,128]{1,0:T(8,128)(2,1)S(1)} %collective-permute-done.3.c_ref, ...), custom_call_target="tpu_custom_call" | custom-call | tf_op jit(solution)/shard_map/pallas_call | solution.py:281
  21.6 1.6 %shard_map.58 = bf16[768,256]{1,0:T(8,128)(2,1)S(1)} custom-call(bf16[3,10,26,16,128]{4,3,2,1,0:T(8,128)(2,1)S(1)} %shard_map.57.spread_ref, bf16[3456,256]{1,0:T(8,128)(2,1)S(1)} %bitcast.3), custom_call_target="tpu_custom_call" | custom-call | flops 1358954496 | bytes 786432 | tf_op jit(solution)/shard_map/pallas_call | solution.py:293
  23.2 0.9 %shard_map.62 = bf16[384,256]{1,0:T(8,128)(2,1)S(1)} custom-call(bf16[3,10,26,16,128]{4,3,2,1,0:T(8,128)(2,1)S(1)} %shard_map.57.spread_ref, bf16[3456,256]{1,0:T(8,128)(2,1)S(1)} %bitcast.4), custom_call_target="tpu_custom_call" | custom-call | flops 679477248 | bytes 393216 | tf_op jit(solution)/shard_map/pallas_call | solution.py:293
  24.1 1.8 %collective-permute-start.8 = (bf16[384,256]{1,0:T(8,128)(2,1)S(1)}, bf16[384,256]{1,0:T(8,128)(2,1)S(1)}, u32[]{:S(2)}, u32[]{:S(2)}) collective-permute-start(bf16[384,256]{1,0:T(8,128)(2,1)S(1)} %shard_map.62), channel_id=1, source_target_pairs={{0,4},{4,0},{8,12},{12,8},{1,5},{5,1},{9,13},{13,9},{2,6},{6,2},{1... | collective-permute-start | bytes 589832 | tf_op jit(solution)/shard_map/ppermute | solution.py:314
  25.9 0.3 collective-permute-start.5
  26.2 0.9 %shard_map.60 = bf16[384,256]{1,0:T(8,128)(2,1)S(1)} custom-call(bf16[3,10,26,16,128]{4,3,2,1,0:T(8,128)(2,1)S(1)} %shard_map.57.spread_ref, bf16[3456,256]{1,0:T(8,128)(2,1)S(1)} %bitcast.5), custom_call_target="tpu_custom_call" | custom-call | flops 679477248 | bytes 393216 | tf_op jit(solution)/shard_map/pallas_call | solution.py:293
  27.1 1.8 %collective-permute-start.6 = (bf16[384,256]{1,0:T(8,128)(2,1)S(1)}, bf16[384,256]{1,0:T(8,128)(2,1)S(1)}, u32[]{:S(2)}, u32[]{:S(2)}) collective-permute-start(bf16[384,256]{1,0:T(8,128)(2,1)S(1)} %shard_map.60), channel_id=1, source_target_pairs={{0,4},{4,0},{8,12},{12,8},{1,5},{5,1},{9,13},{13,9},{2,6},{6,2},{1... | collective-permute-start | bytes 589832 | tf_op jit(solution)/shard_map/ppermute | solution.py:314
  28.9 3.0 %collective-permute-done.8.rest_0_ = bf16[384,256]{1,0:T(8,128)(2,1)S(1)} collective-permute-done((bf16[384,256]{1,0:T(8,128)(2,1)S(1)}, bf16[384,256]{1,0:T(8,128)(2,1)S(1)}, u32[]{:S(2)}, u32[]{:S(2)}) %collective-permute-start.8) | collective-permute-done | bytes 196640 | tf_op jit(solution)/shard_map/ppermute | solution.py:314
  31.9 0.9 %shard_map.63 = bf16[384,256]{1,0:T(8,128)(2,1)S(1)} custom-call(bf16[3,10,26,16,128]{4,3,2,1,0:T(8,128)(2,1)S(1)} %shard_map.57.spread_ref, bf16[3456,256]{1,0:T(8,128)(2,1)S(1)} %bitcast.6, bf16[384,256]{1,0:T(8,128)(2,1)S(1)} %collective-permute-done.8.rest_0_), custom_call_target="tpu_custom_call" | custom-call | flops 679477248 | bytes 393216 | tf_op jit(solution)/shard_map/pallas_call | solution.py:293
  32.8 0.0 copy-start.2
  32.8 0.9 %collective-permute-start.9 = (bf16[384,256]{1,0:T(8,128)(2,1)S(1)}, bf16[384,256]{1,0:T(8,128)(2,1)S(1)}, u32[]{:S(2)}, u32[]{:S(2)}) collective-permute-start(bf16[384,256]{1,0:T(8,128)(2,1)S(1)} %shard_map.63), channel_id=1, source_target_pairs={{0,12},{4,8},{8,4},{12,0},{1,13},{5,9},{9,5},{13,1},{2,14},{6,10},... | collective-permute-start | bytes 589832 | tf_op jit(solution)/shard_map/ppermute | solution.py:317
  33.7 10.8 %collective-permute-done.6.rest_0_ = bf16[384,256]{1,0:T(8,128)(2,1)S(1)} collective-permute-done((bf16[384,256]{1,0:T(8,128)(2,1)S(1)}, bf16[384,256]{1,0:T(8,128)(2,1)S(1)}, u32[]{:S(2)}, u32[]{:S(2)}) %collective-permute-start.6) | collective-permute-done | bytes 196640 | tf_op jit(solution)/shard_map/ppermute | solution.py:314
  44.5 0.9 %shard_map.61 = bf16[384,256]{1,0:T(8,128)(2,1)S(1)} custom-call(bf16[3,10,26,16,128]{4,3,2,1,0:T(8,128)(2,1)S(1)} %shard_map.57.spread_ref, bf16[3456,256]{1,0:T(8,128)(2,1)S(1)} %bitcast.7, bf16[384,256]{1,0:T(8,128)(2,1)S(1)} %collective-permute-done.6.rest_0_), custom_call_target="tpu_custom_call" | custom-call | flops 679477248 | bytes 393216 | tf_op jit(solution)/shard_map/pallas_call | solution.py:293
  45.4 0.9 %collective-permute-start.7 = (bf16[384,256]{1,0:T(8,128)(2,1)S(1)}, bf16[384,256]{1,0:T(8,128)(2,1)S(1)}, u32[]{:S(2)}, u32[]{:S(2)}) collective-permute-start(bf16[384,256]{1,0:T(8,128)(2,1)S(1)} %shard_map.61), channel_id=1, source_target_pairs={{0,12},{4,8},{8,4},{12,0},{1,13},{5,9},{9,5},{13,1},{2,14},{6,10},... | collective-permute-start | bytes 589832 | tf_op jit(solution)/shard_map/ppermute | solution.py:317
  46.3 0.0 collective-permute-done.5.rest_0_
  46.3 1.6 %shard_map.59 = f32[768,256]{1,0:T(8,128)S(1)} custom-call(bf16[3,10,26,16,128]{4,3,2,1,0:T(8,128)(2,1)S(1)} %shard_map.57.spread_ref, bf16[3456,256]{1,0:T(8,128)(2,1)S(1)} %bitcast.8, bf16[768,256]{1,0:T(8,128)(2,1)S(1)} %collective-permute-done.5.rest_0_, bf16[1,256]{1,0:T(2,128)(2,1)S(1)} %reshape.22.rest_1_), custom_call_target="tpu_custom_call" | custom-call | flops 1358954496 | bytes 786432 | tf_op jit(solution)/shard_map/pallas_call | solution.py:293
  47.9 9.0 %collective-permute-done.7 = bf16[384,256]{1,0:T(8,128)(2,1)S(1)} collective-permute-done((bf16[384,256]{1,0:T(8,128)(2,1)S(1)}, bf16[384,256]{1,0:T(8,128)(2,1)S(1)}, u32[]{:S(2)}, u32[]{:S(2)}) %collective-permute-start.7) | collective-permute-done | bytes 196640 | tf_op jit(solution)/shard_map/ppermute | solution.py:317
  57.0 0.9 %add_convert_fusion = bf16[768,256]{1,0:T(8,128)(2,1)} fusion(f32[768,256]{1,0:T(8,128)S(1)} %shard_map.59, bf16[384,256]{1,0:T(8,128)(2,1)S(1)} %collective-permute-done.9, bf16[384,256]{1,0:T(8,128)(2,1)S(1)} %collective-permute-done.7), kind=kLoop, calls=%fused_computation | loop fusion | flops 1179648 | bytes 1572864 | tf_op jit(solution)/shard_map/convert_element_type | solution.py:322
  (7 shorter events, 0.0 us)
Async XLA Ops:
  0.0 21.6 %copy-start = (bf16[27,128,256]{2,1,0:T(8,128)(2,1)S(1)}, bf16[27,128,256]{2,1,0:T(8,128)(2,1)}, u32[]{:S(2)}) copy-start(bf16[27,128,256]{2,1,0:T(8,128)(2,1)} %param.8) | copy-start | bytes 5308420
  0.0 1.1 %copy-start.1 = (bf16[2,24,16,256]{3,2,1,0:T(8,128)(2,1)S(1)}, bf16[2,24,16,256]{3,2,1,0:T(8,128)(2,1)}, u32[]{:S(2)}) copy-start(bf16[2,24,16,256]{3,2,1,0:T(8,128)(2,1)} %param.5) | copy-start | bytes 1179652
  1.3 4.2 %collective-permute-start = (f32[56,256]{1,0:T(8,128)S(1)}, f32[56,256]{1,0:T(8,128)S(1)}, u32[]{:S(2)}, u32[]{:S(2)}) collective-permute-start(f32[56,256]{1,0:T(8,128)S(1)} %shard_map.55.own_ref), channel_id=1, source_target_pairs={{0,2},{2,0},{1,3},{3,1},{4,6},{6,4},{5,7},{7,5},{8,10},{10,8},{9,1... | collective-permute-start | bytes 172040 | tf_op jit(solution)/shard_map/ppermute | solution.py:262
  5.7 6.7 %collective-permute-start.1 = (bf16[832,128]{1,0:T(8,128)(2,1)S(1)}, bf16[832,128]{1,0:T(8,128)(2,1)S(1)}, u32[]{:S(2)}, u32[]{:S(2)}) collective-permute-start(bf16[832,128]{1,0:T(8,128)(2,1)S(1)} %get-tuple-element.8), channel_id=1, source_target_pairs={{0,4},{1,12},{4,0},{5,8},{9,13},{8,5},{13,9},{12,1},{2,6},{3,14},{... | collective-permute-start | bytes 638984 | tf_op jit(solution)/shard_map/ppermute | solution.py:277
  5.7 9.8 %collective-permute-start.2 = (bf16[832,128]{1,0:T(8,128)(2,1)S(1)}, bf16[832,128]{1,0:T(8,128)(2,1)S(1)}, u32[]{:S(2)}, u32[]{:S(2)}) collective-permute-start(bf16[832,128]{1,0:T(8,128)(2,1)S(1)} %get-tuple-element.7.same_ref), channel_id=1, source_target_pairs={{0,1},{1,9},{4,5},{5,13},{9,8},{8,0},{13,12},{12,4},{2,3},{3,11},{... | collective-permute-start | bytes 638984 | tf_op jit(solution)/shard_map/ppermute | solution.py:278
  12.3 6.6 %collective-permute-start.3 = (bf16[832,128]{1,0:T(8,128)(2,1)S(1)}, bf16[832,128]{1,0:T(8,128)(2,1)S(1)}, u32[]{:S(2)}, u32[]{:S(2)}) collective-permute-start(bf16[832,128]{1,0:T(8,128)(2,1)S(1)} %collective-permute-done.1.a_ref), channel_id=1, source_target_pairs={{0,1},{1,0},{2,3},{3,2},{4,5},{5,4},{6,7},{7,6},{8,9},{9,8},{10,11... | collective-permute-start | bytes 638984 | tf_op jit(solution)/shard_map/ppermute | solution.py:279
  15.5 4.5 %collective-permute-start.4 = (bf16[832,128]{1,0:T(8,128)(2,1)S(1)}, bf16[832,128]{1,0:T(8,128)(2,1)S(1)}, u32[]{:S(2)}, u32[]{:S(2)}) collective-permute-start(bf16[832,128]{1,0:T(8,128)(2,1)S(1)} %collective-permute-done.2.b_ref), channel_id=1, source_target_pairs={{0,1},{4,5},{9,8},{13,12},{2,3},{6,7},{11,10},{15,14},{16,17},{20,... | collective-permute-start | bytes 638984 | tf_op jit(solution)/shard_map/ppermute | solution.py:280
  24.1 7.8 %collective-permute-start.8 = (bf16[384,256]{1,0:T(8,128)(2,1)S(1)}, bf16[384,256]{1,0:T(8,128)(2,1)S(1)}, u32[]{:S(2)}, u32[]{:S(2)}) collective-permute-start(bf16[384,256]{1,0:T(8,128)(2,1)S(1)} %shard_map.62), channel_id=1, source_target_pairs={{0,4},{4,0},{8,12},{12,8},{1,5},{5,1},{9,13},{13,9},{2,6},{6,2},{1... | collective-permute-start | bytes 589832 | tf_op jit(solution)/shard_map/ppermute | solution.py:314
  25.9 20.4 %collective-permute-start.5 = (bf16[768,256]{1,0:T(8,128)(2,1)S(1)}, bf16[768,256]{1,0:T(8,128)(2,1)S(1)}, u32[]{:S(2)}, u32[]{:S(2)}) collective-permute-start(bf16[768,256]{1,0:T(8,128)(2,1)S(1)} %shard_map.58), channel_id=1, source_target_pairs={{0,4},{4,0},{8,12},{12,8},{1,5},{5,1},{9,13},{13,9},{2,6},{6,2},{1... | collective-permute-start | bytes 1179656 | tf_op jit(solution)/shard_map/ppermute | solution.py:319
  27.1 17.4 %collective-permute-start.6 = (bf16[384,256]{1,0:T(8,128)(2,1)S(1)}, bf16[384,256]{1,0:T(8,128)(2,1)S(1)}, u32[]{:S(2)}, u32[]{:S(2)}) collective-permute-start(bf16[384,256]{1,0:T(8,128)(2,1)S(1)} %shard_map.60), channel_id=1, source_target_pairs={{0,4},{4,0},{8,12},{12,8},{1,5},{5,1},{9,13},{13,9},{2,6},{6,2},{1... | collective-permute-start | bytes 589832 | tf_op jit(solution)/shard_map/ppermute | solution.py:314
  32.8 13.6 %copy-start.2 = (bf16[256]{0:T(256)(128)(2,1)S(1)}, bf16[256]{0:T(256)(128)(2,1)}, u32[]{:S(2)}) copy-start(bf16[256]{0:T(256)(128)(2,1)} %param.9) | copy-start | bytes 1540
  32.8 15.1 %collective-permute-start.9 = (bf16[384,256]{1,0:T(8,128)(2,1)S(1)}, bf16[384,256]{1,0:T(8,128)(2,1)S(1)}, u32[]{:S(2)}, u32[]{:S(2)}) collective-permute-start(bf16[384,256]{1,0:T(8,128)(2,1)S(1)} %shard_map.63), channel_id=1, source_target_pairs={{0,12},{4,8},{8,4},{12,0},{1,13},{5,9},{9,5},{13,1},{2,14},{6,10},... | collective-permute-start | bytes 589832 | tf_op jit(solution)/shard_map/ppermute | solution.py:317
  45.4 11.6 %collective-permute-start.7 = (bf16[384,256]{1,0:T(8,128)(2,1)S(1)}, bf16[384,256]{1,0:T(8,128)(2,1)S(1)}, u32[]{:S(2)}, u32[]{:S(2)}) collective-permute-start(bf16[384,256]{1,0:T(8,128)(2,1)S(1)} %shard_map.61), channel_id=1, source_target_pairs={{0,12},{4,8},{8,4},{12,0},{1,13},{5,9},{9,5},{13,1},{2,14},{6,10},... | collective-permute-start | bytes 589832 | tf_op jit(solution)/shard_map/ppermute | solution.py:317

commit v2 on v1

--- a/solution.py
+++ b/solution.py
@@ -232,12 +232,21 @@
             axis=1,
         )
         total = jnp.dot(stacked, weight_ref[...], preferred_element_type=jnp.float32)
-        here = slice(k * span, (k + 1) * span)
-        for ref in rest[:adds]:
-            total = total + ref[here].astype(jnp.float32)
+        for ref, frame in zip(rest, adds):
+            if frame == f:
+                total = total + ref[...].astype(jnp.float32)
         if with_bias:
-            total = total + rest[adds][...].astype(jnp.float32)
-        out_ref[here] = total.astype(out_ref.dtype)
+            total = total + rest[len(adds)][...].astype(jnp.float32)
+        out_ref[k * span : (k + 1) * span] = total.astype(out_ref.dtype)
+
+
+def finish_kernel(home_ref, beside_ref, *rest, span):
+    out_ref = rest[-1]
+    total = home_ref[...] + beside_ref[...].astype(jnp.float32)
+    out_ref[:span] = total[:span].astype(out_ref.dtype)
+    for k, ref in enumerate(rest[:-1]):
+        here = slice((k + 1) * span, (k + 2) * span)
+        out_ref[here] = (total[here] + ref[...].astype(jnp.float32)).astype(out_ref.dtype)
 
 
 def params():
@@ -288,7 +297,10 @@
     weight = conv_weight.reshape(27 * LANES, outs)
     bias = conv_bias.reshape(1, outs)
 
-    def partial_sum(block_of, frame_list, adds=(), with_bias=False, dtype=jnp.bfloat16):
+    every = tuple(range(frames))
+
+    def partial_sum(block_of, frame_list=every, adds=(), with_bias=False, dtype=jnp.bfloat16, after=None, cost=1):
+        source = spread if after is None else lax.optimization_barrier((spread, after))[0]
         size = len(frame_list) * rows * cols
         return pl.pallas_call(
             functools.partial(
@@ -298,28 +310,30 @@
                 frames=frames,
                 rows=rows,
                 cols=cols,
-                adds=len(adds),
+                adds=frame_list[: len(adds)],
                 with_bias=with_bias,
             ),
             out_shape=jax.ShapeDtypeStruct((size, outs), dtype),
             compiler_params=params(),
-            cost_estimate=pl.CostEstimate(
-                flops=2 * size * 27 * LANES * outs, transcendentals=0, bytes_accessed=4 * size * outs
-            ),
-        )(spread, weight, *adds, *([bias] if with_bias else []))
+            cost_estimate=pl.CostEstimate(flops=cost, transcendentals=0, bytes_accessed=1),
+        )(source, weight, *adds, *([bias] if with_bias else []))
 
     near_route = [(s, near_of(s)) for s in range(n_blocks)]
     far_route = [(s, far_of(s)) for s in range(n_blocks)]
-    beyond = [
-        lax.ppermute(partial_sum(lambda s: far_of(near_of(s)), (f,)), "tm", near_route) for f in range(frames)
-    ]
-    arrived = [
-        lax.ppermute(partial_sum(far_of, (f,), (beyond[f],)), "tm", far_route) for f in range(frames)
-    ]
-    beside = lax.ppermute(partial_sum(near_of, tuple(range(frames))), "tm", near_route)
-    home = partial_sum(lambda s: s, tuple(range(frames)), (beside,), True, jnp.float32)
-    result = home + jnp.concatenate(arrived, axis=0).astype(jnp.float32)
-    return result.astype(jnp.bfloat16).reshape(frames, rows, cols, outs)
+    parts = []
+    for f in every:
+        parts.append(partial_sum(lambda s: far_of(near_of(s)), (f,), after=parts[-1] if parts else None, cost=1 << 32))
+    beyond = [lax.ppermute(part, "tm", near_route) for part in parts]
+    sums = [partial_sum(far_of, (f,), (beyond[f],)) for f in every]
+    arrived = [lax.ppermute(part, "tm", far_route) for part in sums]
+    beside = lax.ppermute(partial_sum(near_of, after=(sums[0], beyond[-1])), "tm", near_route)
+    home = partial_sum(lambda s: s, every, arrived[:1], True, jnp.float32, cost=1 << 35)
+    result = pl.pallas_call(
+        functools.partial(finish_kernel, span=rows * cols),
+        out_shape=jax.ShapeDtypeStruct((cells, outs), jnp.bfloat16),
+        compiler_params=params(),
+    )(home, beside, *arrived[1:])
+    return result.reshape(frames, rows, cols, outs)
 
 
 def splits(mesh):

time: 58 us -> 55.4 us (0.955)
  the two profiles are of different devices: /device:TPU:8 before, /device:TPU:0 now
where the time goes in v2:
time: 55.4 us; the launch traced here: 55.2 us
  waiting for transfers between devices  26.4 us (48%)
  starting transfers between devices  16.9 us (31%)
  Pallas kernels  9.35 us (17%)
  local copies, waits for them, and re-layouts  2.46 us (4%)
    ppermute x1, waiting for transfers between devices, split_body(): lax.ppermute(partial_sum(near_of, after=(sums[0], beyond[-1])), 'tm', nea...  7.06 us
    pallas_call x6, Pallas kernels, partial_sum(): pl.pallas_call(functools.partial(partial_kernel, block_of=block_of, frame...  6.68 us
    ppermute x1, waiting for transfers between devices, split_body(): got_b = lax.ppermute(same, both, route_b)  5.47 us
    ppermute x2, waiting for transfers between devices, split_body(): beyond = [lax.ppermute(part, 'tm', near_route) for part in parts]  5.39 us
    ppermute x2, waiting for transfers between devices, split_body(): arrived = [lax.ppermute(part, 'tm', far_route) for part in sums]  4.58 us
    ppermute x2, starting transfers between devices, split_body(): arrived = [lax.ppermute(part, 'tm', far_route) for part in sums]  3.97 us
    ppermute x1, starting transfers between devices, split_body(): other = lax.ppermute(own, 'tile', [(0, 1), (1, 0)])  3 us
    ppermute x1, starting transfers between devices, split_body(): got_a = lax.ppermute(following, both, route_a)  2.17 us
  transfers between devices with their start and end apart: 10, of which 9 were waited for; matrix products, arithmetic and copies ran while one was open for 2% of the time, Pallas kernels for 11%

profile of v2, /device:TPU:0, one launch (start us, length us, event | category | flops | bytes accessed | tf_op | source)
XLA Modules:
  0.0 55.2 jit_solution(3644170604881050796)
XLA Ops:
  0.0 1.1 %copy-done.1 = bf16[2,24,16,256]{3,2,1,0:T(8,128)(2,1)S(1)} copy-done((bf16[2,24,16,256]{3,2,1,0:T(8,128)(2,1)S(1)}, bf16[2,24,16,256]{3,2,1,0:T(8,128)(2,1)}, u32[]{:S(2)}) %copy-start.1) | copy-done | bytes 393240
  1.1 0.2 shard_map.55.own_ref
  1.3 3.0 %collective-permute-start = (f32[56,256]{1,0:T(8,128)S(1)}, f32[56,256]{1,0:T(8,128)S(1)}, u32[]{:S(2)}, u32[]{:S(2)}) collective-permute-start(f32[56,256]{1,0:T(8,128)S(1)} %shard_map.55.own_ref), channel_id=1, source_target_pairs={{0,2},{2,0},{1,3},{3,1},{4,6},{6,4},{5,7},{7,5},{8,10},{10,8},{9,1... | collective-permute-start | bytes 172040 | tf_op jit(solution)/shard_map/ppermute | solution.py:271
  4.3 0.7 %reshape.19.gain_ref = bf16[1,256]{1,0:T(2,128)(2,1)S(1)} reshape(bf16[256]{0:T(256)(128)(2,1)} %param.6) | data formatting | bytes 1024 | tf_op jit(solution)/shard_map/reshape | solution.py:277
  5.0 0.7 %reshape.20.bias_ref = bf16[1,256]{1,0:T(2,128)(2,1)S(1)} reshape(bf16[256]{0:T(256)(128)(2,1)} %param.7) | data formatting | bytes 1024 | tf_op jit(solution)/shard_map/reshape | solution.py:277
  5.6 0.8 %collective-permute-done.other_ref = f32[56,256]{1,0:T(8,128)S(1)} collective-permute-done((f32[56,256]{1,0:T(8,128)S(1)}, f32[56,256]{1,0:T(8,128)S(1)}, u32[]{:S(2)}, u32[]{:S(2)}) %collective-permute-start) | collective-permute-done | bytes 57376 | tf_op jit(solution)/shard_map/ppermute | solution.py:271
  6.5 0.1 shard_map.56
  6.6 2.2 %collective-permute-start.1 = (bf16[832,128]{1,0:T(8,128)(2,1)S(1)}, bf16[832,128]{1,0:T(8,128)(2,1)S(1)}, u32[]{:S(2)}, u32[]{:S(2)}) collective-permute-start(bf16[832,128]{1,0:T(8,128)(2,1)S(1)} %get-tuple-element.10), channel_id=1, source_target_pairs={{0,4},{1,12},{4,0},{5,8},{9,13},{8,5},{13,9},{12,1},{2,6},{3,14},{... | collective-permute-start | bytes 638984 | tf_op jit(solution)/shard_map/ppermute | solution.py:286
  8.7 2.1 %collective-permute-start.2 = (bf16[832,128]{1,0:T(8,128)(2,1)S(1)}, bf16[832,128]{1,0:T(8,128)(2,1)S(1)}, u32[]{:S(2)}, u32[]{:S(2)}) collective-permute-start(bf16[832,128]{1,0:T(8,128)(2,1)S(1)} %get-tuple-element.9.same_ref), channel_id=1, source_target_pairs={{0,1},{1,9},{4,5},{5,13},{9,8},{8,0},{13,12},{12,4},{2,3},{3,11},{... | collective-permute-start | bytes 638984 | tf_op jit(solution)/shard_map/ppermute | solution.py:287
  10.9 2.0 %collective-permute-done.1.a_ref = bf16[832,128]{1,0:T(8,128)(2,1)S(1)} collective-permute-done((bf16[832,128]{1,0:T(8,128)(2,1)S(1)}, bf16[832,128]{1,0:T(8,128)(2,1)S(1)}, u32[]{:S(2)}, u32[]{:S(2)}) %collective-permute-start.1) | collective-permute-done | bytes 213024 | tf_op jit(solution)/shard_map/ppermute | solution.py:286
  12.9 2.1 %collective-permute-start.3 = (bf16[832,128]{1,0:T(8,128)(2,1)S(1)}, bf16[832,128]{1,0:T(8,128)(2,1)S(1)}, u32[]{:S(2)}, u32[]{:S(2)}) collective-permute-start(bf16[832,128]{1,0:T(8,128)(2,1)S(1)} %collective-permute-done.1.a_ref), channel_id=1, source_target_pairs={{0,1},{1,0},{2,3},{3,2},{4,5},{5,4},{6,7},{7,6},{8,9},{9,8},{10,11... | collective-permute-start | bytes 638984 | tf_op jit(solution)/shard_map/ppermute | solution.py:288
  15.0 5.5 %collective-permute-done.2.b_ref = bf16[832,128]{1,0:T(8,128)(2,1)S(1)} collective-permute-done((bf16[832,128]{1,0:T(8,128)(2,1)S(1)}, bf16[832,128]{1,0:T(8,128)(2,1)S(1)}, u32[]{:S(2)}, u32[]{:S(2)}) %collective-permute-start.2) | collective-permute-done | bytes 213024 | tf_op jit(solution)/shard_map/ppermute | solution.py:287
  20.4 1.3 %collective-permute-start.4 = (bf16[832,128]{1,0:T(8,128)(2,1)S(1)}, bf16[832,128]{1,0:T(8,128)(2,1)S(1)}, u32[]{:S(2)}, u32[]{:S(2)}) collective-permute-start(bf16[832,128]{1,0:T(8,128)(2,1)S(1)} %collective-permute-done.2.b_ref), channel_id=1, source_target_pairs={{0,1},{4,5},{9,8},{13,12},{2,3},{6,7},{11,10},{15,14},{16,17},{20,... | collective-permute-start | bytes 638984 | tf_op jit(solution)/shard_map/ppermute | solution.py:289
  21.7 1.1 %collective-permute-done.4.d_ref = bf16[832,128]{1,0:T(8,128)(2,1)S(1)} collective-permute-done((bf16[832,128]{1,0:T(8,128)(2,1)S(1)}, bf16[832,128]{1,0:T(8,128)(2,1)S(1)}, u32[]{:S(2)}, u32[]{:S(2)}) %collective-permute-start.4) | collective-permute-done | bytes 213024 | tf_op jit(solution)/shard_map/ppermute | solution.py:289
  22.8 1.5 %shard_map.57.spread_ref = bf16[3,10,26,16,128]{4,3,2,1,0:T(8,128)(2,1)S(1)} custom-call(bf16[832,128]{1,0:T(8,128)(2,1)S(1)} %get-tuple-element.9.same_ref, bf16[832,128]{1,0:T(8,128)(2,1)S(1)} %collective-permute-done.1.a_ref, bf16[832,128]{1,0:T(8,128)(2,1)S(1)} %collective-permute-done.2.b_ref, bf16[832,128]{1,0:T(8,128)(2,1)S(1)} %collective-permute-done.3.c_ref, ...), custom_call_target="tpu_custom_call" | custom-call | tf_op jit(solution)/shard_map/pallas_call | solution.py:290
  24.4 0.9 %shard_map.58 = bf16[384,256]{1,0:T(8,128)(2,1)S(1)} custom-call(bf16[3,10,26,16,128]{4,3,2,1,0:T(8,128)(2,1)S(1)} %shard_map.57.spread_ref, bf16[3456,256]{1,0:T(8,128)(2,1)S(1)} %bitcast.3), custom_call_target="tpu_custom_call" | custom-call | flops 4294967296 | bytes 1 | tf_op jit(solution)/shard_map/pallas_call | solution.py:305
  25.2 0.3 collective-permute-start.5
  25.6 0.9 %shard_map.61 = bf16[384,256]{1,0:T(8,128)(2,1)S(1)} custom-call(bf16[3,10,26,16,128]{4,3,2,1,0:T(8,128)(2,1)S(1)} %shard_map.57.spread_ref, bf16[3456,256]{1,0:T(8,128)(2,1)S(1)} %bitcast.4), custom_call_target="tpu_custom_call" | custom-call | flops 4294967296 | bytes 1 | tf_op jit(solution)/shard_map/pallas_call | solution.py:305
  26.5 1.8 %collective-permute-start.7 = (bf16[384,256]{1,0:T(8,128)(2,1)S(1)}, bf16[384,256]{1,0:T(8,128)(2,1)S(1)}, u32[]{:S(2)}, u32[]{:S(2)}) collective-permute-start(bf16[384,256]{1,0:T(8,128)(2,1)S(1)} %shard_map.61), channel_id=1, source_target_pairs={{0,4},{4,0},{8,12},{12,8},{1,5},{5,1},{9,13},{13,9},{2,6},{6,2},{1... | collective-permute-start | bytes 589832 | tf_op jit(solution)/shard_map/ppermute | solution.py:326
  28.3 4.7 %collective-permute-done.5.rest_0_ = bf16[384,256]{1,0:T(8,128)(2,1)S(1)} collective-permute-done((bf16[384,256]{1,0:T(8,128)(2,1)S(1)}, bf16[384,256]{1,0:T(8,128)(2,1)S(1)}, u32[]{:S(2)}, u32[]{:S(2)}) %collective-permute-start.5) | collective-permute-done | bytes 196640 | tf_op jit(solution)/shard_map/ppermute | solution.py:326
  33.0 0.9 %shard_map.59 = bf16[384,256]{1,0:T(8,128)(2,1)S(1)} custom-call(bf16[3,10,26,16,128]{4,3,2,1,0:T(8,128)(2,1)S(1)} %shard_map.57.spread_ref, bf16[3456,256]{1,0:T(8,128)(2,1)S(1)} %bitcast.5, bf16[384,256]{1,0:T(8,128)(2,1)S(1)} %collective-permute-done.5.rest_0_), custom_call_target="tpu_custom_call" | custom-call | flops 1 | bytes 1 | tf_op jit(solution)/shard_map/pallas_call | solution.py:305
  33.9 2.1 %collective-permute-start.6 = (bf16[384,256]{1,0:T(8,128)(2,1)S(1)}, bf16[384,256]{1,0:T(8,128)(2,1)S(1)}, u32[]{:S(2)}, u32[]{:S(2)}) collective-permute-start(bf16[384,256]{1,0:T(8,128)(2,1)S(1)} %shard_map.59), channel_id=1, source_target_pairs={{0,12},{4,8},{8,4},{12,0},{1,13},{5,9},{9,5},{13,1},{2,14},{6,10},... | collective-permute-start | bytes 589832 | tf_op jit(solution)/shard_map/ppermute | solution.py:328
  36.0 0.7 %collective-permute-done.7.rest_0_ = bf16[384,256]{1,0:T(8,128)(2,1)S(1)} collective-permute-done((bf16[384,256]{1,0:T(8,128)(2,1)S(1)}, bf16[384,256]{1,0:T(8,128)(2,1)S(1)}, u32[]{:S(2)}, u32[]{:S(2)}) %collective-permute-start.7) | collective-permute-done | bytes 196640 | tf_op jit(solution)/shard_map/ppermute | solution.py:326
  36.7 0.9 %shard_map.63 = bf16[384,256]{1,0:T(8,128)(2,1)S(1)} custom-call(bf16[3,10,26,16,128]{4,3,2,1,0:T(8,128)(2,1)S(1)} %shard_map.57.spread_ref, bf16[3456,256]{1,0:T(8,128)(2,1)S(1)} %bitcast.6, bf16[384,256]{1,0:T(8,128)(2,1)S(1)} %collective-permute-done.7.rest_0_), custom_call_target="tpu_custom_call" | custom-call | flops 1 | bytes 1 | tf_op jit(solution)/shard_map/pallas_call | solution.py:305
  37.6 1.9 %collective-permute-start.9 = (bf16[384,256]{1,0:T(8,128)(2,1)S(1)}, bf16[384,256]{1,0:T(8,128)(2,1)S(1)}, u32[]{:S(2)}, u32[]{:S(2)}) collective-permute-start(bf16[384,256]{1,0:T(8,128)(2,1)S(1)} %shard_map.63), channel_id=1, source_target_pairs={{0,12},{4,8},{8,4},{12,0},{1,13},{5,9},{9,5},{13,1},{2,14},{6,10},... | collective-permute-start | bytes 589832 | tf_op jit(solution)/shard_map/ppermute | solution.py:328
  39.5 1.6 %shard_map.62 = bf16[768,256]{1,0:T(8,128)(2,1)S(1)} custom-call(bf16[3,10,26,16,128]{4,3,2,1,0:T(8,128)(2,1)S(1)} %shard_map.57.spread_ref, bf16[3456,256]{1,0:T(8,128)(2,1)S(1)} %bitcast.7), custom_call_target="tpu_custom_call" | custom-call | flops 1 | bytes 1 | tf_op jit(solution)/shard_map/pallas_call | solution.py:305
  41.0 0.1 collective-permute-start.8
  41.1 0.6 %collective-permute-done.6.rest_0_ = bf16[384,256]{1,0:T(8,128)(2,1)S(1)} collective-permute-done((bf16[384,256]{1,0:T(8,128)(2,1)S(1)}, bf16[384,256]{1,0:T(8,128)(2,1)S(1)}, u32[]{:S(2)}, u32[]{:S(2)}) %collective-permute-start.6) | collective-permute-done | bytes 196640 | tf_op jit(solution)/shard_map/ppermute | solution.py:328
  41.7 1.6 %shard_map.60.home_ref = f32[768,256]{1,0:T(8,128)S(1)} custom-call(bf16[3,10,26,16,128]{4,3,2,1,0:T(8,128)(2,1)S(1)} %shard_map.57.spread_ref, bf16[3456,256]{1,0:T(8,128)(2,1)S(1)} %bitcast.8, bf16[384,256]{1,0:T(8,128)(2,1)S(1)} %collective-permute-done.6.rest_0_, bf16[1,256]{1,0:T(2,128)(2,1)S(1)} %reshape.22.rest_1_), custom_call_target="tpu_custom_call" | custom-call | flops 34359738368 | bytes 1 | tf_op jit(solution)/shard_map/pallas_call | solution.py:305
  43.3 4.0 %collective-permute-done.9.rest_0_ = bf16[384,256]{1,0:T(8,128)(2,1)S(1)} collective-permute-done((bf16[384,256]{1,0:T(8,128)(2,1)S(1)}, bf16[384,256]{1,0:T(8,128)(2,1)S(1)}, u32[]{:S(2)}, u32[]{:S(2)}) %collective-permute-start.9) | collective-permute-done | bytes 196640 | tf_op jit(solution)/shard_map/ppermute | solution.py:328
  47.3 7.1 %collective-permute-done.8.beside_ref = bf16[768,256]{1,0:T(8,128)(2,1)S(1)} collective-permute-done((bf16[768,256]{1,0:T(8,128)(2,1)S(1)}, bf16[768,256]{1,0:T(8,128)(2,1)S(1)}, u32[]{:S(2)}, u32[]{:S(2)}) %collective-permute-start.8) | collective-permute-done | bytes 393248 | tf_op jit(solution)/shard_map/ppermute | solution.py:329
  54.3 0.9 %shard_map.64 = bf16[768,256]{1,0:T(8,128)(2,1)} custom-call(f32[768,256]{1,0:T(8,128)S(1)} %shard_map.60.home_ref, bf16[768,256]{1,0:T(8,128)(2,1)S(1)} %collective-permute-done.8.beside_ref, bf16[384,256]{1,0:T(8,128)(2,1)S(1)} %collective-permute-done.9.rest_0_), custom_call_target="tpu_custom_call" | custom-call | tf_op jit(solution)/shard_map/pallas_call | solution.py:331
  (7 shorter events, 0.0 us)
Async XLA Ops:
  0.0 24.3 %copy-start = (bf16[27,128,256]{2,1,0:T(8,128)(2,1)S(1)}, bf16[27,128,256]{2,1,0:T(8,128)(2,1)}, u32[]{:S(2)}) copy-start(bf16[27,128,256]{2,1,0:T(8,128)(2,1)} %param.8) | copy-start | bytes 5308420
  0.0 1.1 %copy-start.1 = (bf16[2,24,16,256]{3,2,1,0:T(8,128)(2,1)S(1)}, bf16[2,24,16,256]{3,2,1,0:T(8,128)(2,1)}, u32[]{:S(2)}) copy-start(bf16[2,24,16,256]{3,2,1,0:T(8,128)(2,1)} %param.5) | copy-start | bytes 1179652
  1.3 5.2 %collective-permute-start = (f32[56,256]{1,0:T(8,128)S(1)}, f32[56,256]{1,0:T(8,128)S(1)}, u32[]{:S(2)}, u32[]{:S(2)}) collective-permute-start(f32[56,256]{1,0:T(8,128)S(1)} %shard_map.55.own_ref), channel_id=1, source_target_pairs={{0,2},{2,0},{1,3},{3,1},{4,6},{6,4},{5,7},{7,5},{8,10},{10,8},{9,1... | collective-permute-start | bytes 172040 | tf_op jit(solution)/shard_map/ppermute | solution.py:271
  6.6 6.3 %collective-permute-start.1 = (bf16[832,128]{1,0:T(8,128)(2,1)S(1)}, bf16[832,128]{1,0:T(8,128)(2,1)S(1)}, u32[]{:S(2)}, u32[]{:S(2)}) collective-permute-start(bf16[832,128]{1,0:T(8,128)(2,1)S(1)} %get-tuple-element.10), channel_id=1, source_target_pairs={{0,4},{1,12},{4,0},{5,8},{9,13},{8,5},{13,9},{12,1},{2,6},{3,14},{... | collective-permute-start | bytes 638984 | tf_op jit(solution)/shard_map/ppermute | solution.py:286
  8.7 11.7 %collective-permute-start.2 = (bf16[832,128]{1,0:T(8,128)(2,1)S(1)}, bf16[832,128]{1,0:T(8,128)(2,1)S(1)}, u32[]{:S(2)}, u32[]{:S(2)}) collective-permute-start(bf16[832,128]{1,0:T(8,128)(2,1)S(1)} %get-tuple-element.9.same_ref), channel_id=1, source_target_pairs={{0,1},{1,9},{4,5},{5,13},{9,8},{8,0},{13,12},{12,4},{2,3},{3,11},{... | collective-permute-start | bytes 638984 | tf_op jit(solution)/shard_map/ppermute | solution.py:287
  12.9 8.9 %collective-permute-start.3 = (bf16[832,128]{1,0:T(8,128)(2,1)S(1)}, bf16[832,128]{1,0:T(8,128)(2,1)S(1)}, u32[]{:S(2)}, u32[]{:S(2)}) collective-permute-start(bf16[832,128]{1,0:T(8,128)(2,1)S(1)} %collective-permute-done.1.a_ref), channel_id=1, source_target_pairs={{0,1},{1,0},{2,3},{3,2},{4,5},{5,4},{6,7},{7,6},{8,9},{9,8},{10,11... | collective-permute-start | bytes 638984 | tf_op jit(solution)/shard_map/ppermute | solution.py:288
  20.4 2.4 %collective-permute-start.4 = (bf16[832,128]{1,0:T(8,128)(2,1)S(1)}, bf16[832,128]{1,0:T(8,128)(2,1)S(1)}, u32[]{:S(2)}, u32[]{:S(2)}) collective-permute-start(bf16[832,128]{1,0:T(8,128)(2,1)S(1)} %collective-permute-done.2.b_ref), channel_id=1, source_target_pairs={{0,1},{4,5},{9,8},{13,12},{2,3},{6,7},{11,10},{15,14},{16,17},{20,... | collective-permute-start | bytes 638984 | tf_op jit(solution)/shard_map/ppermute | solution.py:289
  25.2 7.8 %collective-permute-start.5 = (bf16[384,256]{1,0:T(8,128)(2,1)S(1)}, bf16[384,256]{1,0:T(8,128)(2,1)S(1)}, u32[]{:S(2)}, u32[]{:S(2)}) collective-permute-start(bf16[384,256]{1,0:T(8,128)(2,1)S(1)} %shard_map.58), channel_id=1, source_target_pairs={{0,4},{4,0},{8,12},{12,8},{1,5},{5,1},{9,13},{13,9},{2,6},{6,2},{1... | collective-permute-start | bytes 589832 | tf_op jit(solution)/shard_map/ppermute | solution.py:326
  26.5 9.6 %copy-start.2 = (bf16[256]{0:T(256)(128)(2,1)S(1)}, bf16[256]{0:T(256)(128)(2,1)}, u32[]{:S(2)}) copy-start(bf16[256]{0:T(256)(128)(2,1)} %param.9) | copy-start | bytes 1540
  26.5 10.2 %collective-permute-start.7 = (bf16[384,256]{1,0:T(8,128)(2,1)S(1)}, bf16[384,256]{1,0:T(8,128)(2,1)S(1)}, u32[]{:S(2)}, u32[]{:S(2)}) collective-permute-start(bf16[384,256]{1,0:T(8,128)(2,1)S(1)} %shard_map.61), channel_id=1, source_target_pairs={{0,4},{4,0},{8,12},{12,8},{1,5},{5,1},{9,13},{13,9},{2,6},{6,2},{1... | collective-permute-start | bytes 589832 | tf_op jit(solution)/shard_map/ppermute | solution.py:326
  33.9 7.8 %collective-permute-start.6 = (bf16[384,256]{1,0:T(8,128)(2,1)S(1)}, bf16[384,256]{1,0:T(8,128)(2,1)S(1)}, u32[]{:S(2)}, u32[]{:S(2)}) collective-permute-start(bf16[384,256]{1,0:T(8,128)(2,1)S(1)} %shard_map.59), channel_id=1, source_target_pairs={{0,12},{4,8},{8,4},{12,0},{1,13},{5,9},{9,5},{13,1},{2,14},{6,10},... | collective-permute-start | bytes 589832 | tf_op jit(solution)/shard_map/ppermute | solution.py:328
  37.6 9.7 %collective-permute-start.9 = (bf16[384,256]{1,0:T(8,128)(2,1)S(1)}, bf16[384,256]{1,0:T(8,128)(2,1)S(1)}, u32[]{:S(2)}, u32[]{:S(2)}) collective-permute-start(bf16[384,256]{1,0:T(8,128)(2,1)S(1)} %shard_map.63), channel_id=1, source_target_pairs={{0,12},{4,8},{8,4},{12,0},{1,13},{5,9},{9,5},{13,1},{2,14},{6,10},... | collective-permute-start | bytes 589832 | tf_op jit(solution)/shard_map/ppermute | solution.py:328
  41.0 13.3 %collective-permute-start.8 = (bf16[768,256]{1,0:T(8,128)(2,1)S(1)}, bf16[768,256]{1,0:T(8,128)(2,1)S(1)}, u32[]{:S(2)}, u32[]{:S(2)}) collective-permute-start(bf16[768,256]{1,0:T(8,128)(2,1)S(1)} %shard_map.62), channel_id=1, source_target_pairs={{0,4},{4,0},{8,12},{12,8},{1,5},{5,1},{9,13},{13,9},{2,6},{6,2},{1... | collective-permute-start | bytes 1179656 | tf_op jit(solution)/shard_map/ppermute | solution.py:329

commit v3 on v2

--- a/solution.py
+++ b/solution.py
@@ -11,7 +11,7 @@
 GROUPS = 32
 EPS = 1e-06
 LANES = 128
-VMEM = 48 << 20
+VMEM = 24 << 20
 STAT_ROWS = 16
 
 
@@ -216,12 +216,12 @@
             out_ref[2, at, 1 : rows + 1] = right.astype(jnp.bfloat16)
 
 
-def partial_kernel(spread_ref, weight_ref, *rest, block_of, frame_list, frames, rows, cols, adds, with_bias):
-    out_ref = rest[-1]
-    block = block_of(lax.axis_index("tm"))
+def partial_kernel(spread_ref, weight_ref, *rest, jobs, n_adds, n_outs, frames, rows, cols, with_bias):
+    outs = rest[len(rest) - n_outs :]
+    s = lax.axis_index("tm")
     span = rows * cols
-    for k, f in enumerate(frame_list):
-        at = block * frames + f
+    for block_of, f, out, place, added in jobs:
+        at = block_of(s) * frames + f
         stacked = jnp.concatenate(
             [
                 spread_ref[d, at + a, b : b + rows].reshape(span, LANES)
@@ -232,12 +232,11 @@
             axis=1,
         )
         total = jnp.dot(stacked, weight_ref[...], preferred_element_type=jnp.float32)
-        for ref, frame in zip(rest, adds):
-            if frame == f:
-                total = total + ref[...].astype(jnp.float32)
+        if added is not None:
+            total = total + rest[added][...].astype(jnp.float32)
         if with_bias:
-            total = total + rest[len(adds)][...].astype(jnp.float32)
-        out_ref[k * span : (k + 1) * span] = total.astype(out_ref.dtype)
+            total = total + rest[n_adds][...].astype(jnp.float32)
+        outs[out][place * span : (place + 1) * span] = total.astype(outs[out].dtype)
 
 
 def finish_kernel(home_ref, beside_ref, *rest, span):
@@ -299,35 +298,48 @@
 
     every = tuple(range(frames))
 
-    def partial_sum(block_of, frame_list=every, adds=(), with_bias=False, dtype=jnp.bfloat16, after=None, cost=1):
+    def partial_sums(jobs, spans, adds=(), with_bias=False, dtype=jnp.bfloat16, after=None, cost=1):
         source = spread if after is None else lax.optimization_barrier((spread, after))[0]
-        size = len(frame_list) * rows * cols
         return pl.pallas_call(
             functools.partial(
                 partial_kernel,
-                block_of=block_of,
-                frame_list=frame_list,
+                jobs=jobs,
+                n_adds=len(adds),
+                n_outs=len(spans),
                 frames=frames,
                 rows=rows,
                 cols=cols,
-                adds=frame_list[: len(adds)],
                 with_bias=with_bias,
             ),
-            out_shape=jax.ShapeDtypeStruct((size, outs), dtype),
+            out_shape=[jax.ShapeDtypeStruct((n * rows * cols, outs), dtype) for n in spans],
             compiler_params=params(),
             cost_estimate=pl.CostEstimate(flops=cost, transcendentals=0, bytes_accessed=1),
         )(source, weight, *adds, *([bias] if with_bias else []))
+
+    def beyond_of(s):
+        return far_of(near_of(s))
 
     near_route = [(s, near_of(s)) for s in range(n_blocks)]
     far_route = [(s, far_of(s)) for s in range(n_blocks)]
     parts = []
     for f in every:
-        parts.append(partial_sum(lambda s: far_of(near_of(s)), (f,), after=parts[-1] if parts else None, cost=1 << 32))
-    beyond = [lax.ppermute(part, "tm", near_route) for part in parts]
-    sums = [partial_sum(far_of, (f,), (beyond[f],)) for f in every]
+        jobs, spans = [(beyond_of, f, 0, 0, None)], [1]
+        if f == frames - 1:
+            jobs += [(near_of, g, 1, g, None) for g in every]
+            spans += [frames]
+        parts.append(partial_sums(jobs, spans, after=parts[-1] if parts else None, cost=1 << 32))
+    beyond = [lax.ppermute(part[0], "tm", near_route) for part in parts]
+    sums = [partial_sums([(far_of, f, 0, 0, 0)], [1], (beyond[f],))[0] for f in every]
     arrived = [lax.ppermute(part, "tm", far_route) for part in sums]
-    beside = lax.ppermute(partial_sum(near_of, after=(sums[0], beyond[-1])), "tm", near_route)
-    home = partial_sum(lambda s: s, every, arrived[:1], True, jnp.float32, cost=1 << 35)
+    beside = lax.ppermute(parts[-1][1], "tm", near_route)
+    home = partial_sums(
+        [(lambda s: s, f, 0, f, None if f else 0) for f in every],
+        [frames],
+        arrived[:1],
+        True,
+        jnp.float32,
+        cost=1 << 35,
+    )[0]
     result = pl.pallas_call(
         functools.partial(finish_kernel, span=rows * cols),
         out_shape=jax.ShapeDtypeStruct((cells, outs), jnp.bfloat16),

time: 55.4 us -> 53.6 us (0.968)
  waiting for transfers between devices: 26.4 us -> 24.7 us
    ppermute x3, waiting for transfers between devices: 12.4 us -> 3.11 us  [the longest x2 3.11 us: split_body(): beyond = [lax.ppermute(part[0], 'tm', near_route) for part in parts]]
    ppermute x2, waiting for transfers between devices: 4.58 us -> 13.9 us  [split_body(): arrived = [lax.ppermute(part, 'tm', far_route) for part in sums]]
    ppermute x1, starting transfers between devices: 2.14 us -> 0.07 us  [split_body(): got_b = lax.ppermute(same, both, route_b)]
    ppermute x1, waiting for transfers between devices: 1.99 us -> 0.01 us  [split_body(): got_a = lax.ppermute(following, both, route_a)]
    ppermute x1, waiting for transfers between devices: 0.01 us -> 1.09 us  [split_body(): got_c = lax.ppermute(got_a, 'chan', [(0, 1), (1, 0)])]
    ppermute x1, starting transfers between devices: 2.08 us -> 3.15 us  [split_body(): got_c = lax.ppermute(got_a, 'chan', [(0, 1), (1, 0)])]
    ppermute x1, waiting for transfers between devices: 1.05 us -> 0.01 us  [split_body(): got_d = lax.ppermute(got_b, both, route_d)]
    ppermute x3, starting transfers between devices: 2.24 us -> 3.11 us  [the longest x2 2.17 us: split_body(): beyond = [lax.ppermute(part[0], 'tm', near_route) for part in parts]]
  transfers between devices with their start and end apart: 10 -> 10, of which waited for: 9 -> 6; matrix products, arithmetic and copies ran while one was open for 2% -> 2% of each run, Pallas kernels for 11% -> 11%
where the time goes in v3:
time: 53.6 us; the launch traced here: 53.4 us
  waiting for transfers between devices  24.7 us (46%)
  starting transfers between devices  17 us (32%)
  Pallas kernels  9.18 us (17%)
  local copies, waits for them, and re-layouts  2.46 us (5%)
    ppermute x2, waiting for transfers between devices, split_body(): arrived = [lax.ppermute(part, 'tm', far_route) for part in sums]  13.9 us
    pallas_call x5, Pallas kernels, partial_sums(): pl.pallas_call(functools.partial(partial_kernel, jobs=jobs, n_adds=len(ad...  6.52 us
    ppermute x1, waiting for transfers between devices, split_body(): got_b = lax.ppermute(same, both, route_b)  5.79 us
    ppermute x2, starting transfers between devices, split_body(): arrived = [lax.ppermute(part, 'tm', far_route) for part in sums]  4.19 us
    ppermute x1, starting transfers between devices, split_body(): got_c = lax.ppermute(got_a, 'chan', [(0, 1), (1, 0)])  3.15 us
    ppermute x2, waiting for transfers between devices, split_body(): beyond = [lax.ppermute(part[0], 'tm', near_route) for part in parts]  3.11 us
    ppermute x1, starting transfers between devices, split_body(): other = lax.ppermute(own, 'tile', [(0, 1), (1, 0)])  3 us
    ppermute x2, starting transfers between devices, split_body(): beyond = [lax.ppermute(part[0], 'tm', near_route) for part in parts]  2.17 us
  transfers between devices with their start and end apart: 10, of which 6 were waited for; matrix products, arithmetic and copies ran while one was open for 2% of the time, Pallas kernels for 11%

profile of v3, /device:TPU:0, one launch (start us, length us, event | category | flops | bytes accessed | tf_op | source)
XLA Modules:
  0.0 53.4 jit_solution(16245519072232684082)
XLA Ops:
  0.0 1.1 %copy-done.1 = bf16[2,24,16,256]{3,2,1,0:T(8,128)(2,1)S(1)} copy-done((bf16[2,24,16,256]{3,2,1,0:T(8,128)(2,1)S(1)}, bf16[2,24,16,256]{3,2,1,0:T(8,128)(2,1)}, u32[]{:S(2)}) %copy-start.1) | copy-done | bytes 393240
  1.1 0.2 shard_map.55.own_ref
  1.3 3.0 %collective-permute-start = (f32[56,256]{1,0:T(8,128)S(1)}, f32[56,256]{1,0:T(8,128)S(1)}, u32[]{:S(2)}, u32[]{:S(2)}) collective-permute-start(f32[56,256]{1,0:T(8,128)S(1)} %shard_map.55.own_ref), channel_id=1, source_target_pairs={{0,2},{2,0},{1,3},{3,1},{4,6},{6,4},{5,7},{7,5},{8,10},{10,8},{9,1... | collective-permute-start | bytes 172040 | tf_op jit(solution)/shard_map/ppermute | solution.py:270
  4.3 0.7 %reshape.19.gain_ref = bf16[1,256]{1,0:T(2,128)(2,1)S(1)} reshape(bf16[256]{0:T(256)(128)(2,1)} %param.6) | data formatting | bytes 1024 | tf_op jit(solution)/shard_map/reshape | solution.py:276
  5.0 0.7 %reshape.20.bias_ref = bf16[1,256]{1,0:T(2,128)(2,1)S(1)} reshape(bf16[256]{0:T(256)(128)(2,1)} %param.7) | data formatting | bytes 1024 | tf_op jit(solution)/shard_map/reshape | solution.py:276
  5.6 0.8 %collective-permute-done.other_ref = f32[56,256]{1,0:T(8,128)S(1)} collective-permute-done((f32[56,256]{1,0:T(8,128)S(1)}, f32[56,256]{1,0:T(8,128)S(1)}, u32[]{:S(2)}, u32[]{:S(2)}) %collective-permute-start) | collective-permute-done | bytes 57376 | tf_op jit(solution)/shard_map/ppermute | solution.py:270
  6.5 0.1 shard_map.56
  6.6 0.1 collective-permute-start.2
  6.7 2.2 %collective-permute-start.1 = (bf16[832,128]{1,0:T(8,128)(2,1)S(1)}, bf16[832,128]{1,0:T(8,128)(2,1)S(1)}, u32[]{:S(2)}, u32[]{:S(2)}) collective-permute-start(bf16[832,128]{1,0:T(8,128)(2,1)S(1)} %get-tuple-element.11), channel_id=1, source_target_pairs={{0,4},{1,12},{4,0},{5,8},{9,13},{8,5},{13,9},{12,1},{2,6},{3,14},{... | collective-permute-start | bytes 638984 | tf_op jit(solution)/shard_map/ppermute | solution.py:285
  8.8 5.8 %collective-permute-done.2.b_ref = bf16[832,128]{1,0:T(8,128)(2,1)S(1)} collective-permute-done((bf16[832,128]{1,0:T(8,128)(2,1)S(1)}, bf16[832,128]{1,0:T(8,128)(2,1)S(1)}, u32[]{:S(2)}, u32[]{:S(2)}) %collective-permute-start.2) | collective-permute-done | bytes 213024 | tf_op jit(solution)/shard_map/ppermute | solution.py:286
  14.6 1.3 %collective-permute-start.4 = (bf16[832,128]{1,0:T(8,128)(2,1)S(1)}, bf16[832,128]{1,0:T(8,128)(2,1)S(1)}, u32[]{:S(2)}, u32[]{:S(2)}) collective-permute-start(bf16[832,128]{1,0:T(8,128)(2,1)S(1)} %collective-permute-done.2.b_ref), channel_id=1, source_target_pairs={{0,1},{4,5},{9,8},{13,12},{2,3},{6,7},{11,10},{15,14},{16,17},{20,... | collective-permute-start | bytes 638984 | tf_op jit(solution)/shard_map/ppermute | solution.py:288
  15.9 0.0 collective-permute-done.1.a_ref
  15.9 3.2 %collective-permute-start.3 = (bf16[832,128]{1,0:T(8,128)(2,1)S(1)}, bf16[832,128]{1,0:T(8,128)(2,1)S(1)}, u32[]{:S(2)}, u32[]{:S(2)}) collective-permute-start(bf16[832,128]{1,0:T(8,128)(2,1)S(1)} %collective-permute-done.1.a_ref), channel_id=1, source_target_pairs={{0,1},{1,0},{2,3},{3,2},{4,5},{5,4},{6,7},{7,6},{8,9},{9,8},{10,11... | collective-permute-start | bytes 638984 | tf_op jit(solution)/shard_map/ppermute | solution.py:287
  19.1 1.1 %collective-permute-done.3.c_ref = bf16[832,128]{1,0:T(8,128)(2,1)S(1)} collective-permute-done((bf16[832,128]{1,0:T(8,128)(2,1)S(1)}, bf16[832,128]{1,0:T(8,128)(2,1)S(1)}, u32[]{:S(2)}, u32[]{:S(2)}) %collective-permute-start.3) | collective-permute-done | bytes 213024 | tf_op jit(solution)/shard_map/ppermute | solution.py:287
  20.2 1.5 %shard_map.57.spread_ref = bf16[3,10,26,16,128]{4,3,2,1,0:T(8,128)(2,1)S(1)} custom-call(bf16[832,128]{1,0:T(8,128)(2,1)S(1)} %get-tuple-element.10.same_ref, bf16[832,128]{1,0:T(8,128)(2,1)S(1)} %collective-permute-done.1.a_ref, bf16[832,128]{1,0:T(8,128)(2,1)S(1)} %collective-permute-done.2.b_ref, bf16[832,128]{1,0:T(8,128)(2,1)S(1)} %collective-permute-done.3.c_ref, ...), custom_call_target="tpu_custom_call" | custom-call | tf_op jit(solution)/shard_map/pallas_call | solution.py:289
  21.7 0.9 %shard_map.58 = bf16[384,256]{1,0:T(8,128)(2,1)S(1)} custom-call(bf16[3,10,26,16,128]{4,3,2,1,0:T(8,128)(2,1)S(1)} %shard_map.57.spread_ref, bf16[3456,256]{1,0:T(8,128)(2,1)S(1)} %bitcast.3), custom_call_target="tpu_custom_call" | custom-call | flops 4294967296 | bytes 1 | tf_op jit(solution)/shard_map/pallas_call | solution.py:303
  22.6 1.9 %collective-permute-start.5 = (bf16[384,256]{1,0:T(8,128)(2,1)S(1)}, bf16[384,256]{1,0:T(8,128)(2,1)S(1)}, u32[]{:S(2)}, u32[]{:S(2)}) collective-permute-start(bf16[384,256]{1,0:T(8,128)(2,1)S(1)} %shard_map.58), channel_id=1, source_target_pairs={{0,4},{4,0},{8,12},{12,8},{1,5},{5,1},{9,13},{13,9},{2,6},{6,2},{1... | collective-permute-start | bytes 589832 | tf_op jit(solution)/shard_map/ppermute | solution.py:331
  24.5 2.3 %shard_map.61 = (bf16[384,256]{1,0:T(8,128)(2,1)S(1)}, bf16[768,256]{1,0:T(8,128)(2,1)S(1)}) custom-call(bf16[3,10,26,16,128]{4,3,2,1,0:T(8,128)(2,1)S(1)} %shard_map.57.spread_ref, bf16[3456,256]{1,0:T(8,128)(2,1)S(1)} %bitcast.4), custom_call_target="tpu_custom_call" | custom-call | flops 4294967296 | bytes 1 | tf_op jit(solution)/shard_map/pallas_call | solution.py:303
  26.8 0.0 copy-start.2
  26.8 0.3 collective-permute-start.8
  27.1 3.1 %collective-permute-done.5.rest_0_ = bf16[384,256]{1,0:T(8,128)(2,1)S(1)} collective-permute-done((bf16[384,256]{1,0:T(8,128)(2,1)S(1)}, bf16[384,256]{1,0:T(8,128)(2,1)S(1)}, u32[]{:S(2)}, u32[]{:S(2)}) %collective-permute-start.5) | collective-permute-done | bytes 196640 | tf_op jit(solution)/shard_map/ppermute | solution.py:331
  30.2 0.9 %shard_map.59 = bf16[384,256]{1,0:T(8,128)(2,1)S(1)} custom-call(bf16[3,10,26,16,128]{4,3,2,1,0:T(8,128)(2,1)S(1)} %shard_map.57.spread_ref, bf16[3456,256]{1,0:T(8,128)(2,1)S(1)} %bitcast.5, bf16[384,256]{1,0:T(8,128)(2,1)S(1)} %collective-permute-done.5.rest_0_), custom_call_target="tpu_custom_call" | custom-call | flops 1 | bytes 1 | tf_op jit(solution)/shard_map/pallas_call | solution.py:303
  31.1 2.3 %collective-permute-start.6 = (bf16[384,256]{1,0:T(8,128)(2,1)S(1)}, bf16[384,256]{1,0:T(8,128)(2,1)S(1)}, u32[]{:S(2)}, u32[]{:S(2)}) collective-permute-start(bf16[384,256]{1,0:T(8,128)(2,1)S(1)} %shard_map.59), channel_id=1, source_target_pairs={{0,12},{4,8},{8,4},{12,0},{1,13},{5,9},{9,5},{13,1},{2,14},{6,10},... | collective-permute-start | bytes 589832 | tf_op jit(solution)/shard_map/ppermute | solution.py:333
  33.4 0.9 %collective-permute-start.7 = (bf16[768,256]{1,0:T(8,128)(2,1)S(1)}, bf16[768,256]{1,0:T(8,128)(2,1)S(1)}, u32[]{:S(2)}, u32[]{:S(2)}) collective-permute-start(bf16[768,256]{1,0:T(8,128)(2,1)S(1)} %get-tuple-element.13), channel_id=1, source_target_pairs={{0,4},{4,0},{8,12},{12,8},{1,5},{5,1},{9,13},{13,9},{2,6},{6,2},{1... | collective-permute-start | bytes 1179656 | tf_op jit(solution)/shard_map/ppermute | solution.py:334
  34.4 0.0 collective-permute-done.8.rest_0_
  34.4 0.9 %shard_map.62 = bf16[384,256]{1,0:T(8,128)(2,1)S(1)} custom-call(bf16[3,10,26,16,128]{4,3,2,1,0:T(8,128)(2,1)S(1)} %shard_map.57.spread_ref, bf16[3456,256]{1,0:T(8,128)(2,1)S(1)} %bitcast.6, bf16[384,256]{1,0:T(8,128)(2,1)S(1)} %collective-permute-done.8.rest_0_), custom_call_target="tpu_custom_call" | custom-call | flops 1 | bytes 1 | tf_op jit(solution)/shard_map/pallas_call | solution.py:303
  35.3 1.9 %collective-permute-start.9 = (bf16[384,256]{1,0:T(8,128)(2,1)S(1)}, bf16[384,256]{1,0:T(8,128)(2,1)S(1)}, u32[]{:S(2)}, u32[]{:S(2)}) collective-permute-start(bf16[384,256]{1,0:T(8,128)(2,1)S(1)} %shard_map.62), channel_id=1, source_target_pairs={{0,12},{4,8},{8,4},{12,0},{1,13},{5,9},{9,5},{13,1},{2,14},{6,10},... | collective-permute-start | bytes 589832 | tf_op jit(solution)/shard_map/ppermute | solution.py:333
  37.1 3.7 %collective-permute-done.6.rest_0_ = bf16[384,256]{1,0:T(8,128)(2,1)S(1)} collective-permute-done((bf16[384,256]{1,0:T(8,128)(2,1)S(1)}, bf16[384,256]{1,0:T(8,128)(2,1)S(1)}, u32[]{:S(2)}, u32[]{:S(2)}) %collective-permute-start.6) | collective-permute-done | bytes 196640 | tf_op jit(solution)/shard_map/ppermute | solution.py:333
  40.9 1.6 %shard_map.60.home_ref = f32[768,256]{1,0:T(8,128)S(1)} custom-call(bf16[3,10,26,16,128]{4,3,2,1,0:T(8,128)(2,1)S(1)} %shard_map.57.spread_ref, bf16[3456,256]{1,0:T(8,128)(2,1)S(1)} %bitcast.7, bf16[384,256]{1,0:T(8,128)(2,1)S(1)} %collective-permute-done.6.rest_0_, bf16[1,256]{1,0:T(2,128)(2,1)S(1)} %reshape.22.rest_1_), custom_call_target="tpu_custom_call" | custom-call | flops 34359738368 | bytes 1 | tf_op jit(solution)/shard_map/pallas_call | solution.py:303
  42.4 10.1 %collective-permute-done.9.rest_0_ = bf16[384,256]{1,0:T(8,128)(2,1)S(1)} collective-permute-done((bf16[384,256]{1,0:T(8,128)(2,1)S(1)}, bf16[384,256]{1,0:T(8,128)(2,1)S(1)}, u32[]{:S(2)}, u32[]{:S(2)}) %collective-permute-start.9) | collective-permute-done | bytes 196640 | tf_op jit(solution)/shard_map/ppermute | solution.py:333
  52.6 0.0 collective-permute-done.7.beside_ref
  52.6 0.8 %shard_map.63 = bf16[768,256]{1,0:T(8,128)(2,1)} custom-call(f32[768,256]{1,0:T(8,128)S(1)} %shard_map.60.home_ref, bf16[768,256]{1,0:T(8,128)(2,1)S(1)} %collective-permute-done.7.beside_ref, bf16[384,256]{1,0:T(8,128)(2,1)S(1)} %collective-permute-done.9.rest_0_), custom_call_target="tpu_custom_call" | custom-call | tf_op jit(solution)/shard_map/pallas_call | solution.py:343
  (6 shorter events, 0.0 us)
Async XLA Ops:
  0.0 21.7 %copy-start = (bf16[27,128,256]{2,1,0:T(8,128)(2,1)S(1)}, bf16[27,128,256]{2,1,0:T(8,128)(2,1)}, u32[]{:S(2)}) copy-start(bf16[27,128,256]{2,1,0:T(8,128)(2,1)} %param.8) | copy-start | bytes 5308420
  0.0 1.1 %copy-start.1 = (bf16[2,24,16,256]{3,2,1,0:T(8,128)(2,1)S(1)}, bf16[2,24,16,256]{3,2,1,0:T(8,128)(2,1)}, u32[]{:S(2)}) copy-start(bf16[2,24,16,256]{3,2,1,0:T(8,128)(2,1)} %param.5) | copy-start | bytes 1179652
  1.3 5.2 %collective-permute-start = (f32[56,256]{1,0:T(8,128)S(1)}, f32[56,256]{1,0:T(8,128)S(1)}, u32[]{:S(2)}, u32[]{:S(2)}) collective-permute-start(f32[56,256]{1,0:T(8,128)S(1)} %shard_map.55.own_ref), channel_id=1, source_target_pairs={{0,2},{2,0},{1,3},{3,1},{4,6},{6,4},{5,7},{7,5},{8,10},{10,8},{9,1... | collective-permute-start | bytes 172040 | tf_op jit(solution)/shard_map/ppermute | solution.py:270
  6.6 8.0 %collective-permute-start.2 = (bf16[832,128]{1,0:T(8,128)(2,1)S(1)}, bf16[832,128]{1,0:T(8,128)(2,1)S(1)}, u32[]{:S(2)}, u32[]{:S(2)}) collective-permute-start(bf16[832,128]{1,0:T(8,128)(2,1)S(1)} %get-tuple-element.10.same_ref), channel_id=1, source_target_pairs={{0,1},{1,9},{4,5},{5,13},{9,8},{8,0},{13,12},{12,4},{2,3},{3,11},{... | collective-permute-start | bytes 638984 | tf_op jit(solution)/shard_map/ppermute | solution.py:286
  6.7 9.3 %collective-permute-start.1 = (bf16[832,128]{1,0:T(8,128)(2,1)S(1)}, bf16[832,128]{1,0:T(8,128)(2,1)S(1)}, u32[]{:S(2)}, u32[]{:S(2)}) collective-permute-start(bf16[832,128]{1,0:T(8,128)(2,1)S(1)} %get-tuple-element.11), channel_id=1, source_target_pairs={{0,4},{1,12},{4,0},{5,8},{9,13},{8,5},{13,9},{12,1},{2,6},{3,14},{... | collective-permute-start | bytes 638984 | tf_op jit(solution)/shard_map/ppermute | solution.py:285
  14.6 4.5 %collective-permute-start.4 = (bf16[832,128]{1,0:T(8,128)(2,1)S(1)}, bf16[832,128]{1,0:T(8,128)(2,1)S(1)}, u32[]{:S(2)}, u32[]{:S(2)}) collective-permute-start(bf16[832,128]{1,0:T(8,128)(2,1)S(1)} %collective-permute-done.2.b_ref), channel_id=1, source_target_pairs={{0,1},{4,5},{9,8},{13,12},{2,3},{6,7},{11,10},{15,14},{16,17},{20,... | collective-permute-start | bytes 638984 | tf_op jit(solution)/shard_map/ppermute | solution.py:288
  15.9 4.2 %collective-permute-start.3 = (bf16[832,128]{1,0:T(8,128)(2,1)S(1)}, bf16[832,128]{1,0:T(8,128)(2,1)S(1)}, u32[]{:S(2)}, u32[]{:S(2)}) collective-permute-start(bf16[832,128]{1,0:T(8,128)(2,1)S(1)} %collective-permute-done.1.a_ref), channel_id=1, source_target_pairs={{0,1},{1,0},{2,3},{3,2},{4,5},{5,4},{6,7},{7,6},{8,9},{9,8},{10,11... | collective-permute-start | bytes 638984 | tf_op jit(solution)/shard_map/ppermute | solution.py:287
  22.6 7.6 %collective-permute-start.5 = (bf16[384,256]{1,0:T(8,128)(2,1)S(1)}, bf16[384,256]{1,0:T(8,128)(2,1)S(1)}, u32[]{:S(2)}, u32[]{:S(2)}) collective-permute-start(bf16[384,256]{1,0:T(8,128)(2,1)S(1)} %shard_map.58), channel_id=1, source_target_pairs={{0,4},{4,0},{8,12},{12,8},{1,5},{5,1},{9,13},{13,9},{2,6},{6,2},{1... | collective-permute-start | bytes 589832 | tf_op jit(solution)/shard_map/ppermute | solution.py:331
  26.8 6.6 %copy-start.2 = (bf16[256]{0:T(256)(128)(2,1)S(1)}, bf16[256]{0:T(256)(128)(2,1)}, u32[]{:S(2)}) copy-start(bf16[256]{0:T(256)(128)(2,1)} %param.9) | copy-start | bytes 1540
  26.8 7.6 %collective-permute-start.8 = (bf16[384,256]{1,0:T(8,128)(2,1)S(1)}, bf16[384,256]{1,0:T(8,128)(2,1)S(1)}, u32[]{:S(2)}, u32[]{:S(2)}) collective-permute-start(bf16[384,256]{1,0:T(8,128)(2,1)S(1)} %get-tuple-element.14), channel_id=1, source_target_pairs={{0,4},{4,0},{8,12},{12,8},{1,5},{5,1},{9,13},{13,9},{2,6},{6,2},{1... | collective-permute-start | bytes 589832 | tf_op jit(solution)/shard_map/ppermute | solution.py:331
  31.1 9.8 %collective-permute-start.6 = (bf16[384,256]{1,0:T(8,128)(2,1)S(1)}, bf16[384,256]{1,0:T(8,128)(2,1)S(1)}, u32[]{:S(2)}, u32[]{:S(2)}) collective-permute-start(bf16[384,256]{1,0:T(8,128)(2,1)S(1)} %shard_map.59), channel_id=1, source_target_pairs={{0,12},{4,8},{8,4},{12,0},{1,13},{5,9},{9,5},{13,1},{2,14},{6,10},... | collective-permute-start | bytes 589832 | tf_op jit(solution)/shard_map/ppermute | solution.py:333
  33.4 19.2 %collective-permute-start.7 = (bf16[768,256]{1,0:T(8,128)(2,1)S(1)}, bf16[768,256]{1,0:T(8,128)(2,1)S(1)}, u32[]{:S(2)}, u32[]{:S(2)}) collective-permute-start(bf16[768,256]{1,0:T(8,128)(2,1)S(1)} %get-tuple-element.13), channel_id=1, source_target_pairs={{0,4},{4,0},{8,12},{12,8},{1,5},{5,1},{9,13},{13,9},{2,6},{6,2},{1... | collective-permute-start | bytes 1179656 | tf_op jit(solution)/shard_map/ppermute | solution.py:334
  35.3 17.3 %collective-permute-start.9 = (bf16[384,256]{1,0:T(8,128)(2,1)S(1)}, bf16[384,256]{1,0:T(8,128)(2,1)S(1)}, u32[]{:S(2)}, u32[]{:S(2)}) collective-permute-start(bf16[384,256]{1,0:T(8,128)(2,1)S(1)} %shard_map.62), channel_id=1, source_target_pairs={{0,12},{4,8},{8,4},{12,0},{1,13},{5,9},{9,5},{13,1},{2,14},{6,10},... | collective-permute-start | bytes 589832 | tf_op jit(solution)/shard_map/ppermute | solution.py:333

commit v4 on v3

--- a/solution.py
+++ b/solution.py
@@ -99,51 +99,65 @@
     return 3 - s
 
 
-def edges_kernel(latent_ref, out_ref, wide_ref, *, cells, cols):
-    wide = latent_ref[...].astype(jnp.float32)
-    edges = cells // cols
-    first = jnp.where(lax.axis_index("tile") == 0, cols - 1, 0)
-    for k in range(wide.shape[1] // LANES):
-        lanes = slice(k * LANES, (k + 1) * LANES)
-        wide_ref[...] = wide[:, lanes]
-        out_ref[:edges, lanes] = wide_ref[pl.ds(first, edges, stride=cols), :]
-    total = jnp.sum(wide, axis=0, keepdims=True)
-    square = jnp.sum(wide * wide, axis=0, keepdims=True)
-    out_ref[edges:] = jnp.concatenate([total, square, jnp.zeros((6, wide.shape[1]), jnp.float32)], axis=0)
-
-
 def three(value):
     high = value.astype(jnp.bfloat16)
     rest = value - high.astype(jnp.float32)
     mid = rest.astype(jnp.bfloat16)
     low = (rest - mid.astype(jnp.float32)).astype(jnp.bfloat16)
-    return [high, mid, low]
-
-
-def pack_kernel(latent_ref, own_ref, other_ref, gain_ref, bias_ref, same_ref, next_ref, *, cells, edges):
-    sums = own_ref[edges : edges + 2] + other_ref[edges : edges + 2]
-    tail = three(sums[0:1]) + three(sums[1:2]) + [gain_ref[...], bias_ref[...]]
-    tail = jnp.concatenate([row.astype(jnp.float32) for row in tail], axis=0)
-    tail = jnp.concatenate([tail, jnp.zeros_like(tail)], axis=0).astype(jnp.bfloat16)
-    edge = other_ref[:edges].astype(jnp.bfloat16)
-
-    def fill(out_ref, block):
-        lanes = slice(block * LANES, (block + 1) * LANES)
-        out_ref[:cells] = latent_ref[:, lanes]
-        out_ref[cells : cells + edges] = edge[:, lanes]
-        out_ref[cells + edges :] = tail[:, lanes]
-
+    return [high.astype(jnp.float32), mid.astype(jnp.float32), low.astype(jnp.float32)]
+
+
+def tail_rows(rows):
+    rows = jnp.concatenate(rows, axis=0)
+    filler = jnp.zeros((STAT_ROWS - rows.shape[0], rows.shape[1]), jnp.float32)
+    return jnp.concatenate([rows, filler], axis=0).astype(jnp.bfloat16)
+
+
+def sum_rows(wide):
+    total = jnp.sum(wide, axis=0, keepdims=True)
+    square = jnp.sum(wide * wide, axis=0, keepdims=True)
+    return three(total) + three(square)
+
+
+def by_parity(fill):
     parity = lax.axis_index("tm") % 2
 
     @pl.when(parity == 0)
     def _():
-        fill(same_ref, 0)
-        fill(next_ref, 1)
+        fill(slice(0, LANES), slice(LANES, 2 * LANES))
 
     @pl.when(parity == 1)
     def _():
-        fill(same_ref, 1)
-        fill(next_ref, 0)
+        fill(slice(LANES, 2 * LANES), slice(0, LANES))
+
+
+def cells_kernel(latent_ref, same_ref, next_ref, *, cells):
+    def fill(same, following):
+        for out_ref, lanes in ((same_ref, same), (next_ref, following)):
+            out_ref[:cells] = latent_ref[:, lanes]
+            out_ref[cells:] = tail_rows(sum_rows(latent_ref[:, lanes].astype(jnp.float32)))
+
+    by_parity(fill)
+
+
+def edges_kernel(latent_ref, gain_ref, bias_ref, same_ref, next_ref, wide_ref, *, edges, cols):
+    first = jnp.where(lax.axis_index("tile") == 0, cols - 1, 0)
+
+    def fill(same, following):
+        for out_ref, lanes in ((same_ref, same), (next_ref, following)):
+            wide = latent_ref[:, lanes].astype(jnp.float32)
+            wide_ref[...] = wide
+            out_ref[:edges] = wide_ref[pl.ds(first, edges, stride=cols), :].astype(jnp.bfloat16)
+            params_rows = [ref[:, lanes].astype(jnp.float32) for ref in (gain_ref, bias_ref)]
+            out_ref[edges:] = tail_rows(sum_rows(wide) + params_rows)
+
+    by_parity(fill)
+
+
+def join_kernel(first_ref, second_ref, out_ref):
+    split = first_ref.shape[0]
+    out_ref[:split] = first_ref[...]
+    out_ref[split:] = second_ref[...]
 
 
 def group_total(row, group_ch):
@@ -157,13 +171,15 @@
     return row
 
 
-def spread_kernel(same_ref, a_ref, b_ref, c_ref, d_ref, out_ref, own_ref, *, frames, rows, cols, entries):
+def spread_kernel(
+    same_ref, a_ref, edge_a_ref, b_ref, edge_b_ref, c_ref, d_ref, out_ref, own_ref, *, frames, rows, cols, entries
+):
     s = lax.axis_index("tm")
     home = lax.axis_index("chan") == s // 2
     tile = lax.axis_index("tile")
     cells = frames * rows * cols
     edges = frames * rows
-    base = cells + edges
+    split = cells + STAT_ROWS
 
     @pl.when(home)
     def _():
@@ -171,21 +187,23 @@
 
     @pl.when(jnp.logical_not(home))
     def _():
-        own_ref[...] = d_ref[...]
+        own_ref[...] = d_ref[:split]
 
     near, mid, far = near_of(s), mid_of(s), far_of(s)
     pieces = (
-        (own_ref, jnp.where(home, s, mid)),
-        (a_ref, jnp.where(home, near, far)),
-        (b_ref, jnp.where(home, mid, s)),
-        (c_ref, jnp.where(home, far, near)),
+        (own_ref, d_ref, split, jnp.where(home, s, mid)),
+        (a_ref, edge_a_ref, 0, jnp.where(home, near, far)),
+        (b_ref, edge_b_ref, 0, jnp.where(home, mid, s)),
+        (c_ref, c_ref, split, jnp.where(home, far, near)),
     )
-    tails = [ref[base : base + STAT_ROWS].astype(jnp.float32) for ref, _ in pieces]
-    stats = tails[0] + tails[1] + tails[2] + tails[3]
+    stats = jnp.zeros((STAT_ROWS, LANES), jnp.float32)
+    for ref, edge_ref, skip, _ in pieces:
+        last = edge_ref[skip + edges : skip + edges + STAT_ROWS].astype(jnp.float32)
+        stats = stats + ref[cells : cells + STAT_ROWS].astype(jnp.float32) + last
     total = group_total(stats[0:1] + stats[1:2] + stats[2:3], CH // GROUPS) / entries
     square = group_total(stats[3:4] + stats[4:5] + stats[5:6], CH // GROUPS) / entries
-    scale = lax.rsqrt(square - total * total + EPS) * tails[0][6:7]
-    shift = tails[0][7:8]
+    scale = lax.rsqrt(square - total * total + EPS) * last[6:7]
+    shift = last[7:8]
 
     def normed(raw):
         value = (raw.astype(jnp.float32) - total) * scale + shift
@@ -201,10 +219,10 @@
             out_ref[d, f, 1 : rows + 1] = jnp.zeros((rows, cols, LANES), jnp.bfloat16)
     col = lax.broadcasted_iota(jnp.int32, (rows, cols, LANES), 1)
     span = rows * cols
-    for ref, block in pieces:
+    for ref, edge_ref, skip, block in pieces:
         for f in range(frames):
             value = normed(ref[f * span : (f + 1) * span])
-            edge = normed(ref[cells + f * rows : cells + (f + 1) * rows])
+            edge = normed(edge_ref[skip + f * rows : skip + (f + 1) * rows])
             edge = jnp.broadcast_to(edge[:, None, :], (rows, cols, LANES))
             left = pltpu.roll(value, 1, 0).reshape(rows, cols, LANES)
             left = jnp.where(col == 0, jnp.where(tile == 1, edge, 0.0), left)
@@ -261,37 +279,55 @@
     entries = cells * n_blocks * lax.axis_size("tile") * (CH // GROUPS)
     flat = latent.reshape(cells, chans)
 
-    own = pl.pallas_call(
-        functools.partial(edges_kernel, cells=cells, cols=cols),
-        out_shape=jax.ShapeDtypeStruct((edges + 8, chans), jnp.float32),
+    def table(height):
+        return jax.ShapeDtypeStruct((height, LANES), jnp.bfloat16)
+
+    same, following = pl.pallas_call(
+        functools.partial(cells_kernel, cells=cells),
+        out_shape=(table(cells + STAT_ROWS),) * 2,
+        compiler_params=params(),
+    )(flat)
+    edge_same, edge_following = pl.pallas_call(
+        functools.partial(edges_kernel, edges=edges, cols=cols),
+        out_shape=(table(edges + STAT_ROWS),) * 2,
         scratch_shapes=[pltpu.VMEM((cells, LANES), jnp.float32)],
         compiler_params=params(),
-    )(flat)
-    other = lax.ppermute(own, "tile", [(0, 1), (1, 0)])
-    packed = jax.ShapeDtypeStruct((cells + edges + STAT_ROWS, LANES), jnp.bfloat16)
-    same, following = pl.pallas_call(
-        functools.partial(pack_kernel, cells=cells, edges=edges),
-        out_shape=(packed, packed),
-        compiler_params=params(),
-    )(flat, own, other, gn_gain.reshape(1, chans), gn_bias.reshape(1, chans))
-
-    both = ("tm", "chan")
-    route_a, route_b, route_d = [], [], []
+    )(flat, gn_gain.reshape(1, chans), gn_bias.reshape(1, chans))
+
+    route_a, route_b, edge_a, edge_b = [], [], [], []
     for s in range(n_blocks):
         h = s // 2
-        route_a += [(2 * s + h, 2 * near_of(s) + h), (2 * s + 1 - h, 2 * far_of(s) + h)]
-        route_b += [(2 * s + h, 2 * s + 1 - h), (2 * s + 1 - h, 2 * mid_of(s) + 1 - h)]
-        route_d += [(2 * s + h, 2 * s + 1 - h)]
-    got_a = lax.ppermute(following, both, route_a)
-    got_b = lax.ppermute(same, both, route_b)
-    got_c = lax.ppermute(got_a, "chan", [(0, 1), (1, 0)])
-    got_d = lax.ppermute(got_b, both, route_d)
+        hops = [
+            (route_a, edge_a, h, near_of(s), h),
+            (route_a, edge_a, 1 - h, far_of(s), h),
+            (route_b, edge_b, h, s, 1 - h),
+            (route_b, edge_b, 1 - h, mid_of(s), 1 - h),
+        ]
+        for route, edge_route, core, there, core_there in hops:
+            route.append((2 * s + core, 2 * there + core_there))
+            for x in range(2):
+                edge_route.append((4 * s + 2 * x + core, 4 * there + 2 * (1 - x) + core_there))
+    swap = [(0, 1), (1, 0)]
+    got_b = lax.ppermute(same, ("tm", "chan"), route_b)
+    got_a = lax.ppermute(following, ("tm", "chan"), route_a)
+    got_edge_b = lax.ppermute(edge_same, ("tm", "tile", "chan"), edge_b)
+    got_edge_a = lax.ppermute(edge_following, ("tm", "tile", "chan"), edge_a)
+
+    def joined(first, second):
+        return pl.pallas_call(
+            join_kernel,
+            out_shape=table(first.shape[0] + second.shape[0]),
+            compiler_params=params(),
+        )(first, second)
+
+    got_d = lax.ppermute(joined(got_b, got_edge_b), "chan", swap)
+    got_c = lax.ppermute(joined(got_a, got_edge_a), "chan", swap)
     spread = pl.pallas_call(
         functools.partial(spread_kernel, frames=frames, rows=rows, cols=cols, entries=entries),
         out_shape=jax.ShapeDtypeStruct((3, n_blocks * frames + 2, rows + 2, cols, LANES), jnp.bfloat16),
-        scratch_shapes=[pltpu.VMEM(packed.shape, jnp.bfloat16)],
+        scratch_shapes=[pltpu.VMEM(same.shape, jnp.bfloat16)],
         compiler_params=params(),
-    )(same, got_a, got_b, got_c, got_d)
+    )(same, got_a, got_edge_a, got_b, got_edge_b, got_c, got_d)
 
     weight = conv_weight.reshape(27 * LANES, outs)
     bias = conv_bias.reshape(1, outs)

time: 53.6 us -> 51.6 us (0.963)
  starting transfers between devices: 17 us -> 13.4 us
  waiting for transfers between devices: 24.7 us -> 26.2 us
    ppermute x5 -> x6, starting transfers between devices: 9.68 us -> 7.33 us  [the longest x1 3.55 us: split_body(): got_edge_b = lax.ppermute(edge_same, ('tm', 'tile', 'chan'), edge_b)]
    ppermute x5 -> x6, waiting for transfers between devices: 7.72 us -> 9 us  [the longest x1 7.81 us: split_body(): got_edge_b = lax.ppermute(edge_same, ('tm', 'tile', 'chan'), edge_b)]
    ppermute x1, starting transfers between devices: 0.94 us -> 0.01 us  [split_body(): beside = lax.ppermute(parts[-1][1], 'tm', near_route)]
    ppermute x2, waiting for transfers between devices: 3.11 us -> 4.03 us  [split_body(): beyond = [lax.ppermute(part[0], 'tm', near_route) for part in parts]]
    ppermute x2, waiting for transfers between devices: 13.9 us -> 13.1 us  [split_body(): arrived = [lax.ppermute(part, 'tm', far_route) for part in sums]]
  transfers between devices with their start and end apart: 10 -> 11, of which waited for: 6 -> 7; matrix products, arithmetic and copies ran while one was open for 2% -> 3% of each run, Pallas kernels for 11% -> 11%
where the time goes in v4:
time: 51.6 us; the launch traced here: 51.5 us
  waiting for transfers between devices  26.2 us (51%)
  starting transfers between devices  13.4 us (26%)
  Pallas kernels  9.37 us (18%)
  local copies, waits for them, and re-layouts  2.46 us (5%)
    ppermute x2, waiting for transfers between devices, split_body(): arrived = [lax.ppermute(part, 'tm', far_route) for part in sums]  13.1 us
    ppermute x1, waiting for transfers between devices, split_body(): got_edge_b = lax.ppermute(edge_same, ('tm', 'tile', 'chan'), edge_b)  7.81 us
    pallas_call x5, Pallas kernels, partial_sums(): pl.pallas_call(functools.partial(partial_kernel, jobs=jobs, n_adds=len(ad...  6.49 us
    ppermute x2, waiting for transfers between devices, split_body(): beyond = [lax.ppermute(part[0], 'tm', near_route) for part in parts]  4.03 us
    ppermute x2, starting transfers between devices, split_body(): arrived = [lax.ppermute(part, 'tm', far_route) for part in sums]  3.89 us
    ppermute x1, starting transfers between devices, split_body(): got_edge_b = lax.ppermute(edge_same, ('tm', 'tile', 'chan'), edge_b)  3.55 us
    ppermute x1, starting transfers between devices, split_body(): got_a = lax.ppermute(following, ('tm', 'chan'), route_a)  2.64 us
    ppermute x2, starting transfers between devices, split_body(): beyond = [lax.ppermute(part[0], 'tm', near_route) for part in parts]  2.15 us
  transfers between devices with their start and end apart: 11, of which 7 were waited for; matrix products, arithmetic and copies ran while one was open for 3% of the time, Pallas kernels for 11%

profile of v4, /device:TPU:0, one launch (start us, length us, event | category | flops | bytes accessed | tf_op | source)
XLA Modules:
  0.0 51.5 jit_solution(10856391003255651156)
XLA Ops:
  0.0 1.1 %copy-done.1 = bf16[2,24,16,256]{3,2,1,0:T(8,128)(2,1)S(1)} copy-done((bf16[2,24,16,256]{3,2,1,0:T(8,128)(2,1)S(1)}, bf16[2,24,16,256]{3,2,1,0:T(8,128)(2,1)}, u32[]{:S(2)}) %copy-start.1) | copy-done | bytes 393240
  1.1 0.2 shard_map.55
  1.4 0.5 collective-permute-start.2
  1.9 2.6 %collective-permute-start = (bf16[784,128]{1,0:T(8,128)(2,1)S(1)}, bf16[784,128]{1,0:T(8,128)(2,1)S(1)}, u32[]{:S(2)}, u32[]{:S(2)}) collective-permute-start(bf16[784,128]{1,0:T(8,128)(2,1)S(1)} %get-tuple-element.13), channel_id=1, source_target_pairs={{0,4},{1,12},{4,0},{5,8},{9,13},{8,5},{13,9},{12,1},{2,6},{3,14},{... | collective-permute-start | bytes 602120 | tf_op jit(solution)/shard_map/ppermute | solution.py:312
  4.5 0.7 %reshape.19.gain_ref = bf16[1,256]{1,0:T(2,128)(2,1)S(1)} reshape(bf16[256]{0:T(256)(128)(2,1)} %param.6) | data formatting | bytes 1024 | tf_op jit(solution)/shard_map/reshape | solution.py:295
  5.2 0.7 %reshape.20.bias_ref = bf16[1,256]{1,0:T(2,128)(2,1)S(1)} reshape(bf16[256]{0:T(256)(128)(2,1)} %param.7) | data formatting | bytes 1024 | tf_op jit(solution)/shard_map/reshape | solution.py:295
  5.8 0.2 shard_map.56
  6.1 3.5 %collective-permute-start.3 = (bf16[64,128]{1,0:T(8,128)(2,1)S(1)}, bf16[64,128]{1,0:T(8,128)(2,1)S(1)}, u32[]{:S(2)}, u32[]{:S(2)}) collective-permute-start(bf16[64,128]{1,0:T(8,128)(2,1)S(1)} %get-tuple-element.15), channel_id=1, source_target_pairs={{0,3},{2,1},{1,11},{3,9},{4,7},{6,5},{5,15},{7,13},{9,10},{11,8},{... | collective-permute-start | bytes 49160 | tf_op jit(solution)/shard_map/ppermute | solution.py:313
  9.6 7.8 %collective-permute-done.3.second_ref.edge_b_ref = bf16[64,128]{1,0:T(8,128)(2,1)S(1)} collective-permute-done((bf16[64,128]{1,0:T(8,128)(2,1)S(1)}, bf16[64,128]{1,0:T(8,128)(2,1)S(1)}, u32[]{:S(2)}, u32[]{:S(2)}) %collective-permute-start.3) | collective-permute-done | bytes 16416 | tf_op jit(solution)/shard_map/ppermute | solution.py:313
  17.4 0.0 collective-permute-done.2.first_ref.b_ref
  17.5 0.1 collective-permute-start.5
  17.5 0.0 collective-permute-done.first_ref.a_ref
  17.6 0.5 %collective-permute-start.4 = (bf16[848,128]{1,0:T(8,128)(2,1)S(1)}, bf16[848,128]{1,0:T(8,128)(2,1)S(1)}, u32[]{:S(2)}, u32[]{:S(2)}) collective-permute-start(bf16[848,128]{1,0:T(8,128)(2,1)S(1)} %shard_map.57), channel_id=1, source_target_pairs={{0,1},{1,0},{2,3},{3,2},{4,5},{5,4},{6,7},{7,6},{8,9},{9,8},{10,11... | collective-permute-start | bytes 651272 | tf_op jit(solution)/shard_map/ppermute | solution.py:324
  18.1 0.9 %collective-permute-done.5.d_ref = bf16[848,128]{1,0:T(8,128)(2,1)S(1)} collective-permute-done((bf16[848,128]{1,0:T(8,128)(2,1)S(1)}, bf16[848,128]{1,0:T(8,128)(2,1)S(1)}, u32[]{:S(2)}, u32[]{:S(2)}) %collective-permute-start.5) | collective-permute-done | bytes 217120 | tf_op jit(solution)/shard_map/ppermute | solution.py:323
  19.0 0.3 collective-permute-done.4.c_ref
  19.3 1.6 %shard_map.59.spread_ref = bf16[3,10,26,16,128]{4,3,2,1,0:T(8,128)(2,1)S(1)} custom-call(bf16[784,128]{1,0:T(8,128)(2,1)S(1)} %get-tuple-element.12.same_ref, bf16[784,128]{1,0:T(8,128)(2,1)S(1)} %collective-permute-done.first_ref.a_ref, bf16[64,128]{1,0:T(8,128)(2,1)S(1)} %collective-permute-done.1.second_ref.edge_a_ref, ...), custom_call_target="tpu_custom_call" | custom-call | tf_op jit(solution)/shard_map/pallas_call | solution.py:325
  20.9 0.9 %shard_map.60 = bf16[384,256]{1,0:T(8,128)(2,1)S(1)} custom-call(bf16[3,10,26,16,128]{4,3,2,1,0:T(8,128)(2,1)S(1)} %shard_map.59.spread_ref, bf16[3456,256]{1,0:T(8,128)(2,1)S(1)} %bitcast.3), custom_call_target="tpu_custom_call" | custom-call | flops 4294967296 | bytes 1 | tf_op jit(solution)/shard_map/pallas_call | solution.py:339
  21.8 0.1 collective-permute-start.6
  21.8 2.3 %shard_map.63 = (bf16[384,256]{1,0:T(8,128)(2,1)S(1)}, bf16[768,256]{1,0:T(8,128)(2,1)S(1)}) custom-call(bf16[3,10,26,16,128]{4,3,2,1,0:T(8,128)(2,1)S(1)} %shard_map.59.spread_ref, bf16[3456,256]{1,0:T(8,128)(2,1)S(1)} %bitcast.4), custom_call_target="tpu_custom_call" | custom-call | flops 4294967296 | bytes 1 | tf_op jit(solution)/shard_map/pallas_call | solution.py:339
  24.1 0.0 copy-start.2
  24.1 2.1 %collective-permute-start.9 = (bf16[384,256]{1,0:T(8,128)(2,1)S(1)}, bf16[384,256]{1,0:T(8,128)(2,1)S(1)}, u32[]{:S(2)}, u32[]{:S(2)}) collective-permute-start(bf16[384,256]{1,0:T(8,128)(2,1)S(1)} %get-tuple-element.18), channel_id=1, source_target_pairs={{0,4},{4,0},{8,12},{12,8},{1,5},{5,1},{9,13},{13,9},{2,6},{6,2},{1... | collective-permute-start | bytes 589832 | tf_op jit(solution)/shard_map/ppermute | solution.py:367
  26.2 3.3 %collective-permute-done.6.rest_0_ = bf16[384,256]{1,0:T(8,128)(2,1)S(1)} collective-permute-done((bf16[384,256]{1,0:T(8,128)(2,1)S(1)}, bf16[384,256]{1,0:T(8,128)(2,1)S(1)}, u32[]{:S(2)}, u32[]{:S(2)}) %collective-permute-start.6) | collective-permute-done | bytes 196640 | tf_op jit(solution)/shard_map/ppermute | solution.py:367
  29.5 0.9 %shard_map.61 = bf16[384,256]{1,0:T(8,128)(2,1)S(1)} custom-call(bf16[3,10,26,16,128]{4,3,2,1,0:T(8,128)(2,1)S(1)} %shard_map.59.spread_ref, bf16[3456,256]{1,0:T(8,128)(2,1)S(1)} %bitcast.5, bf16[384,256]{1,0:T(8,128)(2,1)S(1)} %collective-permute-done.6.rest_0_), custom_call_target="tpu_custom_call" | custom-call | flops 1 | bytes 1 | tf_op jit(solution)/shard_map/pallas_call | solution.py:339
  30.4 2.0 %collective-permute-start.7 = (bf16[384,256]{1,0:T(8,128)(2,1)S(1)}, bf16[384,256]{1,0:T(8,128)(2,1)S(1)}, u32[]{:S(2)}, u32[]{:S(2)}) collective-permute-start(bf16[384,256]{1,0:T(8,128)(2,1)S(1)} %shard_map.61), channel_id=1, source_target_pairs={{0,12},{4,8},{8,4},{12,0},{1,13},{5,9},{9,5},{13,1},{2,14},{6,10},... | collective-permute-start | bytes 589832 | tf_op jit(solution)/shard_map/ppermute | solution.py:369
  32.4 0.0 collective-permute-start.8
  32.4 0.7 %collective-permute-done.9.rest_0_ = bf16[384,256]{1,0:T(8,128)(2,1)S(1)} collective-permute-done((bf16[384,256]{1,0:T(8,128)(2,1)S(1)}, bf16[384,256]{1,0:T(8,128)(2,1)S(1)}, u32[]{:S(2)}, u32[]{:S(2)}) %collective-permute-start.9) | collective-permute-done | bytes 196640 | tf_op jit(solution)/shard_map/ppermute | solution.py:367
  33.1 0.9 %shard_map.64 = bf16[384,256]{1,0:T(8,128)(2,1)S(1)} custom-call(bf16[3,10,26,16,128]{4,3,2,1,0:T(8,128)(2,1)S(1)} %shard_map.59.spread_ref, bf16[3456,256]{1,0:T(8,128)(2,1)S(1)} %bitcast.6, bf16[384,256]{1,0:T(8,128)(2,1)S(1)} %collective-permute-done.9.rest_0_), custom_call_target="tpu_custom_call" | custom-call | flops 1 | bytes 1 | tf_op jit(solution)/shard_map/pallas_call | solution.py:339
  34.0 1.9 %collective-permute-start.10 = (bf16[384,256]{1,0:T(8,128)(2,1)S(1)}, bf16[384,256]{1,0:T(8,128)(2,1)S(1)}, u32[]{:S(2)}, u32[]{:S(2)}) collective-permute-start(bf16[384,256]{1,0:T(8,128)(2,1)S(1)} %shard_map.64), channel_id=1, source_target_pairs={{0,12},{4,8},{8,4},{12,0},{1,13},{5,9},{9,5},{13,1},{2,14},{6,10},... | collective-permute-start | bytes 589832 | tf_op jit(solution)/shard_map/ppermute | solution.py:369
  35.9 4.2 %collective-permute-done.7.rest_0_ = bf16[384,256]{1,0:T(8,128)(2,1)S(1)} collective-permute-done((bf16[384,256]{1,0:T(8,128)(2,1)S(1)}, bf16[384,256]{1,0:T(8,128)(2,1)S(1)}, u32[]{:S(2)}, u32[]{:S(2)}) %collective-permute-start.7) | collective-permute-done | bytes 196640 | tf_op jit(solution)/shard_map/ppermute | solution.py:369
  40.1 1.6 %shard_map.62.home_ref = f32[768,256]{1,0:T(8,128)S(1)} custom-call(bf16[3,10,26,16,128]{4,3,2,1,0:T(8,128)(2,1)S(1)} %shard_map.59.spread_ref, bf16[3456,256]{1,0:T(8,128)(2,1)S(1)} %bitcast.7, bf16[384,256]{1,0:T(8,128)(2,1)S(1)} %collective-permute-done.7.rest_0_, bf16[1,256]{1,0:T(2,128)(2,1)S(1)} %reshape.22.rest_1_), custom_call_target="tpu_custom_call" | custom-call | flops 34359738368 | bytes 1 | tf_op jit(solution)/shard_map/pallas_call | solution.py:339
  41.7 8.9 %collective-permute-done.10.rest_0_ = bf16[384,256]{1,0:T(8,128)(2,1)S(1)} collective-permute-done((bf16[384,256]{1,0:T(8,128)(2,1)S(1)}, bf16[384,256]{1,0:T(8,128)(2,1)S(1)}, u32[]{:S(2)}, u32[]{:S(2)}) %collective-permute-start.10) | collective-permute-done | bytes 196640 | tf_op jit(solution)/shard_map/ppermute | solution.py:369
  50.6 0.8 %shard_map.65 = bf16[768,256]{1,0:T(8,128)(2,1)} custom-call(f32[768,256]{1,0:T(8,128)S(1)} %shard_map.62.home_ref, bf16[768,256]{1,0:T(8,128)(2,1)S(1)} %collective-permute-done.8.beside_ref, bf16[384,256]{1,0:T(8,128)(2,1)S(1)} %collective-permute-done.10.rest_0_), custom_call_target="tpu_custom_call" | custom-call | tf_op jit(solution)/shard_map/pallas_call | solution.py:379
  (10 shorter events, 0.1 us)
Async XLA Ops:
  0.0 20.9 %copy-start = (bf16[27,128,256]{2,1,0:T(8,128)(2,1)S(1)}, bf16[27,128,256]{2,1,0:T(8,128)(2,1)}, u32[]{:S(2)}) copy-start(bf16[27,128,256]{2,1,0:T(8,128)(2,1)} %param.8) | copy-start | bytes 5308420
  0.0 1.1 %copy-start.1 = (bf16[2,24,16,256]{3,2,1,0:T(8,128)(2,1)S(1)}, bf16[2,24,16,256]{3,2,1,0:T(8,128)(2,1)}, u32[]{:S(2)}) copy-start(bf16[2,24,16,256]{3,2,1,0:T(8,128)(2,1)} %param.5) | copy-start | bytes 1179652
  1.4 16.1 %collective-permute-start.2 = (bf16[784,128]{1,0:T(8,128)(2,1)S(1)}, bf16[784,128]{1,0:T(8,128)(2,1)S(1)}, u32[]{:S(2)}, u32[]{:S(2)}) collective-permute-start(bf16[784,128]{1,0:T(8,128)(2,1)S(1)} %get-tuple-element.12.same_ref), channel_id=1, source_target_pairs={{0,1},{1,9},{4,5},{5,13},{9,8},{8,0},{13,12},{12,4},{2,3},{3,11},{... | collective-permute-start | bytes 602120 | tf_op jit(solution)/shard_map/ppermute | solution.py:311
  1.9 15.7 %collective-permute-start = (bf16[784,128]{1,0:T(8,128)(2,1)S(1)}, bf16[784,128]{1,0:T(8,128)(2,1)S(1)}, u32[]{:S(2)}, u32[]{:S(2)}) collective-permute-start(bf16[784,128]{1,0:T(8,128)(2,1)S(1)} %get-tuple-element.13), channel_id=1, source_target_pairs={{0,4},{1,12},{4,0},{5,8},{9,13},{8,5},{13,9},{12,1},{2,6},{3,14},{... | collective-permute-start | bytes 602120 | tf_op jit(solution)/shard_map/ppermute | solution.py:312
  6.1 11.4 %collective-permute-start.3 = (bf16[64,128]{1,0:T(8,128)(2,1)S(1)}, bf16[64,128]{1,0:T(8,128)(2,1)S(1)}, u32[]{:S(2)}, u32[]{:S(2)}) collective-permute-start(bf16[64,128]{1,0:T(8,128)(2,1)S(1)} %get-tuple-element.15), channel_id=1, source_target_pairs={{0,3},{2,1},{1,11},{3,9},{4,7},{6,5},{5,15},{7,13},{9,10},{11,8},{... | collective-permute-start | bytes 49160 | tf_op jit(solution)/shard_map/ppermute | solution.py:313
  9.6 7.9 %collective-permute-start.1 = (bf16[64,128]{1,0:T(8,128)(2,1)S(1)}, bf16[64,128]{1,0:T(8,128)(2,1)S(1)}, u32[]{:S(2)}, u32[]{:S(2)}) collective-permute-start(bf16[64,128]{1,0:T(8,128)(2,1)S(1)} %get-tuple-element.14), channel_id=1, source_target_pairs={{0,6},{2,4},{1,14},{3,12},{4,2},{6,0},{5,10},{7,8},{9,15},{11,13},... | collective-permute-start | bytes 49160 | tf_op jit(solution)/shard_map/ppermute | solution.py:314
  17.5 1.5 %collective-permute-start.5 = (bf16[848,128]{1,0:T(8,128)(2,1)S(1)}, bf16[848,128]{1,0:T(8,128)(2,1)S(1)}, u32[]{:S(2)}, u32[]{:S(2)}) collective-permute-start(bf16[848,128]{1,0:T(8,128)(2,1)S(1)} %shard_map.58), channel_id=1, source_target_pairs={{0,1},{1,0},{2,3},{3,2},{4,5},{5,4},{6,7},{7,6},{8,9},{9,8},{10,11... | collective-permute-start | bytes 651272 | tf_op jit(solution)/shard_map/ppermute | solution.py:323
  17.6 1.7 %collective-permute-start.4 = (bf16[848,128]{1,0:T(8,128)(2,1)S(1)}, bf16[848,128]{1,0:T(8,128)(2,1)S(1)}, u32[]{:S(2)}, u32[]{:S(2)}) collective-permute-start(bf16[848,128]{1,0:T(8,128)(2,1)S(1)} %shard_map.57), channel_id=1, source_target_pairs={{0,1},{1,0},{2,3},{3,2},{4,5},{5,4},{6,7},{7,6},{8,9},{9,8},{10,11... | collective-permute-start | bytes 651272 | tf_op jit(solution)/shard_map/ppermute | solution.py:324
  21.8 7.8 %collective-permute-start.6 = (bf16[384,256]{1,0:T(8,128)(2,1)S(1)}, bf16[384,256]{1,0:T(8,128)(2,1)S(1)}, u32[]{:S(2)}, u32[]{:S(2)}) collective-permute-start(bf16[384,256]{1,0:T(8,128)(2,1)S(1)} %shard_map.60), channel_id=1, source_target_pairs={{0,4},{4,0},{8,12},{12,8},{1,5},{5,1},{9,13},{13,9},{2,6},{6,2},{1... | collective-permute-start | bytes 589832 | tf_op jit(solution)/shard_map/ppermute | solution.py:367
  24.1 8.3 %copy-start.2 = (bf16[256]{0:T(256)(128)(2,1)S(1)}, bf16[256]{0:T(256)(128)(2,1)}, u32[]{:S(2)}) copy-start(bf16[256]{0:T(256)(128)(2,1)} %param.9) | copy-start | bytes 1540
  24.1 9.0 %collective-permute-start.9 = (bf16[384,256]{1,0:T(8,128)(2,1)S(1)}, bf16[384,256]{1,0:T(8,128)(2,1)S(1)}, u32[]{:S(2)}, u32[]{:S(2)}) collective-permute-start(bf16[384,256]{1,0:T(8,128)(2,1)S(1)} %get-tuple-element.18), channel_id=1, source_target_pairs={{0,4},{4,0},{8,12},{12,8},{1,5},{5,1},{9,13},{13,9},{2,6},{6,2},{1... | collective-permute-start | bytes 589832 | tf_op jit(solution)/shard_map/ppermute | solution.py:367
  30.4 9.7 %collective-permute-start.7 = (bf16[384,256]{1,0:T(8,128)(2,1)S(1)}, bf16[384,256]{1,0:T(8,128)(2,1)S(1)}, u32[]{:S(2)}, u32[]{:S(2)}) collective-permute-start(bf16[384,256]{1,0:T(8,128)(2,1)S(1)} %shard_map.61), channel_id=1, source_target_pairs={{0,12},{4,8},{8,4},{12,0},{1,13},{5,9},{9,5},{13,1},{2,14},{6,10},... | collective-permute-start | bytes 589832 | tf_op jit(solution)/shard_map/ppermute | solution.py:369
  32.4 18.2 %collective-permute-start.8 = (bf16[768,256]{1,0:T(8,128)(2,1)S(1)}, bf16[768,256]{1,0:T(8,128)(2,1)S(1)}, u32[]{:S(2)}, u32[]{:S(2)}) collective-permute-start(bf16[768,256]{1,0:T(8,128)(2,1)S(1)} %get-tuple-element.17), channel_id=1, source_target_pairs={{0,4},{4,0},{8,12},{12,8},{1,5},{5,1},{9,13},{13,9},{2,6},{6,2},{1... | collective-permute-start | bytes 1179656 | tf_op jit(solution)/shard_map/ppermute | solution.py:370
  34.0 16.6 %collective-permute-start.10 = (bf16[384,256]{1,0:T(8,128)(2,1)S(1)}, bf16[384,256]{1,0:T(8,128)(2,1)S(1)}, u32[]{:S(2)}, u32[]{:S(2)}) collective-permute-start(bf16[384,256]{1,0:T(8,128)(2,1)S(1)} %shard_map.64), channel_id=1, source_target_pairs={{0,12},{4,8},{8,4},{12,0},{1,13},{5,9},{9,5},{13,1},{2,14},{6,10},... | collective-permute-start | bytes 589832 | tf_op jit(solution)/shard_map/ppermute | solution.py:369

commit v5 on v4

--- a/solution.py
+++ b/solution.py
@@ -154,10 +154,12 @@
     by_parity(fill)
 
 
-def join_kernel(first_ref, second_ref, out_ref):
-    split = first_ref.shape[0]
-    out_ref[:split] = first_ref[...]
-    out_ref[split:] = second_ref[...]
+def join_kernel(*refs):
+    out_ref = refs[-1]
+    at = 0
+    for ref in refs[:-1]:
+        out_ref[at : at + ref.shape[0]] = ref[...]
+        at += ref.shape[0]
 
 
 def group_total(row, group_ch):
@@ -172,7 +174,8 @@
 
 
 def spread_kernel(
-    same_ref, a_ref, edge_a_ref, b_ref, edge_b_ref, c_ref, d_ref, out_ref, own_ref, *, frames, rows, cols, entries
+    same_ref, a_ref, edge_a_ref, b_ref, edge_b_ref, swapped_ref, out_ref, own_ref,
+    *, frames, rows, cols, entries, first,
 ):
     s = lax.axis_index("tm")
     home = lax.axis_index("chan") == s // 2
@@ -180,6 +183,7 @@
     cells = frames * rows * cols
     edges = frames * rows
     split = cells + STAT_ROWS
+    height = split + edges + STAT_ROWS
 
     @pl.when(home)
     def _():
@@ -187,14 +191,14 @@
 
     @pl.when(jnp.logical_not(home))
     def _():
-        own_ref[...] = d_ref[:split]
+        own_ref[...] = swapped_ref[height : height + split]
 
     near, mid, far = near_of(s), mid_of(s), far_of(s)
     pieces = (
-        (own_ref, d_ref, split, jnp.where(home, s, mid)),
+        (own_ref, swapped_ref, height + split, jnp.where(home, s, mid)),
         (a_ref, edge_a_ref, 0, jnp.where(home, near, far)),
         (b_ref, edge_b_ref, 0, jnp.where(home, mid, s)),
-        (c_ref, c_ref, split, jnp.where(home, far, near)),
+        (swapped_ref, swapped_ref, split, jnp.where(home, far, near)),
     )
     stats = jnp.zeros((STAT_ROWS, LANES), jnp.float32)
     for ref, edge_ref, skip, _ in pieces:
@@ -215,11 +219,16 @@
         for f in range(n_all):
             out_ref[d, f, 0] = zero_row
             out_ref[d, f, rows + 1] = zero_row
-        for f in range(2):
-            out_ref[d, f, 1 : rows + 1] = jnp.zeros((rows, cols, LANES), jnp.bfloat16)
+
+    def clear():
+        for d in range(3):
+            for f in range(2):
+                out_ref[d, f, 1 : rows + 1] = jnp.zeros((rows, cols, LANES), jnp.bfloat16)
+
     col = lax.broadcasted_iota(jnp.int32, (rows, cols, LANES), 1)
     span = rows * cols
-    for ref, edge_ref, skip, block in pieces:
+
+    def place(ref, edge_ref, skip, start):
         for f in range(frames):
             value = normed(ref[f * span : (f + 1) * span])
             edge = normed(edge_ref[skip + f * rows : skip + (f + 1) * rows])
@@ -228,10 +237,21 @@
             left = jnp.where(col == 0, jnp.where(tile == 1, edge, 0.0), left)
             right = pltpu.roll(value, span - 1, 0).reshape(rows, cols, LANES)
             right = jnp.where(col == cols - 1, jnp.where(tile == 0, edge, 0.0), right)
-            at = 2 + block * frames + f
+            at = start + f
             out_ref[0, at, 1 : rows + 1] = left.astype(jnp.bfloat16)
             out_ref[1, at, 1 : rows + 1] = value.reshape(rows, cols, LANES).astype(jnp.bfloat16)
             out_ref[2, at, 1 : rows + 1] = right.astype(jnp.bfloat16)
+
+    if first:
+        pl.when(mid == 0)(clear)
+        for ref, edge_ref, skip, block in pieces:
+            wanted = jnp.logical_or(block == mid, block == mid - 1)
+            start = (block - mid + 1) * frames
+            pl.when(wanted)(functools.partial(place, ref, edge_ref, skip, start))
+    else:
+        clear()
+        for ref, edge_ref, skip, block in pieces:
+            place(ref, edge_ref, skip, 2 + block * frames)
 
 
 def partial_kernel(spread_ref, weight_ref, *rest, jobs, n_adds, n_outs, frames, rows, cols, with_bias):
@@ -250,20 +270,22 @@
             axis=1,
         )
         total = jnp.dot(stacked, weight_ref[...], preferred_element_type=jnp.float32)
-        if added is not None:
-            total = total + rest[added][...].astype(jnp.float32)
+        for ref, core in added:
+            more = rest[ref][...].astype(jnp.float32)
+            total = total + (more if core is None else jnp.where(lax.axis_index("chan") == core, more, 0.0))
         if with_bias:
             total = total + rest[n_adds][...].astype(jnp.float32)
         outs[out][place * span : (place + 1) * span] = total.astype(outs[out].dtype)
 
 
-def finish_kernel(home_ref, beside_ref, *rest, span):
-    out_ref = rest[-1]
-    total = home_ref[...] + beside_ref[...].astype(jnp.float32)
-    out_ref[:span] = total[:span].astype(out_ref.dtype)
-    for k, ref in enumerate(rest[:-1]):
-        here = slice((k + 1) * span, (k + 2) * span)
-        out_ref[here] = (total[here] + ref[...].astype(jnp.float32)).astype(out_ref.dtype)
+def finish_kernel(*refs):
+    last_ref, out_ref = refs[-2:]
+    span = last_ref.shape[0]
+    for k, ref in enumerate(refs[:-2]):
+        total = ref[...]
+        if k == len(refs) - 3:
+            total = total + last_ref[...].astype(jnp.float32)
+        out_ref[k * span : (k + 1) * span] = total.astype(out_ref.dtype)
 
 
 def params():
@@ -308,34 +330,40 @@
             for x in range(2):
                 edge_route.append((4 * s + 2 * x + core, 4 * there + 2 * (1 - x) + core_there))
     swap = [(0, 1), (1, 0)]
-    got_b = lax.ppermute(same, ("tm", "chan"), route_b)
-    got_a = lax.ppermute(following, ("tm", "chan"), route_a)
+    both = ("tm", "chan")
+    got_b = lax.ppermute(same, both, route_b)
+    got_a = lax.ppermute(following, both, route_a)
     got_edge_b = lax.ppermute(edge_same, ("tm", "tile", "chan"), edge_b)
     got_edge_a = lax.ppermute(edge_following, ("tm", "tile", "chan"), edge_a)
 
-    def joined(first, second):
+    received = (got_a, got_edge_a, got_b, got_edge_b)
+    joined = pl.pallas_call(
+        join_kernel,
+        out_shape=table(sum(part.shape[0] for part in received)),
+        compiler_params=params(),
+    )(*received)
+    swapped = lax.ppermute(joined, "chan", swap)
+
+    def spread_out(n_frames, first, after=None):
+        head = same if after is None else lax.optimization_barrier((same, after))[0]
         return pl.pallas_call(
-            join_kernel,
-            out_shape=table(first.shape[0] + second.shape[0]),
+            functools.partial(
+                spread_kernel, frames=frames, rows=rows, cols=cols, entries=entries, first=first
+            ),
+            out_shape=jax.ShapeDtypeStruct((3, n_frames, rows + 2, cols, LANES), jnp.bfloat16),
+            scratch_shapes=[pltpu.VMEM(same.shape, jnp.bfloat16)],
             compiler_params=params(),
-        )(first, second)
-
-    got_d = lax.ppermute(joined(got_b, got_edge_b), "chan", swap)
-    got_c = lax.ppermute(joined(got_a, got_edge_a), "chan", swap)
-    spread = pl.pallas_call(
-        functools.partial(spread_kernel, frames=frames, rows=rows, cols=cols, entries=entries),
-        out_shape=jax.ShapeDtypeStruct((3, n_blocks * frames + 2, rows + 2, cols, LANES), jnp.bfloat16),
-        scratch_shapes=[pltpu.VMEM(same.shape, jnp.bfloat16)],
-        compiler_params=params(),
-    )(same, got_a, got_edge_a, got_b, got_edge_b, got_c, got_d)
+        )(head, *received, swapped)
+
+    narrow = spread_out(2 + frames, True)
 
     weight = conv_weight.reshape(27 * LANES, outs)
     bias = conv_bias.reshape(1, outs)
 
     every = tuple(range(frames))
 
-    def partial_sums(jobs, spans, adds=(), with_bias=False, dtype=jnp.bfloat16, after=None, cost=1):
-        source = spread if after is None else lax.optimization_barrier((spread, after))[0]
+    def partial_sums(acts, jobs, spans, adds=(), with_bias=False, dtype=jnp.bfloat16, after=None, cost=1):
+        source = acts if after is None else lax.optimization_barrier((acts, after))[0]
         return pl.pallas_call(
             functools.partial(
                 partial_kernel,
@@ -355,32 +383,39 @@
     def beyond_of(s):
         return far_of(near_of(s))
 
+    def mixed(core):
+        return lambda s: jnp.where(lax.axis_index("chan") == core, far_of(s), near_of(s))
+
     near_route = [(s, near_of(s)) for s in range(n_blocks)]
-    far_route = [(s, far_of(s)) for s in range(n_blocks)]
-    parts = []
+    mixed_route = [
+        [
+            (2 * s + c, 2 * (far_of(s) if c == core else near_of(s)) + c)
+            for s in range(n_blocks)
+            for c in range(2)
+        ]
+        for core in range(2)
+    ]
+    parts = partial_sums(narrow, [(lambda s: 0, 0, 0, 0, ())], [1], cost=1 << 32)
+    spread = spread_out(2 + n_blocks * frames, False, parts[0])
+    for f in every[1:]:
+        parts += partial_sums(spread, [(beyond_of, f, 0, 0, ())], [1], after=parts, cost=1 << 32)
+    beyond = [lax.ppermute(part, "tm", near_route) for part in parts]
+    arrived, sums = [], None
     for f in every:
-        jobs, spans = [(beyond_of, f, 0, 0, None)], [1]
-        if f == frames - 1:
-            jobs += [(near_of, g, 1, g, None) for g in every]
-            spans += [frames]
-        parts.append(partial_sums(jobs, spans, after=parts[-1] if parts else None, cost=1 << 32))
-    beyond = [lax.ppermute(part[0], "tm", near_route) for part in parts]
-    sums = [partial_sums([(far_of, f, 0, 0, 0)], [1], (beyond[f],))[0] for f in every]
-    arrived = [lax.ppermute(part, "tm", far_route) for part in sums]
-    beside = lax.ppermute(parts[-1][1], "tm", near_route)
-    home = partial_sums(
-        [(lambda s: s, f, 0, f, None if f else 0) for f in every],
-        [frames],
-        arrived[:1],
-        True,
-        jnp.float32,
-        cost=1 << 35,
-    )[0]
+        jobs = [(mixed(core), f, core, 0, ((0, core),)) for core in range(2)]
+        sums = partial_sums(spread, jobs, [1, 1], (beyond[f],), after=sums)
+        arrived += [lax.ppermute(part, both, route) for part, route in zip(sums, mixed_route)]
+    home = []
+    for f in every:
+        adds = arrived[2 * f : 2 * f + 2] if f < frames - 1 else arrived[2 * f : 2 * f + 1]
+        jobs = [(lambda s: s, f, 0, 0, tuple((k, None) for k in range(len(adds))))]
+        after = home or None
+        home += partial_sums(spread, jobs, [1], adds, True, jnp.float32, after=after, cost=1 << 35)
     result = pl.pallas_call(
-        functools.partial(finish_kernel, span=rows * cols),
+        finish_kernel,
         out_shape=jax.ShapeDtypeStruct((cells, outs), jnp.bfloat16),
         compiler_params=params(),
-    )(home, beside, *arrived[1:])
+    )(*home, arrived[-1])
     return result.reshape(frames, rows, cols, outs)
 
 

time: 51.6 us -> 50.7 us (0.983)
  waiting for transfers between devices: 26.2 us -> 22.7 us
  starting transfers between devices: 13.4 us -> 15 us
  Pallas kernels: 9.37 us -> 10.4 us
    ppermute x1, waiting for transfers between devices: 7.81 us -> 5.69 us  [split_body(): got_edge_b = lax.ppermute(edge_same, ('tm', 'tile', 'chan'), edge_b)]
    ppermute x9, waiting for transfers between devices: 18.4 us -> 16.3 us  [the longest x4 10.8 us: split_body(): lax.ppermute(part, both, route)]
    ppermute x1, starting transfers between devices: 0.01 us -> 1.44 us  [split_body(): got_edge_a = lax.ppermute(edge_following, ('tm', 'tile', 'chan'), edge_a)]
    pallas_call x4, Pallas kernels: 2.42 us -> 3.27 us  [the longest x2 2.42 us: spread_out(): pl.pallas_call(functools.partial(spread_kernel, frames=frames, rows=rows,...]
    ppermute x1, waiting for transfers between devices: 0.01 us -> 0.68 us  [split_body(): got_edge_a = lax.ppermute(edge_following, ('tm', 'tile', 'chan'), edge_a)]
    pallas_call x5 -> x6, Pallas kernels: 6.49 us -> 6.68 us  [partial_sums(): pl.pallas_call(functools.partial(partial_kernel, jobs=jobs, n_adds=len(ad...]
  transfers between devices with their start and end apart: 11 -> 11, of which waited for: 7 -> 9; matrix products, arithmetic and copies ran while one was open for 3% -> 3% of each run, Pallas kernels for 11% -> 15%
where the time goes in v5:
time: 50.7 us; the launch traced here: 50.6 us
  waiting for transfers between devices  22.7 us (45%)
  starting transfers between devices  15 us (30%)
  Pallas kernels  10.4 us (21%)
  local copies, waits for them, and re-layouts  2.33 us (5%)
    ppermute x4, waiting for transfers between devices, split_body(): lax.ppermute(part, both, route)  10.8 us
    pallas_call x6, Pallas kernels, partial_sums(): pl.pallas_call(functools.partial(partial_kernel, jobs=jobs, n_adds=len(ad...  6.68 us
    ppermute x1, waiting for transfers between devices, split_body(): got_edge_b = lax.ppermute(edge_same, ('tm', 'tile', 'chan'), edge_b)  5.69 us
    ppermute x4, starting transfers between devices, split_body(): lax.ppermute(part, both, route)  4.48 us
    ppermute x2, waiting for transfers between devices, split_body(): beyond = [lax.ppermute(part, 'tm', near_route) for part in parts]  3.81 us
    ppermute x1, starting transfers between devices, split_body(): got_edge_b = lax.ppermute(edge_same, ('tm', 'tile', 'chan'), edge_b)  3.73 us
    ppermute x1, starting transfers between devices, split_body(): got_a = lax.ppermute(following, both, route_a)  2.64 us
    pallas_call x2, Pallas kernels, spread_out(): pl.pallas_call(functools.partial(spread_kernel, frames=frames, rows=rows,...  2.42 us
  transfers between devices with their start and end apart: 11, of which 9 were waited for; matrix products, arithmetic and copies ran while one was open for 3% of the time, Pallas kernels for 15%

profile of v5, /device:TPU:0, one launch (start us, length us, event | category | flops | bytes accessed | tf_op | source)
XLA Modules:
  0.0 50.6 jit_solution(8921195820497421953)
XLA Ops:
  0.0 1.0 %copy-done.1 = bf16[2,24,16,256]{3,2,1,0:T(8,128)(2,1)S(1)} copy-done((bf16[2,24,16,256]{3,2,1,0:T(8,128)(2,1)S(1)}, bf16[2,24,16,256]{3,2,1,0:T(8,128)(2,1)}, u32[]{:S(2)}) %copy-start.1) | copy-done | bytes 393240
  1.0 0.2 shard_map.55
  1.2 0.5 %collective-permute-start.2 = (bf16[784,128]{1,0:T(8,128)(2,1)S(1)}, bf16[784,128]{1,0:T(8,128)(2,1)S(1)}, u32[]{:S(2)}, u32[]{:S(2)}) collective-permute-start(bf16[784,128]{1,0:T(8,128)(2,1)S(1)} %get-tuple-element.21.same_ref), channel_id=1, source_target_pairs={{0,1},{1,9},{4,5},{5,13},{9,8},{8,0},{13,12},{12,4},{2,3},{3,11},{... | collective-permute-start | bytes 602120 | tf_op jit(solution)/shard_map/ppermute | solution.py:334
  1.7 2.6 %collective-permute-start = (bf16[784,128]{1,0:T(8,128)(2,1)S(1)}, bf16[784,128]{1,0:T(8,128)(2,1)S(1)}, u32[]{:S(2)}, u32[]{:S(2)}) collective-permute-start(bf16[784,128]{1,0:T(8,128)(2,1)S(1)} %get-tuple-element.18), channel_id=1, source_target_pairs={{0,4},{1,12},{4,0},{5,8},{9,13},{8,5},{13,9},{12,1},{2,6},{3,14},{... | collective-permute-start | bytes 602120 | tf_op jit(solution)/shard_map/ppermute | solution.py:335
  4.4 0.7 %reshape.19.gain_ref = bf16[1,256]{1,0:T(2,128)(2,1)S(1)} reshape(bf16[256]{0:T(256)(128)(2,1)} %param.6) | data formatting | bytes 1024 | tf_op jit(solution)/shard_map/reshape | solution.py:317
  5.0 0.7 %reshape.20.bias_ref = bf16[1,256]{1,0:T(2,128)(2,1)S(1)} reshape(bf16[256]{0:T(256)(128)(2,1)} %param.7) | data formatting | bytes 1024 | tf_op jit(solution)/shard_map/reshape | solution.py:317
  5.7 0.2 shard_map.56
  5.9 1.4 %collective-permute-start.1 = (bf16[64,128]{1,0:T(8,128)(2,1)S(1)}, bf16[64,128]{1,0:T(8,128)(2,1)S(1)}, u32[]{:S(2)}, u32[]{:S(2)}) collective-permute-start(bf16[64,128]{1,0:T(8,128)(2,1)S(1)} %get-tuple-element.19), channel_id=1, source_target_pairs={{0,6},{2,4},{1,14},{3,12},{4,2},{6,0},{5,10},{7,8},{9,15},{11,13},... | collective-permute-start | bytes 49160 | tf_op jit(solution)/shard_map/ppermute | solution.py:337
  7.4 3.7 %collective-permute-start.3 = (bf16[64,128]{1,0:T(8,128)(2,1)S(1)}, bf16[64,128]{1,0:T(8,128)(2,1)S(1)}, u32[]{:S(2)}, u32[]{:S(2)}) collective-permute-start(bf16[64,128]{1,0:T(8,128)(2,1)S(1)} %get-tuple-element.20), channel_id=1, source_target_pairs={{0,3},{2,1},{1,11},{3,9},{4,7},{6,5},{5,15},{7,13},{9,10},{11,8},{... | collective-permute-start | bytes 49160 | tf_op jit(solution)/shard_map/ppermute | solution.py:336
  11.1 0.7 %collective-permute-done.1.refs_1_.edge_a_ref = bf16[64,128]{1,0:T(8,128)(2,1)S(1)} collective-permute-done((bf16[64,128]{1,0:T(8,128)(2,1)S(1)}, bf16[64,128]{1,0:T(8,128)(2,1)S(1)}, u32[]{:S(2)}, u32[]{:S(2)}) %collective-permute-start.1) | collective-permute-done | bytes 16416 | tf_op jit(solution)/shard_map/ppermute | solution.py:337
  11.8 5.7 %collective-permute-done.3.refs_3_.edge_b_ref = bf16[64,128]{1,0:T(8,128)(2,1)S(1)} collective-permute-done((bf16[64,128]{1,0:T(8,128)(2,1)S(1)}, bf16[64,128]{1,0:T(8,128)(2,1)S(1)}, u32[]{:S(2)}, u32[]{:S(2)}) %collective-permute-start.3) | collective-permute-done | bytes 16416 | tf_op jit(solution)/shard_map/ppermute | solution.py:336
  17.5 0.1 collective-permute-start.4
  17.6 1.8 %collective-permute-done.4.swapped_ref = bf16[1696,128]{1,0:T(8,128)(2,1)S(1)} collective-permute-done((bf16[1696,128]{1,0:T(8,128)(2,1)S(1)}, bf16[1696,128]{1,0:T(8,128)(2,1)S(1)}, u32[]{:S(2)}, u32[]{:S(2)}) %collective-permute-start.4) | collective-permute-done | bytes 434208 | tf_op jit(solution)/shard_map/ppermute | solution.py:345
  19.4 0.9 %shard_map.58.spread_ref = bf16[3,4,26,16,128]{4,3,2,1,0:T(8,128)(2,1)S(1)} custom-call(bf16[784,128]{1,0:T(8,128)(2,1)S(1)} %get-tuple-element.21.same_ref, bf16[784,128]{1,0:T(8,128)(2,1)S(1)} %collective-permute-done.refs_0_.a_ref, bf16[64,128]{1,0:T(8,128)(2,1)S(1)} %collective-permute-done.1.refs_1_.edge_a_ref, ...), custom_call_target="tpu_custom_call" | custom-call | tf_op jit(solution)/shard_map/pallas_call | solution.py:349
  20.2 0.9 %shard_map.59 = bf16[384,256]{1,0:T(8,128)(2,1)S(1)} custom-call(bf16[3,4,26,16,128]{4,3,2,1,0:T(8,128)(2,1)S(1)} %shard_map.58.spread_ref, bf16[3456,256]{1,0:T(8,128)(2,1)S(1)} %bitcast.3), custom_call_target="tpu_custom_call" | custom-call | flops 4294967296 | bytes 1 | tf_op jit(solution)/shard_map/pallas_call | solution.py:367
  21.2 1.6 %shard_map.60.spread_ref = bf16[3,10,26,16,128]{4,3,2,1,0:T(8,128)(2,1)S(1)} custom-call(bf16[784,128]{1,0:T(8,128)(2,1)S(1)} %get-tuple-element.21.same_ref, bf16[784,128]{1,0:T(8,128)(2,1)S(1)} %collective-permute-done.refs_0_.a_ref, bf16[64,128]{1,0:T(8,128)(2,1)S(1)} %collective-permute-done.1.refs_1_.edge_a_ref, ...), custom_call_target="tpu_custom_call" | custom-call | tf_op jit(solution)/shard_map/pallas_call | solution.py:349
  22.8 0.9 %shard_map.63 = bf16[384,256]{1,0:T(8,128)(2,1)S(1)} custom-call(bf16[3,10,26,16,128]{4,3,2,1,0:T(8,128)(2,1)S(1)} %shard_map.60.spread_ref, bf16[3456,256]{1,0:T(8,128)(2,1)S(1)} %bitcast.4), custom_call_target="tpu_custom_call" | custom-call | flops 4294967296 | bytes 1 | tf_op jit(solution)/shard_map/pallas_call | solution.py:367
  23.7 2.1 %collective-permute-start.8 = (bf16[384,256]{1,0:T(8,128)(2,1)S(1)}, bf16[384,256]{1,0:T(8,128)(2,1)S(1)}, u32[]{:S(2)}, u32[]{:S(2)}) collective-permute-start(bf16[384,256]{1,0:T(8,128)(2,1)S(1)} %shard_map.63), channel_id=1, source_target_pairs={{0,4},{4,0},{8,12},{12,8},{1,5},{5,1},{9,13},{13,9},{2,6},{6,2},{1... | collective-permute-start | bytes 589832 | tf_op jit(solution)/shard_map/ppermute | solution.py:402
  25.7 3.2 %collective-permute-done.5.rest_0_ = bf16[384,256]{1,0:T(8,128)(2,1)S(1)} collective-permute-done((bf16[384,256]{1,0:T(8,128)(2,1)S(1)}, bf16[384,256]{1,0:T(8,128)(2,1)S(1)}, u32[]{:S(2)}, u32[]{:S(2)}) %collective-permute-start.5) | collective-permute-done | bytes 196640 | tf_op jit(solution)/shard_map/ppermute | solution.py:402
  28.9 1.6 %shard_map.61 = (bf16[384,256]{1,0:T(8,128)(2,1)S(1)}, bf16[384,256]{1,0:T(8,128)(2,1)S(1)}) custom-call(bf16[3,10,26,16,128]{4,3,2,1,0:T(8,128)(2,1)S(1)} %shard_map.60.spread_ref, bf16[3456,256]{1,0:T(8,128)(2,1)S(1)} %bitcast.5, bf16[384,256]{1,0:T(8,128)(2,1)S(1)} %collective-permute-done.5.rest_0_), custom_call_target="tpu_custom_call" | custom-call | flops 1 | bytes 1 | tf_op jit(solution)/shard_map/pallas_call | solution.py:367
  30.5 1.8 %collective-permute-start.6 = (bf16[384,256]{1,0:T(8,128)(2,1)S(1)}, bf16[384,256]{1,0:T(8,128)(2,1)S(1)}, u32[]{:S(2)}, u32[]{:S(2)}) collective-permute-start(bf16[384,256]{1,0:T(8,128)(2,1)S(1)} %get-tuple-element.22), channel_id=1, source_target_pairs={{0,12},{1,5},{4,8},{5,1},{8,4},{9,13},{12,0},{13,9},{2,14},{3,7},{... | collective-permute-start | bytes 589832 | tf_op jit(solution)/shard_map/ppermute | solution.py:407
  32.3 0.6 %collective-permute-done.8.rest_0_ = bf16[384,256]{1,0:T(8,128)(2,1)S(1)} collective-permute-done((bf16[384,256]{1,0:T(8,128)(2,1)S(1)}, bf16[384,256]{1,0:T(8,128)(2,1)S(1)}, u32[]{:S(2)}, u32[]{:S(2)}) %collective-permute-start.8) | collective-permute-done | bytes 196640 | tf_op jit(solution)/shard_map/ppermute | solution.py:402
  33.0 1.6 %shard_map.64 = (bf16[384,256]{1,0:T(8,128)(2,1)S(1)}, bf16[384,256]{1,0:T(8,128)(2,1)S(1)}) custom-call(bf16[3,10,26,16,128]{4,3,2,1,0:T(8,128)(2,1)S(1)} %shard_map.60.spread_ref, bf16[3456,256]{1,0:T(8,128)(2,1)S(1)} %bitcast.6, bf16[384,256]{1,0:T(8,128)(2,1)S(1)} %collective-permute-done.8.rest_0_), custom_call_target="tpu_custom_call" | custom-call | flops 1 | bytes 1 | tf_op jit(solution)/shard_map/pallas_call | solution.py:367
  34.5 1.8 %collective-permute-start.9 = (bf16[384,256]{1,0:T(8,128)(2,1)S(1)}, bf16[384,256]{1,0:T(8,128)(2,1)S(1)}, u32[]{:S(2)}, u32[]{:S(2)}) collective-permute-start(bf16[384,256]{1,0:T(8,128)(2,1)S(1)} %get-tuple-element.27), channel_id=1, source_target_pairs={{0,12},{1,5},{4,8},{5,1},{8,4},{9,13},{12,0},{13,9},{2,14},{3,7},{... | collective-permute-start | bytes 589832 | tf_op jit(solution)/shard_map/ppermute | solution.py:407
  36.3 0.9 %collective-permute-start.10 = (bf16[384,256]{1,0:T(8,128)(2,1)S(1)}, bf16[384,256]{1,0:T(8,128)(2,1)S(1)}, u32[]{:S(2)}, u32[]{:S(2)}) collective-permute-start(bf16[384,256]{1,0:T(8,128)(2,1)S(1)} %get-tuple-element.28), channel_id=1, source_target_pairs={{0,4},{1,13},{4,0},{5,9},{8,12},{9,5},{12,8},{13,1},{2,6},{3,15},{... | collective-permute-start | bytes 589832 | tf_op jit(solution)/shard_map/ppermute | solution.py:407
  37.2 3.0 %collective-permute-done.6.rest_0_ = bf16[384,256]{1,0:T(8,128)(2,1)S(1)} collective-permute-done((bf16[384,256]{1,0:T(8,128)(2,1)S(1)}, bf16[384,256]{1,0:T(8,128)(2,1)S(1)}, u32[]{:S(2)}, u32[]{:S(2)}) %collective-permute-start.6) | collective-permute-done | bytes 196640 | tf_op jit(solution)/shard_map/ppermute | solution.py:407
  40.2 4.3 %collective-permute-done.7.rest_1_ = bf16[384,256]{1,0:T(8,128)(2,1)S(1)} collective-permute-done((bf16[384,256]{1,0:T(8,128)(2,1)S(1)}, bf16[384,256]{1,0:T(8,128)(2,1)S(1)}, u32[]{:S(2)}, u32[]{:S(2)}) %collective-permute-start.7) | collective-permute-done | bytes 196640 | tf_op jit(solution)/shard_map/ppermute | solution.py:407
  44.5 0.9 %shard_map.62.refs_0_ = f32[384,256]{1,0:T(8,128)S(1)} custom-call(bf16[3,10,26,16,128]{4,3,2,1,0:T(8,128)(2,1)S(1)} %shard_map.60.spread_ref, bf16[3456,256]{1,0:T(8,128)(2,1)S(1)} %bitcast.7, bf16[384,256]{1,0:T(8,128)(2,1)S(1)} %collective-permute-done.6.rest_0_, bf16[384,256]{1,0:T(8,128)(2,1)S(1)} %collective-permute-done.7.rest_1_, ...), custom_call_target="tpu_custom_call" | custom-call | flops 34359738368 | bytes 1 | tf_op jit(solution)/shard_map/pallas_call | solution.py:367
  45.4 2.3 %collective-permute-done.9.rest_0_ = bf16[384,256]{1,0:T(8,128)(2,1)S(1)} collective-permute-done((bf16[384,256]{1,0:T(8,128)(2,1)S(1)}, bf16[384,256]{1,0:T(8,128)(2,1)S(1)}, u32[]{:S(2)}, u32[]{:S(2)}) %collective-permute-start.9) | collective-permute-done | bytes 196640 | tf_op jit(solution)/shard_map/ppermute | solution.py:407
  47.7 0.9 %shard_map.65.refs_1_ = f32[384,256]{1,0:T(8,128)S(1)} custom-call(bf16[3,10,26,16,128]{4,3,2,1,0:T(8,128)(2,1)S(1)} %shard_map.60.spread_ref, bf16[3456,256]{1,0:T(8,128)(2,1)S(1)} %bitcast.8, bf16[384,256]{1,0:T(8,128)(2,1)S(1)} %collective-permute-done.9.rest_0_, bf16[1,256]{1,0:T(2,128)(2,1)S(1)} %reshape.22.rest_2_.rest_1_), custom_call_target="tpu_custom_call" | custom-call | flops 34359738368 | bytes 1 | tf_op jit(solution)/shard_map/pallas_call | solution.py:367
  48.6 1.1 %collective-permute-done.10.refs_2_ = bf16[384,256]{1,0:T(8,128)(2,1)S(1)} collective-permute-done((bf16[384,256]{1,0:T(8,128)(2,1)S(1)}, bf16[384,256]{1,0:T(8,128)(2,1)S(1)}, u32[]{:S(2)}, u32[]{:S(2)}) %collective-permute-start.10) | collective-permute-done | bytes 196640 | tf_op jit(solution)/shard_map/ppermute | solution.py:407
  49.7 0.8 %shard_map.66 = bf16[768,256]{1,0:T(8,128)(2,1)} custom-call(f32[384,256]{1,0:T(8,128)S(1)} %shard_map.62.refs_0_, f32[384,256]{1,0:T(8,128)S(1)} %shard_map.65.refs_1_, bf16[384,256]{1,0:T(8,128)(2,1)S(1)} %collective-permute-done.10.refs_2_), custom_call_target="tpu_custom_call" | custom-call | tf_op jit(solution)/shard_map/pallas_call | solution.py:414
  (11 shorter events, 0.1 us)
Async XLA Ops:
  0.0 1.0 %copy-start.1 = (bf16[2,24,16,256]{3,2,1,0:T(8,128)(2,1)S(1)}, bf16[2,24,16,256]{3,2,1,0:T(8,128)(2,1)}, u32[]{:S(2)}) copy-start(bf16[2,24,16,256]{3,2,1,0:T(8,128)(2,1)} %param.5) | copy-start | bytes 1179652
  1.2 16.3 %collective-permute-start.2 = (bf16[784,128]{1,0:T(8,128)(2,1)S(1)}, bf16[784,128]{1,0:T(8,128)(2,1)S(1)}, u32[]{:S(2)}, u32[]{:S(2)}) collective-permute-start(bf16[784,128]{1,0:T(8,128)(2,1)S(1)} %get-tuple-element.21.same_ref), channel_id=1, source_target_pairs={{0,1},{1,9},{4,5},{5,13},{9,8},{8,0},{13,12},{12,4},{2,3},{3,11},{... | collective-permute-start | bytes 602120 | tf_op jit(solution)/shard_map/ppermute | solution.py:334
  1.7 15.7 %collective-permute-start = (bf16[784,128]{1,0:T(8,128)(2,1)S(1)}, bf16[784,128]{1,0:T(8,128)(2,1)S(1)}, u32[]{:S(2)}, u32[]{:S(2)}) collective-permute-start(bf16[784,128]{1,0:T(8,128)(2,1)S(1)} %get-tuple-element.18), channel_id=1, source_target_pairs={{0,4},{1,12},{4,0},{5,8},{9,13},{8,5},{13,9},{12,1},{2,6},{3,14},{... | collective-permute-start | bytes 602120 | tf_op jit(solution)/shard_map/ppermute | solution.py:335
  5.7 14.5 %copy-start = (bf16[27,128,256]{2,1,0:T(8,128)(2,1)S(1)}, bf16[27,128,256]{2,1,0:T(8,128)(2,1)}, u32[]{:S(2)}) copy-start(bf16[27,128,256]{2,1,0:T(8,128)(2,1)} %param.8) | copy-start | bytes 5308420
  5.9 5.8 %collective-permute-start.1 = (bf16[64,128]{1,0:T(8,128)(2,1)S(1)}, bf16[64,128]{1,0:T(8,128)(2,1)S(1)}, u32[]{:S(2)}, u32[]{:S(2)}) collective-permute-start(bf16[64,128]{1,0:T(8,128)(2,1)S(1)} %get-tuple-element.19), channel_id=1, source_target_pairs={{0,6},{2,4},{1,14},{3,12},{4,2},{6,0},{5,10},{7,8},{9,15},{11,13},... | collective-permute-start | bytes 49160 | tf_op jit(solution)/shard_map/ppermute | solution.py:337
  7.4 10.1 %collective-permute-start.3 = (bf16[64,128]{1,0:T(8,128)(2,1)S(1)}, bf16[64,128]{1,0:T(8,128)(2,1)S(1)}, u32[]{:S(2)}, u32[]{:S(2)}) collective-permute-start(bf16[64,128]{1,0:T(8,128)(2,1)S(1)} %get-tuple-element.20), channel_id=1, source_target_pairs={{0,3},{2,1},{1,11},{3,9},{4,7},{6,5},{5,15},{7,13},{9,10},{11,8},{... | collective-permute-start | bytes 49160 | tf_op jit(solution)/shard_map/ppermute | solution.py:336
  17.5 1.8 %collective-permute-start.4 = (bf16[1696,128]{1,0:T(8,128)(2,1)S(1)}, bf16[1696,128]{1,0:T(8,128)(2,1)S(1)}, u32[]{:S(2)}, u32[]{:S(2)}) collective-permute-start(bf16[1696,128]{1,0:T(8,128)(2,1)S(1)} %shard_map.57), channel_id=1, source_target_pairs={{0,1},{1,0},{2,3},{3,2},{4,5},{5,4},{6,7},{7,6},{8,9},{9,8},{10,11... | collective-permute-start | bytes 1302536 | tf_op jit(solution)/shard_map/ppermute | solution.py:345
  21.1 7.8 %collective-permute-start.5 = (bf16[384,256]{1,0:T(8,128)(2,1)S(1)}, bf16[384,256]{1,0:T(8,128)(2,1)S(1)}, u32[]{:S(2)}, u32[]{:S(2)}) collective-permute-start(bf16[384,256]{1,0:T(8,128)(2,1)S(1)} %shard_map.59), channel_id=1, source_target_pairs={{0,4},{4,0},{8,12},{12,8},{1,5},{5,1},{9,13},{13,9},{2,6},{6,2},{1... | collective-permute-start | bytes 589832 | tf_op jit(solution)/shard_map/ppermute | solution.py:402
  23.7 8.7 %copy-start.2 = (bf16[256]{0:T(256)(128)(2,1)S(1)}, bf16[256]{0:T(256)(128)(2,1)}, u32[]{:S(2)}) copy-start(bf16[256]{0:T(256)(128)(2,1)} %param.9) | copy-start | bytes 1540
  23.7 9.3 %collective-permute-start.8 = (bf16[384,256]{1,0:T(8,128)(2,1)S(1)}, bf16[384,256]{1,0:T(8,128)(2,1)S(1)}, u32[]{:S(2)}, u32[]{:S(2)}) collective-permute-start(bf16[384,256]{1,0:T(8,128)(2,1)S(1)} %shard_map.63), channel_id=1, source_target_pairs={{0,4},{4,0},{8,12},{12,8},{1,5},{5,1},{9,13},{13,9},{2,6},{6,2},{1... | collective-permute-start | bytes 589832 | tf_op jit(solution)/shard_map/ppermute | solution.py:402
  30.5 9.7 %collective-permute-start.6 = (bf16[384,256]{1,0:T(8,128)(2,1)S(1)}, bf16[384,256]{1,0:T(8,128)(2,1)S(1)}, u32[]{:S(2)}, u32[]{:S(2)}) collective-permute-start(bf16[384,256]{1,0:T(8,128)(2,1)S(1)} %get-tuple-element.22), channel_id=1, source_target_pairs={{0,12},{1,5},{4,8},{5,1},{8,4},{9,13},{12,0},{13,9},{2,14},{3,7},{... | collective-permute-start | bytes 589832 | tf_op jit(solution)/shard_map/ppermute | solution.py:407
  32.3 12.2 %collective-permute-start.7 = (bf16[384,256]{1,0:T(8,128)(2,1)S(1)}, bf16[384,256]{1,0:T(8,128)(2,1)S(1)}, u32[]{:S(2)}, u32[]{:S(2)}) collective-permute-start(bf16[384,256]{1,0:T(8,128)(2,1)S(1)} %get-tuple-element.23), channel_id=1, source_target_pairs={{0,4},{1,13},{4,0},{5,9},{8,12},{9,5},{12,8},{13,1},{2,6},{3,15},{... | collective-permute-start | bytes 589832 | tf_op jit(solution)/shard_map/ppermute | solution.py:407
  34.5 13.2 %collective-permute-start.9 = (bf16[384,256]{1,0:T(8,128)(2,1)S(1)}, bf16[384,256]{1,0:T(8,128)(2,1)S(1)}, u32[]{:S(2)}, u32[]{:S(2)}) collective-permute-start(bf16[384,256]{1,0:T(8,128)(2,1)S(1)} %get-tuple-element.27), channel_id=1, source_target_pairs={{0,12},{1,5},{4,8},{5,1},{8,4},{9,13},{12,0},{13,9},{2,14},{3,7},{... | collective-permute-start | bytes 589832 | tf_op jit(solution)/shard_map/ppermute | solution.py:407
  36.3 13.4 %collective-permute-start.10 = (bf16[384,256]{1,0:T(8,128)(2,1)S(1)}, bf16[384,256]{1,0:T(8,128)(2,1)S(1)}, u32[]{:S(2)}, u32[]{:S(2)}) collective-permute-start(bf16[384,256]{1,0:T(8,128)(2,1)S(1)} %get-tuple-element.28), channel_id=1, source_target_pairs={{0,4},{1,13},{4,0},{5,9},{8,12},{9,5},{12,8},{13,1},{2,6},{3,15},{... | collective-permute-start | bytes 589832 | tf_op jit(solution)/shard_map/ppermute | solution.py:407

commit v6 on v5

--- a/solution.py
+++ b/solution.py
@@ -243,10 +243,11 @@
             out_ref[2, at, 1 : rows + 1] = right.astype(jnp.bfloat16)
 
     if first:
-        pl.when(mid == 0)(clear)
+        target = jnp.where(lax.axis_index("chan") == 0, far, mid)
+        pl.when(target == 0)(clear)
         for ref, edge_ref, skip, block in pieces:
-            wanted = jnp.logical_or(block == mid, block == mid - 1)
-            start = (block - mid + 1) * frames
+            wanted = jnp.logical_or(block == target, block == target - 1)
+            start = (block - target + 1) * frames
             pl.when(wanted)(functools.partial(place, ref, edge_ref, skip, start))
     else:
         clear()
@@ -258,8 +259,8 @@
     outs = rest[len(rest) - n_outs :]
     s = lax.axis_index("tm")
     span = rows * cols
-    for block_of, f, out, place, added in jobs:
-        at = block_of(s) * frames + f
+    for frame_of, out, place, added in jobs:
+        at = frame_of(s)
         stacked = jnp.concatenate(
             [
                 spread_ref[d, at + a, b : b + rows].reshape(span, LANES)
@@ -278,14 +279,11 @@
         outs[out][place * span : (place + 1) * span] = total.astype(outs[out].dtype)
 
 
-def finish_kernel(*refs):
-    last_ref, out_ref = refs[-2:]
-    span = last_ref.shape[0]
-    for k, ref in enumerate(refs[:-2]):
-        total = ref[...]
-        if k == len(refs) - 3:
-            total = total + last_ref[...].astype(jnp.float32)
-        out_ref[k * span : (k + 1) * span] = total.astype(out_ref.dtype)
+def finish_kernel(first_ref, second_ref, one_ref, other_ref, out_ref):
+    span = first_ref.shape[0]
+    out_ref[:span] = first_ref[...].astype(out_ref.dtype)
+    total = second_ref[...] + one_ref[...].astype(jnp.float32) + other_ref[...].astype(jnp.float32)
+    out_ref[span:] = total.astype(out_ref.dtype)
 
 
 def params():
@@ -294,6 +292,8 @@
 
 def split_body(latent, gn_gain, gn_bias, conv_weight, conv_bias):
     frames, rows, cols, chans = latent.shape
+    if frames != 2:
+        return body(latent, gn_gain, gn_bias, conv_weight, conv_bias)
     outs = conv_weight.shape[2]
     cells = frames * rows * cols
     edges = frames * rows
@@ -360,8 +360,6 @@
     weight = conv_weight.reshape(27 * LANES, outs)
     bias = conv_bias.reshape(1, outs)
 
-    every = tuple(range(frames))
-
     def partial_sums(acts, jobs, spans, adds=(), with_bias=False, dtype=jnp.bfloat16, after=None, cost=1):
         source = acts if after is None else lax.optimization_barrier((acts, after))[0]
         return pl.pallas_call(
@@ -380,42 +378,49 @@
             cost_estimate=pl.CostEstimate(flops=cost, transcendentals=0, bytes_accessed=1),
         )(source, weight, *adds, *([bias] if with_bias else []))
 
-    def beyond_of(s):
-        return far_of(near_of(s))
-
-    def mixed(core):
-        return lambda s: jnp.where(lax.axis_index("chan") == core, far_of(s), near_of(s))
-
-    near_route = [(s, near_of(s)) for s in range(n_blocks)]
-    mixed_route = [
-        [
-            (2 * s + c, 2 * (far_of(s) if c == core else near_of(s)) + c)
+    def mixed(core, ours, theirs):
+        return lambda s: jnp.where(lax.axis_index("chan") == core, ours(s), theirs(s))
+
+    def frame(block_of, f):
+        return lambda s: block_of(s) * frames + f
+
+    def route(core, goal):
+        return [
+            (2 * s + c, 2 * (goal(s) if c == core else near_of(s)) + c)
             for s in range(n_blocks)
             for c in range(2)
         ]
-        for core in range(2)
+
+    lead = partial_sums(narrow, [(mixed(0, lambda s: 0, lambda s: 1), 0, 0, ())], [1], cost=1 << 32)
+    spread = spread_out(2 + n_blocks * frames, False, lead[0])
+    second = mixed(1, frame(far_of, 0), frame(mid_of, 1))
+    second = partial_sums(spread, [(second, 0, 0, ())], [1], after=lead, cost=1 << 32)
+    jobs = [(mixed(core, frame(mid_of, 0), frame(near_of, 0)), core, 0, ()) for core in range(2)]
+    straight = partial_sums(spread, jobs, [1, 1], after=second, cost=1 << 32)
+    got_1 = lax.ppermute(lead[0], both, route(0, far_of))
+    got_2 = lax.ppermute(second[0], both, route(1, far_of))
+    got_3 = lax.ppermute(straight[0], both, route(0, mid_of))
+    got_4 = lax.ppermute(straight[1], both, route(1, mid_of))
+    last = [
+        partial_sums(
+            spread, [(mixed(core, frame(far_of, 1), frame(near_of, 1)), 0, 0, ((0, core),))], [1], (got,), after=after
+        )[0]
+        for core, got, after in ((0, got_2, straight), (1, got_1, got_2))
     ]
-    parts = partial_sums(narrow, [(lambda s: 0, 0, 0, 0, ())], [1], cost=1 << 32)
-    spread = spread_out(2 + n_blocks * frames, False, parts[0])
-    for f in every[1:]:
-        parts += partial_sums(spread, [(beyond_of, f, 0, 0, ())], [1], after=parts, cost=1 << 32)
-    beyond = [lax.ppermute(part, "tm", near_route) for part in parts]
-    arrived, sums = [], None
-    for f in every:
-        jobs = [(mixed(core), f, core, 0, ((0, core),)) for core in range(2)]
-        sums = partial_sums(spread, jobs, [1, 1], (beyond[f],), after=sums)
-        arrived += [lax.ppermute(part, both, route) for part, route in zip(sums, mixed_route)]
+    got_5, got_6 = [lax.ppermute(sent, both, route(core, far_of)) for core, sent in enumerate(last)]
     home = []
-    for f in every:
-        adds = arrived[2 * f : 2 * f + 2] if f < frames - 1 else arrived[2 * f : 2 * f + 1]
-        jobs = [(lambda s: s, f, 0, 0, tuple((k, None) for k in range(len(adds))))]
+    for f, adds, added in (
+        (0, (got_1, got_2, got_3, got_4), ((0, 0), (1, 1), (2, None), (3, None))),
+        (1, (), ()),
+    ):
+        jobs = [(frame(lambda s: s, f), 0, 0, added)]
         after = home or None
         home += partial_sums(spread, jobs, [1], adds, True, jnp.float32, after=after, cost=1 << 35)
     result = pl.pallas_call(
         finish_kernel,
         out_shape=jax.ShapeDtypeStruct((cells, outs), jnp.bfloat16),
         compiler_params=params(),
-    )(*home, arrived[-1])
+    )(*home, got_5, got_6)
     return result.reshape(frames, rows, cols, outs)
 
 

time: 50.7 us -> 50.5 us (level)
  starting transfers between devices: 15 us -> 12.5 us
  waiting for transfers between devices: 22.7 us -> 24.7 us
    ppermute x1, starting transfers between devices: 3.73 us -> 1 us  [split_body(): got_edge_b = lax.ppermute(edge_same, ('tm', 'tile', 'chan'), edge_b)]
    ppermute x1, waiting for transfers between devices: 0.68 us -> 3.23 us  [split_body(): got_edge_a = lax.ppermute(edge_following, ('tm', 'tile', 'chan'), edge_a)]
    ppermute x1, starting transfers between devices: 0.51 us -> 2.14 us  [split_body(): got_b = lax.ppermute(same, both, route_b)]
    ppermute x1, waiting for transfers between devices: 5.69 us -> 4.33 us  [split_body(): got_edge_b = lax.ppermute(edge_same, ('tm', 'tile', 'chan'), edge_b)]
    ppermute x6, starting transfers between devices: 6.61 us -> 5.7 us  [the longest x1 2.6 us: split_body(): got_3 = lax.ppermute(straight[0], both, route(0, mid_of))]
    ppermute x1, starting transfers between devices: 1.44 us -> 0.54 us  [split_body(): got_edge_a = lax.ppermute(edge_following, ('tm', 'tile', 'chan'), edge_a)]
    ppermute x6, waiting for transfers between devices: 14.6 us -> 15.3 us  [the longest x1 7.09 us: split_body(): got_2 = lax.ppermute(second[0], both, route(1, far_of))]
    pallas_call x6 -> x7, Pallas kernels: 6.68 us -> 6.93 us  [partial_sums(): pl.pallas_call(functools.partial(partial_kernel, jobs=jobs, n_adds=len(ad...]
  transfers between devices with their start and end apart: 11 -> 11, of which waited for: 9 -> 8; matrix products, arithmetic and copies ran while one was open for 3% -> 3% of each run, Pallas kernels for 15% -> 16%
where the time goes in v6:
time: 50.5 us; the launch traced here: 50.3 us
  waiting for transfers between devices  24.7 us (49%)
  starting transfers between devices  12.5 us (25%)
  Pallas kernels  10.6 us (21%)
  local copies, waits for them, and re-layouts  2.33 us (5%)
    ppermute x1, waiting for transfers between devices, split_body(): got_2 = lax.ppermute(second[0], both, route(1, far_of))  7.09 us
    pallas_call x7, Pallas kernels, partial_sums(): pl.pallas_call(functools.partial(partial_kernel, jobs=jobs, n_adds=len(ad...  6.93 us
    ppermute x2, waiting for transfers between devices, split_body(): lax.ppermute(sent, both, route(core, far_of))  5.65 us
    ppermute x1, waiting for transfers between devices, split_body(): got_edge_b = lax.ppermute(edge_same, ('tm', 'tile', 'chan'), edge_b)  4.33 us
    ppermute x1, waiting for transfers between devices, split_body(): got_edge_a = lax.ppermute(edge_following, ('tm', 'tile', 'chan'), edge_a)  3.23 us
    ppermute x1, starting transfers between devices, split_body(): got_a = lax.ppermute(following, both, route_a)  3.08 us
    ppermute x1, starting transfers between devices, split_body(): got_3 = lax.ppermute(straight[0], both, route(0, mid_of))  2.6 us
    pallas_call x2, Pallas kernels, spread_out(): pl.pallas_call(functools.partial(spread_kernel, frames=frames, rows=rows,...  2.4 us
  transfers between devices with their start and end apart: 11, of which 8 were waited for; matrix products, arithmetic and copies ran while one was open for 3% of the time, Pallas kernels for 16%

profile of v6, /device:TPU:0, one launch (start us, length us, event | category | flops | bytes accessed | tf_op | source)
XLA Modules:
  0.0 50.3 jit_solution(17886973705738074862)
XLA Ops:
  0.0 1.0 %copy-done.1 = bf16[2,24,16,256]{3,2,1,0:T(8,128)(2,1)S(1)} copy-done((bf16[2,24,16,256]{3,2,1,0:T(8,128)(2,1)S(1)}, bf16[2,24,16,256]{3,2,1,0:T(8,128)(2,1)}, u32[]{:S(2)}) %copy-start.1) | copy-done | bytes 393240
  1.0 0.2 shard_map.55
  1.2 3.1 %collective-permute-start = (bf16[784,128]{1,0:T(8,128)(2,1)S(1)}, bf16[784,128]{1,0:T(8,128)(2,1)S(1)}, u32[]{:S(2)}, u32[]{:S(2)}) collective-permute-start(bf16[784,128]{1,0:T(8,128)(2,1)S(1)} %get-tuple-element.18), channel_id=1, source_target_pairs={{0,4},{1,12},{4,0},{5,8},{9,13},{8,5},{13,9},{12,1},{2,6},{3,14},{... | collective-permute-start | bytes 602120 | tf_op jit(solution)/shard_map/ppermute | solution.py:335
  4.3 2.1 %collective-permute-start.2 = (bf16[784,128]{1,0:T(8,128)(2,1)S(1)}, bf16[784,128]{1,0:T(8,128)(2,1)S(1)}, u32[]{:S(2)}, u32[]{:S(2)}) collective-permute-start(bf16[784,128]{1,0:T(8,128)(2,1)S(1)} %get-tuple-element.21.same_ref), channel_id=1, source_target_pairs={{0,1},{1,9},{4,5},{5,13},{9,8},{8,0},{13,12},{12,4},{2,3},{3,11},{... | collective-permute-start | bytes 602120 | tf_op jit(solution)/shard_map/ppermute | solution.py:334
  6.4 0.7 %reshape.19.gain_ref = bf16[1,256]{1,0:T(2,128)(2,1)S(1)} reshape(bf16[256]{0:T(256)(128)(2,1)} %param.6) | data formatting | bytes 1024 | tf_op jit(solution)/shard_map/reshape | solution.py:317
  7.1 0.7 %reshape.20.bias_ref = bf16[1,256]{1,0:T(2,128)(2,1)S(1)} reshape(bf16[256]{0:T(256)(128)(2,1)} %param.7) | data formatting | bytes 1024 | tf_op jit(solution)/shard_map/reshape | solution.py:317
  7.8 0.2 shard_map.56
  8.0 0.5 %collective-permute-start.1 = (bf16[64,128]{1,0:T(8,128)(2,1)S(1)}, bf16[64,128]{1,0:T(8,128)(2,1)S(1)}, u32[]{:S(2)}, u32[]{:S(2)}) collective-permute-start(bf16[64,128]{1,0:T(8,128)(2,1)S(1)} %get-tuple-element.19), channel_id=1, source_target_pairs={{0,6},{2,4},{1,14},{3,12},{4,2},{6,0},{5,10},{7,8},{9,15},{11,13},... | collective-permute-start | bytes 49160 | tf_op jit(solution)/shard_map/ppermute | solution.py:337
  8.5 1.0 %collective-permute-start.3 = (bf16[64,128]{1,0:T(8,128)(2,1)S(1)}, bf16[64,128]{1,0:T(8,128)(2,1)S(1)}, u32[]{:S(2)}, u32[]{:S(2)}) collective-permute-start(bf16[64,128]{1,0:T(8,128)(2,1)S(1)} %get-tuple-element.20), channel_id=1, source_target_pairs={{0,3},{2,1},{1,11},{3,9},{4,7},{6,5},{5,15},{7,13},{9,10},{11,8},{... | collective-permute-start | bytes 49160 | tf_op jit(solution)/shard_map/ppermute | solution.py:336
  9.5 3.2 %collective-permute-done.1.refs_1_.edge_a_ref = bf16[64,128]{1,0:T(8,128)(2,1)S(1)} collective-permute-done((bf16[64,128]{1,0:T(8,128)(2,1)S(1)}, bf16[64,128]{1,0:T(8,128)(2,1)S(1)}, u32[]{:S(2)}, u32[]{:S(2)}) %collective-permute-start.1) | collective-permute-done | bytes 16416 | tf_op jit(solution)/shard_map/ppermute | solution.py:337
  12.8 4.3 %collective-permute-done.3.refs_3_.edge_b_ref = bf16[64,128]{1,0:T(8,128)(2,1)S(1)} collective-permute-done((bf16[64,128]{1,0:T(8,128)(2,1)S(1)}, bf16[64,128]{1,0:T(8,128)(2,1)S(1)}, u32[]{:S(2)}, u32[]{:S(2)}) %collective-permute-start.3) | collective-permute-done | bytes 16416 | tf_op jit(solution)/shard_map/ppermute | solution.py:336
  17.1 0.1 collective-permute-start.4
  17.2 1.8 %collective-permute-done.4.swapped_ref = bf16[1696,128]{1,0:T(8,128)(2,1)S(1)} collective-permute-done((bf16[1696,128]{1,0:T(8,128)(2,1)S(1)}, bf16[1696,128]{1,0:T(8,128)(2,1)S(1)}, u32[]{:S(2)}, u32[]{:S(2)}) %collective-permute-start.4) | collective-permute-done | bytes 434208 | tf_op jit(solution)/shard_map/ppermute | solution.py:345
  19.0 0.8 %shard_map.58.spread_ref = bf16[3,4,26,16,128]{4,3,2,1,0:T(8,128)(2,1)S(1)} custom-call(bf16[784,128]{1,0:T(8,128)(2,1)S(1)} %get-tuple-element.21.same_ref, bf16[784,128]{1,0:T(8,128)(2,1)S(1)} %collective-permute-done.refs_0_.a_ref, bf16[64,128]{1,0:T(8,128)(2,1)S(1)} %collective-permute-done.1.refs_1_.edge_a_ref, ...), custom_call_target="tpu_custom_call" | custom-call | tf_op jit(solution)/shard_map/pallas_call | solution.py:349
  19.9 0.9 %shard_map.59 = bf16[384,256]{1,0:T(8,128)(2,1)S(1)} custom-call(bf16[3,4,26,16,128]{4,3,2,1,0:T(8,128)(2,1)S(1)} %shard_map.58.spread_ref, bf16[3456,256]{1,0:T(8,128)(2,1)S(1)} %bitcast.3), custom_call_target="tpu_custom_call" | custom-call | flops 4294967296 | bytes 1 | tf_op jit(solution)/shard_map/pallas_call | solution.py:365
  20.8 1.6 %collective-permute-start.5 = (bf16[384,256]{1,0:T(8,128)(2,1)S(1)}, bf16[384,256]{1,0:T(8,128)(2,1)S(1)}, u32[]{:S(2)}, u32[]{:S(2)}) collective-permute-start(bf16[384,256]{1,0:T(8,128)(2,1)S(1)} %shard_map.59), channel_id=1, source_target_pairs={{0,12},{1,5},{4,8},{5,1},{8,4},{9,13},{12,0},{13,9},{2,14},{3,7},{... | collective-permute-start | bytes 589832 | tf_op jit(solution)/shard_map/ppermute | solution.py:400
  22.4 1.5 %shard_map.60.spread_ref = bf16[3,10,26,16,128]{4,3,2,1,0:T(8,128)(2,1)S(1)} custom-call(bf16[784,128]{1,0:T(8,128)(2,1)S(1)} %get-tuple-element.21.same_ref, bf16[784,128]{1,0:T(8,128)(2,1)S(1)} %collective-permute-done.refs_0_.a_ref, bf16[64,128]{1,0:T(8,128)(2,1)S(1)} %collective-permute-done.1.refs_1_.edge_a_ref, ...), custom_call_target="tpu_custom_call" | custom-call | tf_op jit(solution)/shard_map/pallas_call | solution.py:349
  23.9 0.9 %shard_map.61 = bf16[384,256]{1,0:T(8,128)(2,1)S(1)} custom-call(bf16[3,10,26,16,128]{4,3,2,1,0:T(8,128)(2,1)S(1)} %shard_map.60.spread_ref, bf16[3456,256]{1,0:T(8,128)(2,1)S(1)} %bitcast.4), custom_call_target="tpu_custom_call" | custom-call | flops 4294967296 | bytes 1 | tf_op jit(solution)/shard_map/pallas_call | solution.py:365
  24.8 0.4 collective-permute-start.6
  25.2 1.6 %shard_map.62 = (bf16[384,256]{1,0:T(8,128)(2,1)S(1)}, bf16[384,256]{1,0:T(8,128)(2,1)S(1)}) custom-call(bf16[3,10,26,16,128]{4,3,2,1,0:T(8,128)(2,1)S(1)} %shard_map.60.spread_ref, bf16[3456,256]{1,0:T(8,128)(2,1)S(1)} %bitcast.5), custom_call_target="tpu_custom_call" | custom-call | flops 4294967296 | bytes 1 | tf_op jit(solution)/shard_map/pallas_call | solution.py:365
  26.8 2.6 %collective-permute-start.7 = (bf16[384,256]{1,0:T(8,128)(2,1)S(1)}, bf16[384,256]{1,0:T(8,128)(2,1)S(1)}, u32[]{:S(2)}, u32[]{:S(2)}) collective-permute-start(bf16[384,256]{1,0:T(8,128)(2,1)S(1)} %get-tuple-element.24), channel_id=1, source_target_pairs={{0,8},{1,5},{4,12},{5,1},{8,0},{9,13},{12,4},{13,9},{2,10},{3,7},{... | collective-permute-start | bytes 589832 | tf_op jit(solution)/shard_map/ppermute | solution.py:402
  29.4 7.1 %collective-permute-done.6.rest_1_.rest_0_ = bf16[384,256]{1,0:T(8,128)(2,1)S(1)} collective-permute-done((bf16[384,256]{1,0:T(8,128)(2,1)S(1)}, bf16[384,256]{1,0:T(8,128)(2,1)S(1)}, u32[]{:S(2)}, u32[]{:S(2)}) %collective-permute-start.6) | collective-permute-done | bytes 196640 | tf_op jit(solution)/shard_map/ppermute | solution.py:401
  36.5 0.9 %shard_map.66 = bf16[384,256]{1,0:T(8,128)(2,1)S(1)} custom-call(bf16[3,10,26,16,128]{4,3,2,1,0:T(8,128)(2,1)S(1)} %shard_map.60.spread_ref, bf16[3456,256]{1,0:T(8,128)(2,1)S(1)} %bitcast.6, bf16[384,256]{1,0:T(8,128)(2,1)S(1)} %collective-permute-done.5.rest_0_), custom_call_target="tpu_custom_call" | custom-call | flops 1 | bytes 1 | tf_op jit(solution)/shard_map/pallas_call | solution.py:365
  37.5 0.9 %shard_map.65 = bf16[384,256]{1,0:T(8,128)(2,1)S(1)} custom-call(bf16[3,10,26,16,128]{4,3,2,1,0:T(8,128)(2,1)S(1)} %shard_map.60.spread_ref, bf16[3456,256]{1,0:T(8,128)(2,1)S(1)} %bitcast.7, bf16[384,256]{1,0:T(8,128)(2,1)S(1)} %collective-permute-done.6.rest_1_.rest_0_), custom_call_target="tpu_custom_call" | custom-call | flops 1 | bytes 1 | tf_op jit(solution)/shard_map/pallas_call | solution.py:365
  38.4 1.0 %collective-permute-start.9 = (bf16[384,256]{1,0:T(8,128)(2,1)S(1)}, bf16[384,256]{1,0:T(8,128)(2,1)S(1)}, u32[]{:S(2)}, u32[]{:S(2)}) collective-permute-start(bf16[384,256]{1,0:T(8,128)(2,1)S(1)} %shard_map.65), channel_id=1, source_target_pairs={{0,12},{1,5},{4,8},{5,1},{8,4},{9,13},{12,0},{13,9},{2,14},{3,7},{... | collective-permute-start | bytes 589832 | tf_op jit(solution)/shard_map/ppermute | solution.py:410
  39.4 0.5 collective-permute-done.7.rest_2_
  39.9 2.1 %collective-permute-done.8.rest_3_ = bf16[384,256]{1,0:T(8,128)(2,1)S(1)} collective-permute-done((bf16[384,256]{1,0:T(8,128)(2,1)S(1)}, bf16[384,256]{1,0:T(8,128)(2,1)S(1)}, u32[]{:S(2)}, u32[]{:S(2)}) %collective-permute-start.8) | collective-permute-done | bytes 196640 | tf_op jit(solution)/shard_map/ppermute | solution.py:403
  42.0 0.9 %shard_map.63.first_ref = f32[384,256]{1,0:T(8,128)S(1)} custom-call(bf16[3,10,26,16,128]{4,3,2,1,0:T(8,128)(2,1)S(1)} %shard_map.60.spread_ref, bf16[3456,256]{1,0:T(8,128)(2,1)S(1)} %bitcast.8, bf16[384,256]{1,0:T(8,128)(2,1)S(1)} %collective-permute-done.5.rest_0_, bf16[384,256]{1,0:T(8,128)(2,1)S(1)} %collective-permute-done.6.rest_1_.rest_0_, ...), custom_call_target="tpu_custom_call" | custom-call | flops 34359738368 | bytes 1 | tf_op jit(solution)/shard_map/pallas_call | solution.py:365
  42.9 0.9 %shard_map.64.second_ref = f32[384,256]{1,0:T(8,128)S(1)} custom-call(bf16[3,10,26,16,128]{4,3,2,1,0:T(8,128)(2,1)S(1)} %shard_map.60.spread_ref, bf16[3456,256]{1,0:T(8,128)(2,1)S(1)} %bitcast.9, bf16[1,256]{1,0:T(2,128)(2,1)S(1)} %reshape.22.rest_4_.rest_0_), custom_call_target="tpu_custom_call" | custom-call | flops 34359738368 | bytes 1 | tf_op jit(solution)/shard_map/pallas_call | solution.py:365
  43.8 5.3 %collective-permute-done.10.other_ref = bf16[384,256]{1,0:T(8,128)(2,1)S(1)} collective-permute-done((bf16[384,256]{1,0:T(8,128)(2,1)S(1)}, bf16[384,256]{1,0:T(8,128)(2,1)S(1)}, u32[]{:S(2)}, u32[]{:S(2)}) %collective-permute-start.10) | collective-permute-done | bytes 196640 | tf_op jit(solution)/shard_map/ppermute | solution.py:410
  49.1 0.4 collective-permute-done.9.one_ref
  49.5 0.8 %shard_map.67 = bf16[768,256]{1,0:T(8,128)(2,1)} custom-call(f32[384,256]{1,0:T(8,128)S(1)} %shard_map.63.first_ref, f32[384,256]{1,0:T(8,128)S(1)} %shard_map.64.second_ref, bf16[384,256]{1,0:T(8,128)(2,1)S(1)} %collective-permute-done.9.one_ref, bf16[384,256]{1,0:T(8,128)(2,1)S(1)} %collective-permute-done.10.other_ref), custom_call_target="tpu_custom_call" | custom-call | tf_op jit(solution)/shard_map/pallas_call | solution.py:419
  (12 shorter events, 0.2 us)
Async XLA Ops:
  0.0 1.0 %copy-start.1 = (bf16[2,24,16,256]{3,2,1,0:T(8,128)(2,1)S(1)}, bf16[2,24,16,256]{3,2,1,0:T(8,128)(2,1)}, u32[]{:S(2)}) copy-start(bf16[2,24,16,256]{3,2,1,0:T(8,128)(2,1)} %param.5) | copy-start | bytes 1179652
  1.2 15.9 %collective-permute-start = (bf16[784,128]{1,0:T(8,128)(2,1)S(1)}, bf16[784,128]{1,0:T(8,128)(2,1)S(1)}, u32[]{:S(2)}, u32[]{:S(2)}) collective-permute-start(bf16[784,128]{1,0:T(8,128)(2,1)S(1)} %get-tuple-element.18), channel_id=1, source_target_pairs={{0,4},{1,12},{4,0},{5,8},{9,13},{8,5},{13,9},{12,1},{2,6},{3,14},{... | collective-permute-start | bytes 602120 | tf_op jit(solution)/shard_map/ppermute | solution.py:335
  4.3 12.8 %collective-permute-start.2 = (bf16[784,128]{1,0:T(8,128)(2,1)S(1)}, bf16[784,128]{1,0:T(8,128)(2,1)S(1)}, u32[]{:S(2)}, u32[]{:S(2)}) collective-permute-start(bf16[784,128]{1,0:T(8,128)(2,1)S(1)} %get-tuple-element.21.same_ref), channel_id=1, source_target_pairs={{0,1},{1,9},{4,5},{5,13},{9,8},{8,0},{13,12},{12,4},{2,3},{3,11},{... | collective-permute-start | bytes 602120 | tf_op jit(solution)/shard_map/ppermute | solution.py:334
  7.8 12.1 %copy-start = (bf16[27,128,256]{2,1,0:T(8,128)(2,1)S(1)}, bf16[27,128,256]{2,1,0:T(8,128)(2,1)}, u32[]{:S(2)}) copy-start(bf16[27,128,256]{2,1,0:T(8,128)(2,1)} %param.8) | copy-start | bytes 5308420
  8.0 4.8 %collective-permute-start.1 = (bf16[64,128]{1,0:T(8,128)(2,1)S(1)}, bf16[64,128]{1,0:T(8,128)(2,1)S(1)}, u32[]{:S(2)}, u32[]{:S(2)}) collective-permute-start(bf16[64,128]{1,0:T(8,128)(2,1)S(1)} %get-tuple-element.19), channel_id=1, source_target_pairs={{0,6},{2,4},{1,14},{3,12},{4,2},{6,0},{5,10},{7,8},{9,15},{11,13},... | collective-permute-start | bytes 49160 | tf_op jit(solution)/shard_map/ppermute | solution.py:337
  8.5 8.6 %collective-permute-start.3 = (bf16[64,128]{1,0:T(8,128)(2,1)S(1)}, bf16[64,128]{1,0:T(8,128)(2,1)S(1)}, u32[]{:S(2)}, u32[]{:S(2)}) collective-permute-start(bf16[64,128]{1,0:T(8,128)(2,1)S(1)} %get-tuple-element.20), channel_id=1, source_target_pairs={{0,3},{2,1},{1,11},{3,9},{4,7},{6,5},{5,15},{7,13},{9,10},{11,8},{... | collective-permute-start | bytes 49160 | tf_op jit(solution)/shard_map/ppermute | solution.py:336
  17.1 1.8 %collective-permute-start.4 = (bf16[1696,128]{1,0:T(8,128)(2,1)S(1)}, bf16[1696,128]{1,0:T(8,128)(2,1)S(1)}, u32[]{:S(2)}, u32[]{:S(2)}) collective-permute-start(bf16[1696,128]{1,0:T(8,128)(2,1)S(1)} %shard_map.57), channel_id=1, source_target_pairs={{0,1},{1,0},{2,3},{3,2},{4,5},{5,4},{6,7},{7,6},{8,9},{9,8},{10,11... | collective-permute-start | bytes 1302536 | tf_op jit(solution)/shard_map/ppermute | solution.py:345
  20.8 15.8 %collective-permute-start.5 = (bf16[384,256]{1,0:T(8,128)(2,1)S(1)}, bf16[384,256]{1,0:T(8,128)(2,1)S(1)}, u32[]{:S(2)}, u32[]{:S(2)}) collective-permute-start(bf16[384,256]{1,0:T(8,128)(2,1)S(1)} %shard_map.59), channel_id=1, source_target_pairs={{0,12},{1,5},{4,8},{5,1},{8,4},{9,13},{12,0},{13,9},{2,14},{3,7},{... | collective-permute-start | bytes 589832 | tf_op jit(solution)/shard_map/ppermute | solution.py:400
  24.8 4.6 %copy-start.2 = (bf16[256]{0:T(256)(128)(2,1)S(1)}, bf16[256]{0:T(256)(128)(2,1)}, u32[]{:S(2)}) copy-start(bf16[256]{0:T(256)(128)(2,1)} %param.9) | copy-start | bytes 1540
  24.8 11.7 %collective-permute-start.6 = (bf16[384,256]{1,0:T(8,128)(2,1)S(1)}, bf16[384,256]{1,0:T(8,128)(2,1)S(1)}, u32[]{:S(2)}, u32[]{:S(2)}) collective-permute-start(bf16[384,256]{1,0:T(8,128)(2,1)S(1)} %shard_map.61), channel_id=1, source_target_pairs={{0,4},{1,13},{4,0},{5,9},{8,12},{9,5},{12,8},{13,1},{2,6},{3,15},{... | collective-permute-start | bytes 589832 | tf_op jit(solution)/shard_map/ppermute | solution.py:401
  26.8 13.1 %collective-permute-start.7 = (bf16[384,256]{1,0:T(8,128)(2,1)S(1)}, bf16[384,256]{1,0:T(8,128)(2,1)S(1)}, u32[]{:S(2)}, u32[]{:S(2)}) collective-permute-start(bf16[384,256]{1,0:T(8,128)(2,1)S(1)} %get-tuple-element.24), channel_id=1, source_target_pairs={{0,8},{1,5},{4,12},{5,1},{8,0},{9,13},{12,4},{13,9},{2,10},{3,7},{... | collective-permute-start | bytes 589832 | tf_op jit(solution)/shard_map/ppermute | solution.py:402
  29.4 12.6 %collective-permute-start.8 = (bf16[384,256]{1,0:T(8,128)(2,1)S(1)}, bf16[384,256]{1,0:T(8,128)(2,1)S(1)}, u32[]{:S(2)}, u32[]{:S(2)}) collective-permute-start(bf16[384,256]{1,0:T(8,128)(2,1)S(1)} %get-tuple-element.25), channel_id=1, source_target_pairs={{0,4},{1,9},{4,0},{5,13},{8,12},{9,1},{12,8},{13,5},{2,6},{3,11},{... | collective-permute-start | bytes 589832 | tf_op jit(solution)/shard_map/ppermute | solution.py:403
  37.4 11.6 %collective-permute-start.10 = (bf16[384,256]{1,0:T(8,128)(2,1)S(1)}, bf16[384,256]{1,0:T(8,128)(2,1)S(1)}, u32[]{:S(2)}, u32[]{:S(2)}) collective-permute-start(bf16[384,256]{1,0:T(8,128)(2,1)S(1)} %shard_map.66), channel_id=1, source_target_pairs={{0,4},{1,13},{4,0},{5,9},{8,12},{9,5},{12,8},{13,1},{2,6},{3,15},{... | collective-permute-start | bytes 589832 | tf_op jit(solution)/shard_map/ppermute | solution.py:410
  38.4 11.1 %collective-permute-start.9 = (bf16[384,256]{1,0:T(8,128)(2,1)S(1)}, bf16[384,256]{1,0:T(8,128)(2,1)S(1)}, u32[]{:S(2)}, u32[]{:S(2)}) collective-permute-start(bf16[384,256]{1,0:T(8,128)(2,1)S(1)} %shard_map.65), channel_id=1, source_target_pairs={{0,12},{1,5},{4,8},{5,1},{8,4},{9,13},{12,0},{13,9},{2,14},{3,7},{... | collective-permute-start | bytes 589832 | tf_op jit(solution)/shard_map/ppermute | solution.py:410

commit v7 on v6

--- a/solution.py
+++ b/solution.py
@@ -228,31 +228,34 @@
     col = lax.broadcasted_iota(jnp.int32, (rows, cols, LANES), 1)
     span = rows * cols
 
-    def place(ref, edge_ref, skip, start):
-        for f in range(frames):
-            value = normed(ref[f * span : (f + 1) * span])
-            edge = normed(edge_ref[skip + f * rows : skip + (f + 1) * rows])
-            edge = jnp.broadcast_to(edge[:, None, :], (rows, cols, LANES))
-            left = pltpu.roll(value, 1, 0).reshape(rows, cols, LANES)
-            left = jnp.where(col == 0, jnp.where(tile == 1, edge, 0.0), left)
-            right = pltpu.roll(value, span - 1, 0).reshape(rows, cols, LANES)
-            right = jnp.where(col == cols - 1, jnp.where(tile == 0, edge, 0.0), right)
-            at = start + f
-            out_ref[0, at, 1 : rows + 1] = left.astype(jnp.bfloat16)
-            out_ref[1, at, 1 : rows + 1] = value.reshape(rows, cols, LANES).astype(jnp.bfloat16)
-            out_ref[2, at, 1 : rows + 1] = right.astype(jnp.bfloat16)
+    def place(ref, edge_ref, skip, start, f):
+        value = normed(ref[f * span : (f + 1) * span])
+        edge = normed(edge_ref[skip + f * rows : skip + (f + 1) * rows])
+        edge = jnp.broadcast_to(edge[:, None, :], (rows, cols, LANES))
+        left = pltpu.roll(value, 1, 0).reshape(rows, cols, LANES)
+        left = jnp.where(col == 0, jnp.where(tile == 1, edge, 0.0), left)
+        right = pltpu.roll(value, span - 1, 0).reshape(rows, cols, LANES)
+        right = jnp.where(col == cols - 1, jnp.where(tile == 0, edge, 0.0), right)
+        at = start + f
+        out_ref[0, at, 1 : rows + 1] = left.astype(jnp.bfloat16)
+        out_ref[1, at, 1 : rows + 1] = value.reshape(rows, cols, LANES).astype(jnp.bfloat16)
+        out_ref[2, at, 1 : rows + 1] = right.astype(jnp.bfloat16)
 
     if first:
-        target = jnp.where(lax.axis_index("chan") == 0, far, mid)
+        core = lax.axis_index("chan")
+        target = jnp.where(core == 0, far, mid)
         pl.when(target == 0)(clear)
         for ref, edge_ref, skip, block in pieces:
-            wanted = jnp.logical_or(block == target, block == target - 1)
             start = (block - target + 1) * frames
-            pl.when(wanted)(functools.partial(place, ref, edge_ref, skip, start))
+            for f in range(frames):
+                at = start + f
+                wanted = jnp.logical_and(at >= core, at <= core + 2)
+                pl.when(wanted)(functools.partial(place, ref, edge_ref, skip, start, f))
     else:
         clear()
         for ref, edge_ref, skip, block in pieces:
-            place(ref, edge_ref, skip, 2 + block * frames)
+            for f in range(frames):
+                place(ref, edge_ref, skip, 2 + block * frames, f)
 
 
 def partial_kernel(spread_ref, weight_ref, *rest, jobs, n_adds, n_outs, frames, rows, cols, with_bias):
@@ -279,11 +282,14 @@
         outs[out][place * span : (place + 1) * span] = total.astype(outs[out].dtype)
 
 
-def finish_kernel(first_ref, second_ref, one_ref, other_ref, out_ref):
-    span = first_ref.shape[0]
-    out_ref[:span] = first_ref[...].astype(out_ref.dtype)
+def finish_kernel(whole_ref, second_ref, one_ref, other_ref, out_ref):
+    del whole_ref
     total = second_ref[...] + one_ref[...].astype(jnp.float32) + other_ref[...].astype(jnp.float32)
-    out_ref[span:] = total.astype(out_ref.dtype)
+    out_ref[...] = total.astype(out_ref.dtype)
+
+
+def place_kernel(first_ref, out_ref):
+    out_ref[...] = first_ref[...].astype(out_ref.dtype)
 
 
 def params():
@@ -416,11 +422,24 @@
         jobs = [(frame(lambda s: s, f), 0, 0, added)]
         after = home or None
         home += partial_sums(spread, jobs, [1], adds, True, jnp.float32, after=after, cost=1 << 35)
+    span = rows * cols
+    whole = pl.pallas_call(
+        place_kernel,
+        grid=(1,),
+        in_specs=[pl.BlockSpec((span, outs), lambda i: (0, 0))],
+        out_specs=pl.BlockSpec((span, outs), lambda i: (0, 0)),
+        out_shape=jax.ShapeDtypeStruct((cells, outs), jnp.bfloat16),
+        compiler_params=params(),
+    )(home[0])
     result = pl.pallas_call(
         finish_kernel,
+        grid=(1,),
+        in_specs=[pl.BlockSpec(memory_space=pl.ANY)] + [pl.BlockSpec((span, outs), lambda i: (0, 0))] * 3,
+        out_specs=pl.BlockSpec((span, outs), lambda i: (1, 0)),
         out_shape=jax.ShapeDtypeStruct((cells, outs), jnp.bfloat16),
+        input_output_aliases={0: 0},
         compiler_params=params(),
-    )(*home, got_5, got_6)
+    )(whole, home[1], got_5, got_6)
     return result.reshape(frames, rows, cols, outs)
 
 

time: 50.5 us -> 50.3 us (level)
  waiting for transfers between devices: 24.7 us -> 23.9 us
    ppermute x2, waiting for transfers between devices: 5.65 us -> 4.68 us  [split_body(): lax.ppermute(sent, both, route(core, far_of))]
    pallas_call x1 -> x2, Pallas kernels: 0.83 us -> 1.44 us  [the longest x1 0.74 us: split_body(): pl.pallas_call(finish_kernel, grid=(1,), in_specs=[pl.BlockSpec(memory_sp...]
  transfers between devices with their start and end apart: 11 -> 11, of which waited for: 8 -> 8; matrix products, arithmetic and copies ran while one was open for 3% -> 3% of each run, Pallas kernels for 16% -> 17%
where the time goes in v7:
time: 50.3 us; the launch traced here: 50.1 us
  waiting for transfers between devices  23.9 us (48%)
  starting transfers between devices  12.6 us (25%)
  Pallas kernels  11.1 us (22%)
  local copies, waits for them, and re-layouts  2.33 us (5%)
    ppermute x1, waiting for transfers between devices, split_body(): got_2 = lax.ppermute(second[0], both, route(1, far_of))  7.08 us
    pallas_call x7, Pallas kernels, partial_sums(): pl.pallas_call(functools.partial(partial_kernel, jobs=jobs, n_adds=len(ad...  6.92 us
    ppermute x2, waiting for transfers between devices, split_body(): lax.ppermute(sent, both, route(core, far_of))  4.68 us
    ppermute x1, waiting for transfers between devices, split_body(): got_edge_b = lax.ppermute(edge_same, ('tm', 'tile', 'chan'), edge_b)  4.33 us
    ppermute x1, waiting for transfers between devices, split_body(): got_edge_a = lax.ppermute(edge_following, ('tm', 'tile', 'chan'), edge_a)  3.23 us
    ppermute x1, starting transfers between devices, split_body(): got_a = lax.ppermute(following, both, route_a)  3.08 us
    ppermute x1, starting transfers between devices, split_body(): got_3 = lax.ppermute(straight[0], both, route(0, mid_of))  2.59 us
    ppermute x1, waiting for transfers between devices, split_body(): got_4 = lax.ppermute(straight[1], both, route(1, mid_of))  2.48 us
  transfers between devices with their start and end apart: 11, of which 8 were waited for; matrix products, arithmetic and copies ran while one was open for 3% of the time, Pallas kernels for 17%

profile of v7, /device:TPU:0, one launch (start us, length us, event | category | flops | bytes accessed | tf_op | source)
XLA Modules:
  0.0 50.1 jit_solution(7881801731266946305)
XLA Ops:
  0.0 1.0 %copy-done.1 = bf16[2,24,16,256]{3,2,1,0:T(8,128)(2,1)S(1)} copy-done((bf16[2,24,16,256]{3,2,1,0:T(8,128)(2,1)S(1)}, bf16[2,24,16,256]{3,2,1,0:T(8,128)(2,1)}, u32[]{:S(2)}) %copy-start.1) | copy-done | bytes 393240
  1.0 0.2 shard_map.55
  1.2 3.1 %collective-permute-start = (bf16[784,128]{1,0:T(8,128)(2,1)S(1)}, bf16[784,128]{1,0:T(8,128)(2,1)S(1)}, u32[]{:S(2)}, u32[]{:S(2)}) collective-permute-start(bf16[784,128]{1,0:T(8,128)(2,1)S(1)} %get-tuple-element.18), channel_id=1, source_target_pairs={{0,4},{1,12},{4,0},{5,8},{9,13},{8,5},{13,9},{12,1},{2,6},{3,14},{... | collective-permute-start | bytes 602120 | tf_op jit(solution)/shard_map/ppermute | solution.py:341
  4.3 2.1 %collective-permute-start.2 = (bf16[784,128]{1,0:T(8,128)(2,1)S(1)}, bf16[784,128]{1,0:T(8,128)(2,1)S(1)}, u32[]{:S(2)}, u32[]{:S(2)}) collective-permute-start(bf16[784,128]{1,0:T(8,128)(2,1)S(1)} %get-tuple-element.21.same_ref), channel_id=1, source_target_pairs={{0,1},{1,9},{4,5},{5,13},{9,8},{8,0},{13,12},{12,4},{2,3},{3,11},{... | collective-permute-start | bytes 602120 | tf_op jit(solution)/shard_map/ppermute | solution.py:340
  6.4 0.7 %reshape.19.gain_ref = bf16[1,256]{1,0:T(2,128)(2,1)S(1)} reshape(bf16[256]{0:T(256)(128)(2,1)} %param.6) | data formatting | bytes 1024 | tf_op jit(solution)/shard_map/reshape | solution.py:323
  7.1 0.7 %reshape.20.bias_ref = bf16[1,256]{1,0:T(2,128)(2,1)S(1)} reshape(bf16[256]{0:T(256)(128)(2,1)} %param.7) | data formatting | bytes 1024 | tf_op jit(solution)/shard_map/reshape | solution.py:323
  7.8 0.2 shard_map.56
  8.0 0.5 %collective-permute-start.1 = (bf16[64,128]{1,0:T(8,128)(2,1)S(1)}, bf16[64,128]{1,0:T(8,128)(2,1)S(1)}, u32[]{:S(2)}, u32[]{:S(2)}) collective-permute-start(bf16[64,128]{1,0:T(8,128)(2,1)S(1)} %get-tuple-element.19), channel_id=1, source_target_pairs={{0,6},{2,4},{1,14},{3,12},{4,2},{6,0},{5,10},{7,8},{9,15},{11,13},... | collective-permute-start | bytes 49160 | tf_op jit(solution)/shard_map/ppermute | solution.py:343
  8.5 1.0 %collective-permute-start.3 = (bf16[64,128]{1,0:T(8,128)(2,1)S(1)}, bf16[64,128]{1,0:T(8,128)(2,1)S(1)}, u32[]{:S(2)}, u32[]{:S(2)}) collective-permute-start(bf16[64,128]{1,0:T(8,128)(2,1)S(1)} %get-tuple-element.20), channel_id=1, source_target_pairs={{0,3},{2,1},{1,11},{3,9},{4,7},{6,5},{5,15},{7,13},{9,10},{11,8},{... | collective-permute-start | bytes 49160 | tf_op jit(solution)/shard_map/ppermute | solution.py:342
  9.5 3.2 %collective-permute-done.1.refs_1_.edge_a_ref = bf16[64,128]{1,0:T(8,128)(2,1)S(1)} collective-permute-done((bf16[64,128]{1,0:T(8,128)(2,1)S(1)}, bf16[64,128]{1,0:T(8,128)(2,1)S(1)}, u32[]{:S(2)}, u32[]{:S(2)}) %collective-permute-start.1) | collective-permute-done | bytes 16416 | tf_op jit(solution)/shard_map/ppermute | solution.py:343
  12.8 4.3 %collective-permute-done.3.refs_3_.edge_b_ref = bf16[64,128]{1,0:T(8,128)(2,1)S(1)} collective-permute-done((bf16[64,128]{1,0:T(8,128)(2,1)S(1)}, bf16[64,128]{1,0:T(8,128)(2,1)S(1)}, u32[]{:S(2)}, u32[]{:S(2)}) %collective-permute-start.3) | collective-permute-done | bytes 16416 | tf_op jit(solution)/shard_map/ppermute | solution.py:342
  17.2 1.8 %collective-permute-done.4.swapped_ref = bf16[1696,128]{1,0:T(8,128)(2,1)S(1)} collective-permute-done((bf16[1696,128]{1,0:T(8,128)(2,1)S(1)}, bf16[1696,128]{1,0:T(8,128)(2,1)S(1)}, u32[]{:S(2)}, u32[]{:S(2)}) %collective-permute-start.4) | collective-permute-done | bytes 434208 | tf_op jit(solution)/shard_map/ppermute | solution.py:351
  19.0 0.7 %shard_map.58.spread_ref = bf16[3,4,26,16,128]{4,3,2,1,0:T(8,128)(2,1)S(1)} custom-call(bf16[784,128]{1,0:T(8,128)(2,1)S(1)} %get-tuple-element.21.same_ref, bf16[784,128]{1,0:T(8,128)(2,1)S(1)} %collective-permute-done.refs_0_.a_ref, bf16[64,128]{1,0:T(8,128)(2,1)S(1)} %collective-permute-done.1.refs_1_.edge_a_ref, ...), custom_call_target="tpu_custom_call" | custom-call | tf_op jit(solution)/shard_map/pallas_call | solution.py:355
  19.7 0.9 %shard_map.59 = bf16[384,256]{1,0:T(8,128)(2,1)S(1)} custom-call(bf16[3,4,26,16,128]{4,3,2,1,0:T(8,128)(2,1)S(1)} %shard_map.58.spread_ref, bf16[3456,256]{1,0:T(8,128)(2,1)S(1)} %bitcast.3), custom_call_target="tpu_custom_call" | custom-call | flops 4294967296 | bytes 1 | tf_op jit(solution)/shard_map/pallas_call | solution.py:371
  20.6 1.6 %collective-permute-start.5 = (bf16[384,256]{1,0:T(8,128)(2,1)S(1)}, bf16[384,256]{1,0:T(8,128)(2,1)S(1)}, u32[]{:S(2)}, u32[]{:S(2)}) collective-permute-start(bf16[384,256]{1,0:T(8,128)(2,1)S(1)} %shard_map.59), channel_id=1, source_target_pairs={{0,12},{1,5},{4,8},{5,1},{8,4},{9,13},{12,0},{13,9},{2,14},{3,7},{... | collective-permute-start | bytes 589832 | tf_op jit(solution)/shard_map/ppermute | solution.py:406
  22.3 1.5 %shard_map.60.spread_ref = bf16[3,10,26,16,128]{4,3,2,1,0:T(8,128)(2,1)S(1)} custom-call(bf16[784,128]{1,0:T(8,128)(2,1)S(1)} %get-tuple-element.21.same_ref, bf16[784,128]{1,0:T(8,128)(2,1)S(1)} %collective-permute-done.refs_0_.a_ref, bf16[64,128]{1,0:T(8,128)(2,1)S(1)} %collective-permute-done.1.refs_1_.edge_a_ref, ...), custom_call_target="tpu_custom_call" | custom-call | tf_op jit(solution)/shard_map/pallas_call | solution.py:355
  23.8 0.9 %shard_map.61 = bf16[384,256]{1,0:T(8,128)(2,1)S(1)} custom-call(bf16[3,10,26,16,128]{4,3,2,1,0:T(8,128)(2,1)S(1)} %shard_map.60.spread_ref, bf16[3456,256]{1,0:T(8,128)(2,1)S(1)} %bitcast.4), custom_call_target="tpu_custom_call" | custom-call | flops 4294967296 | bytes 1 | tf_op jit(solution)/shard_map/pallas_call | solution.py:371
  24.7 0.4 collective-permute-start.6
  25.1 1.6 %shard_map.62 = (bf16[384,256]{1,0:T(8,128)(2,1)S(1)}, bf16[384,256]{1,0:T(8,128)(2,1)S(1)}) custom-call(bf16[3,10,26,16,128]{4,3,2,1,0:T(8,128)(2,1)S(1)} %shard_map.60.spread_ref, bf16[3456,256]{1,0:T(8,128)(2,1)S(1)} %bitcast.5), custom_call_target="tpu_custom_call" | custom-call | flops 4294967296 | bytes 1 | tf_op jit(solution)/shard_map/pallas_call | solution.py:371
  26.7 2.6 %collective-permute-start.7 = (bf16[384,256]{1,0:T(8,128)(2,1)S(1)}, bf16[384,256]{1,0:T(8,128)(2,1)S(1)}, u32[]{:S(2)}, u32[]{:S(2)}) collective-permute-start(bf16[384,256]{1,0:T(8,128)(2,1)S(1)} %get-tuple-element.24), channel_id=1, source_target_pairs={{0,8},{1,5},{4,12},{5,1},{8,0},{9,13},{12,4},{13,9},{2,10},{3,7},{... | collective-permute-start | bytes 589832 | tf_op jit(solution)/shard_map/ppermute | solution.py:408
  29.3 7.1 %collective-permute-done.6.rest_1_.rest_0_ = bf16[384,256]{1,0:T(8,128)(2,1)S(1)} collective-permute-done((bf16[384,256]{1,0:T(8,128)(2,1)S(1)}, bf16[384,256]{1,0:T(8,128)(2,1)S(1)}, u32[]{:S(2)}, u32[]{:S(2)}) %collective-permute-start.6) | collective-permute-done | bytes 196640 | tf_op jit(solution)/shard_map/ppermute | solution.py:407
  36.4 0.9 %shard_map.67 = bf16[384,256]{1,0:T(8,128)(2,1)S(1)} custom-call(bf16[3,10,26,16,128]{4,3,2,1,0:T(8,128)(2,1)S(1)} %shard_map.60.spread_ref, bf16[3456,256]{1,0:T(8,128)(2,1)S(1)} %bitcast.6, bf16[384,256]{1,0:T(8,128)(2,1)S(1)} %collective-permute-done.5.rest_0_), custom_call_target="tpu_custom_call" | custom-call | flops 1 | bytes 1 | tf_op jit(solution)/shard_map/pallas_call | solution.py:371
  37.4 0.9 %shard_map.66 = bf16[384,256]{1,0:T(8,128)(2,1)S(1)} custom-call(bf16[3,10,26,16,128]{4,3,2,1,0:T(8,128)(2,1)S(1)} %shard_map.60.spread_ref, bf16[3456,256]{1,0:T(8,128)(2,1)S(1)} %bitcast.7, bf16[384,256]{1,0:T(8,128)(2,1)S(1)} %collective-permute-done.6.rest_1_.rest_0_), custom_call_target="tpu_custom_call" | custom-call | flops 1 | bytes 1 | tf_op jit(solution)/shard_map/pallas_call | solution.py:371
  38.3 1.1 %collective-permute-start.9 = (bf16[384,256]{1,0:T(8,128)(2,1)S(1)}, bf16[384,256]{1,0:T(8,128)(2,1)S(1)}, u32[]{:S(2)}, u32[]{:S(2)}) collective-permute-start(bf16[384,256]{1,0:T(8,128)(2,1)S(1)} %shard_map.66), channel_id=1, source_target_pairs={{0,12},{1,5},{4,8},{5,1},{8,4},{9,13},{12,0},{13,9},{2,14},{3,7},{... | collective-permute-start | bytes 589832 | tf_op jit(solution)/shard_map/ppermute | solution.py:416
  39.4 0.4 collective-permute-done.7.rest_2_
  39.8 2.5 %collective-permute-done.8.rest_3_ = bf16[384,256]{1,0:T(8,128)(2,1)S(1)} collective-permute-done((bf16[384,256]{1,0:T(8,128)(2,1)S(1)}, bf16[384,256]{1,0:T(8,128)(2,1)S(1)}, u32[]{:S(2)}, u32[]{:S(2)}) %collective-permute-start.8) | collective-permute-done | bytes 196640 | tf_op jit(solution)/shard_map/ppermute | solution.py:409
  42.2 0.9 %shard_map.63.first_ref = f32[384,256]{1,0:T(8,128)S(1)} custom-call(bf16[3,10,26,16,128]{4,3,2,1,0:T(8,128)(2,1)S(1)} %shard_map.60.spread_ref, bf16[3456,256]{1,0:T(8,128)(2,1)S(1)} %bitcast.8, bf16[384,256]{1,0:T(8,128)(2,1)S(1)} %collective-permute-done.5.rest_0_, bf16[384,256]{1,0:T(8,128)(2,1)S(1)} %collective-permute-done.6.rest_1_.rest_0_, ...), custom_call_target="tpu_custom_call" | custom-call | flops 34359738368 | bytes 1 | tf_op jit(solution)/shard_map/pallas_call | solution.py:371
  43.1 0.9 %shard_map.65.second_ref = f32[384,256]{1,0:T(8,128)S(1)} custom-call(bf16[3,10,26,16,128]{4,3,2,1,0:T(8,128)(2,1)S(1)} %shard_map.60.spread_ref, bf16[3456,256]{1,0:T(8,128)(2,1)S(1)} %bitcast.9, bf16[1,256]{1,0:T(2,128)(2,1)S(1)} %reshape.22.rest_4_.rest_0_), custom_call_target="tpu_custom_call" | custom-call | flops 34359738368 | bytes 1 | tf_op jit(solution)/shard_map/pallas_call | solution.py:371
  44.0 0.7 %shard_map.64.whole_ref = bf16[768,256]{1,0:T(8,128)(2,1)} custom-call(f32[384,256]{1,0:T(8,128)S(1)} %shard_map.63.first_ref), custom_call_target="tpu_custom_call" | custom-call | tf_op jit(solution)/shard_map/pallas_call | solution.py:426
  44.7 4.3 %collective-permute-done.10.other_ref = bf16[384,256]{1,0:T(8,128)(2,1)S(1)} collective-permute-done((bf16[384,256]{1,0:T(8,128)(2,1)S(1)}, bf16[384,256]{1,0:T(8,128)(2,1)S(1)}, u32[]{:S(2)}, u32[]{:S(2)}) %collective-permute-start.10) | collective-permute-done | bytes 196640 | tf_op jit(solution)/shard_map/ppermute | solution.py:416
  49.0 0.4 collective-permute-done.9.one_ref
  49.4 0.7 %shard_map.68 = bf16[768,256]{1,0:T(8,128)(2,1)} custom-call(bf16[768,256]{1,0:T(8,128)(2,1)} %shard_map.64.whole_ref, f32[384,256]{1,0:T(8,128)S(1)} %shard_map.65.second_ref, bf16[384,256]{1,0:T(8,128)(2,1)S(1)} %collective-permute-done.9.one_ref, bf16[384,256]{1,0:T(8,128)(2,1)S(1)} %collective-permute-done.10.other_ref), custom_call_target="tpu_custom_call", output_to_operand_aliasing={{}: (0, {})} | custom-call | tf_op jit(solution)/shard_map/pallas_call | solution.py:434
  (13 shorter events, 0.2 us)
Async XLA Ops:
  0.0 1.0 %copy-start.1 = (bf16[2,24,16,256]{3,2,1,0:T(8,128)(2,1)S(1)}, bf16[2,24,16,256]{3,2,1,0:T(8,128)(2,1)}, u32[]{:S(2)}) copy-start(bf16[2,24,16,256]{3,2,1,0:T(8,128)(2,1)} %param.5) | copy-start | bytes 1179652
  1.2 15.9 %collective-permute-start = (bf16[784,128]{1,0:T(8,128)(2,1)S(1)}, bf16[784,128]{1,0:T(8,128)(2,1)S(1)}, u32[]{:S(2)}, u32[]{:S(2)}) collective-permute-start(bf16[784,128]{1,0:T(8,128)(2,1)S(1)} %get-tuple-element.18), channel_id=1, source_target_pairs={{0,4},{1,12},{4,0},{5,8},{9,13},{8,5},{13,9},{12,1},{2,6},{3,14},{... | collective-permute-start | bytes 602120 | tf_op jit(solution)/shard_map/ppermute | solution.py:341
  4.3 12.8 %collective-permute-start.2 = (bf16[784,128]{1,0:T(8,128)(2,1)S(1)}, bf16[784,128]{1,0:T(8,128)(2,1)S(1)}, u32[]{:S(2)}, u32[]{:S(2)}) collective-permute-start(bf16[784,128]{1,0:T(8,128)(2,1)S(1)} %get-tuple-element.21.same_ref), channel_id=1, source_target_pairs={{0,1},{1,9},{4,5},{5,13},{9,8},{8,0},{13,12},{12,4},{2,3},{3,11},{... | collective-permute-start | bytes 602120 | tf_op jit(solution)/shard_map/ppermute | solution.py:340
  7.8 12.0 %copy-start = (bf16[27,128,256]{2,1,0:T(8,128)(2,1)S(1)}, bf16[27,128,256]{2,1,0:T(8,128)(2,1)}, u32[]{:S(2)}) copy-start(bf16[27,128,256]{2,1,0:T(8,128)(2,1)} %param.8) | copy-start | bytes 5308420
  8.0 4.8 %collective-permute-start.1 = (bf16[64,128]{1,0:T(8,128)(2,1)S(1)}, bf16[64,128]{1,0:T(8,128)(2,1)S(1)}, u32[]{:S(2)}, u32[]{:S(2)}) collective-permute-start(bf16[64,128]{1,0:T(8,128)(2,1)S(1)} %get-tuple-element.19), channel_id=1, source_target_pairs={{0,6},{2,4},{1,14},{3,12},{4,2},{6,0},{5,10},{7,8},{9,15},{11,13},... | collective-permute-start | bytes 49160 | tf_op jit(solution)/shard_map/ppermute | solution.py:343
  8.5 8.6 %collective-permute-start.3 = (bf16[64,128]{1,0:T(8,128)(2,1)S(1)}, bf16[64,128]{1,0:T(8,128)(2,1)S(1)}, u32[]{:S(2)}, u32[]{:S(2)}) collective-permute-start(bf16[64,128]{1,0:T(8,128)(2,1)S(1)} %get-tuple-element.20), channel_id=1, source_target_pairs={{0,3},{2,1},{1,11},{3,9},{4,7},{6,5},{5,15},{7,13},{9,10},{11,8},{... | collective-permute-start | bytes 49160 | tf_op jit(solution)/shard_map/ppermute | solution.py:342
  17.1 1.8 %collective-permute-start.4 = (bf16[1696,128]{1,0:T(8,128)(2,1)S(1)}, bf16[1696,128]{1,0:T(8,128)(2,1)S(1)}, u32[]{:S(2)}, u32[]{:S(2)}) collective-permute-start(bf16[1696,128]{1,0:T(8,128)(2,1)S(1)} %shard_map.57), channel_id=1, source_target_pairs={{0,1},{1,0},{2,3},{3,2},{4,5},{5,4},{6,7},{7,6},{8,9},{9,8},{10,11... | collective-permute-start | bytes 1302536 | tf_op jit(solution)/shard_map/ppermute | solution.py:351
  20.6 15.8 %collective-permute-start.5 = (bf16[384,256]{1,0:T(8,128)(2,1)S(1)}, bf16[384,256]{1,0:T(8,128)(2,1)S(1)}, u32[]{:S(2)}, u32[]{:S(2)}) collective-permute-start(bf16[384,256]{1,0:T(8,128)(2,1)S(1)} %shard_map.59), channel_id=1, source_target_pairs={{0,12},{1,5},{4,8},{5,1},{8,4},{9,13},{12,0},{13,9},{2,14},{3,7},{... | collective-permute-start | bytes 589832 | tf_op jit(solution)/shard_map/ppermute | solution.py:406
  24.7 4.6 %copy-start.2 = (bf16[256]{0:T(256)(128)(2,1)S(1)}, bf16[256]{0:T(256)(128)(2,1)}, u32[]{:S(2)}) copy-start(bf16[256]{0:T(256)(128)(2,1)} %param.9) | copy-start | bytes 1540
  24.7 11.7 %collective-permute-start.6 = (bf16[384,256]{1,0:T(8,128)(2,1)S(1)}, bf16[384,256]{1,0:T(8,128)(2,1)S(1)}, u32[]{:S(2)}, u32[]{:S(2)}) collective-permute-start(bf16[384,256]{1,0:T(8,128)(2,1)S(1)} %shard_map.61), channel_id=1, source_target_pairs={{0,4},{1,13},{4,0},{5,9},{8,12},{9,5},{12,8},{13,1},{2,6},{3,15},{... | collective-permute-start | bytes 589832 | tf_op jit(solution)/shard_map/ppermute | solution.py:407
  26.7 13.1 %collective-permute-start.7 = (bf16[384,256]{1,0:T(8,128)(2,1)S(1)}, bf16[384,256]{1,0:T(8,128)(2,1)S(1)}, u32[]{:S(2)}, u32[]{:S(2)}) collective-permute-start(bf16[384,256]{1,0:T(8,128)(2,1)S(1)} %get-tuple-element.24), channel_id=1, source_target_pairs={{0,8},{1,5},{4,12},{5,1},{8,0},{9,13},{12,4},{13,9},{2,10},{3,7},{... | collective-permute-start | bytes 589832 | tf_op jit(solution)/shard_map/ppermute | solution.py:408
  29.3 13.0 %collective-permute-start.8 = (bf16[384,256]{1,0:T(8,128)(2,1)S(1)}, bf16[384,256]{1,0:T(8,128)(2,1)S(1)}, u32[]{:S(2)}, u32[]{:S(2)}) collective-permute-start(bf16[384,256]{1,0:T(8,128)(2,1)S(1)} %get-tuple-element.25), channel_id=1, source_target_pairs={{0,4},{1,9},{4,0},{5,13},{8,12},{9,1},{12,8},{13,5},{2,6},{3,11},{... | collective-permute-start | bytes 589832 | tf_op jit(solution)/shard_map/ppermute | solution.py:409
  37.3 11.7 %collective-permute-start.10 = (bf16[384,256]{1,0:T(8,128)(2,1)S(1)}, bf16[384,256]{1,0:T(8,128)(2,1)S(1)}, u32[]{:S(2)}, u32[]{:S(2)}) collective-permute-start(bf16[384,256]{1,0:T(8,128)(2,1)S(1)} %shard_map.67), channel_id=1, source_target_pairs={{0,4},{1,13},{4,0},{5,9},{8,12},{9,5},{12,8},{13,1},{2,6},{3,15},{... | collective-permute-start | bytes 589832 | tf_op jit(solution)/shard_map/ppermute | solution.py:416
  38.3 11.1 %collective-permute-start.9 = (bf16[384,256]{1,0:T(8,128)(2,1)S(1)}, bf16[384,256]{1,0:T(8,128)(2,1)S(1)}, u32[]{:S(2)}, u32[]{:S(2)}) collective-permute-start(bf16[384,256]{1,0:T(8,128)(2,1)S(1)} %shard_map.66), channel_id=1, source_target_pairs={{0,12},{1,5},{4,8},{5,1},{8,4},{9,13},{12,0},{13,9},{2,14},{3,7},{... | collective-permute-start | bytes 589832 | tf_op jit(solution)/shard_map/ppermute | solution.py:416

commit v8 on v7

--- a/solution.py
+++ b/solution.py
@@ -411,9 +411,9 @@
         partial_sums(
             spread, [(mixed(core, frame(far_of, 1), frame(near_of, 1)), 0, 0, ((0, core),))], [1], (got,), after=after
         )[0]
-        for core, got, after in ((0, got_2, straight), (1, got_1, got_2))
+        for core, got, after in ((1, got_1, straight), (0, got_2, got_1))
     ]
-    got_5, got_6 = [lax.ppermute(sent, both, route(core, far_of)) for core, sent in enumerate(last)]
+    got_5, got_6 = [lax.ppermute(sent, both, route(1 - core, far_of)) for core, sent in enumerate(last)]
     home = []
     for f, adds, added in (
         (0, (got_1, got_2, got_3, got_4), ((0, 0), (1, 1), (2, None), (3, None))),

time: 50.3 us -> 50.3 us (level)
  no operation moved by 1% of the time
where the time goes in v8:
time: 50.3 us; the launch traced here: 50.1 us
  waiting for transfers between devices  23.9 us (48%)
  starting transfers between devices  12.6 us (25%)
  Pallas kernels  11.1 us (22%)
  local copies, waits for them, and re-layouts  2.33 us (5%)
    ppermute x1, waiting for transfers between devices, split_body(): got_2 = lax.ppermute(second[0], both, route(1, far_of))  7.07 us
    pallas_call x7, Pallas kernels, partial_sums(): pl.pallas_call(functools.partial(partial_kernel, jobs=jobs, n_adds=len(ad...  6.92 us
    ppermute x1, waiting for transfers between devices, split_body(): got_edge_b = lax.ppermute(edge_same, ('tm', 'tile', 'chan'), edge_b)  4.33 us
    ppermute x2, waiting for transfers between devices, split_body(): lax.ppermute(sent, both, route(1 - core, far_of))  4.29 us
    ppermute x1, waiting for transfers between devices, split_body(): got_edge_a = lax.ppermute(edge_following, ('tm', 'tile', 'chan'), edge_a)  3.23 us
    ppermute x1, starting transfers between devices, split_body(): got_a = lax.ppermute(following, both, route_a)  3.08 us
    ppermute x1, waiting for transfers between devices, split_body(): got_4 = lax.ppermute(straight[1], both, route(1, mid_of))  2.87 us
    ppermute x1, starting transfers between devices, split_body(): got_3 = lax.ppermute(straight[0], both, route(0, mid_of))  2.59 us
  transfers between devices with their start and end apart: 11, of which 8 were waited for; matrix products, arithmetic and copies ran while one was open for 3% of the time, Pallas kernels for 17%

profile of v8, /device:TPU:0, one launch (start us, length us, event | category | flops | bytes accessed | tf_op | source)
XLA Modules:
  0.0 50.1 jit_solution(8408573111821317104)
XLA Ops:
  0.0 1.0 %copy-done.1 = bf16[2,24,16,256]{3,2,1,0:T(8,128)(2,1)S(1)} copy-done((bf16[2,24,16,256]{3,2,1,0:T(8,128)(2,1)S(1)}, bf16[2,24,16,256]{3,2,1,0:T(8,128)(2,1)}, u32[]{:S(2)}) %copy-start.1) | copy-done | bytes 393240
  1.0 0.2 shard_map.55
  1.2 3.1 %collective-permute-start = (bf16[784,128]{1,0:T(8,128)(2,1)S(1)}, bf16[784,128]{1,0:T(8,128)(2,1)S(1)}, u32[]{:S(2)}, u32[]{:S(2)}) collective-permute-start(bf16[784,128]{1,0:T(8,128)(2,1)S(1)} %get-tuple-element.18), channel_id=1, source_target_pairs={{0,4},{1,12},{4,0},{5,8},{9,13},{8,5},{13,9},{12,1},{2,6},{3,14},{... | collective-permute-start | bytes 602120 | tf_op jit(solution)/shard_map/ppermute | solution.py:341
  4.3 2.1 %collective-permute-start.2 = (bf16[784,128]{1,0:T(8,128)(2,1)S(1)}, bf16[784,128]{1,0:T(8,128)(2,1)S(1)}, u32[]{:S(2)}, u32[]{:S(2)}) collective-permute-start(bf16[784,128]{1,0:T(8,128)(2,1)S(1)} %get-tuple-element.21.same_ref), channel_id=1, source_target_pairs={{0,1},{1,9},{4,5},{5,13},{9,8},{8,0},{13,12},{12,4},{2,3},{3,11},{... | collective-permute-start | bytes 602120 | tf_op jit(solution)/shard_map/ppermute | solution.py:340
  6.4 0.7 %reshape.19.gain_ref = bf16[1,256]{1,0:T(2,128)(2,1)S(1)} reshape(bf16[256]{0:T(256)(128)(2,1)} %param.6) | data formatting | bytes 1024 | tf_op jit(solution)/shard_map/reshape | solution.py:323
  7.1 0.7 %reshape.20.bias_ref = bf16[1,256]{1,0:T(2,128)(2,1)S(1)} reshape(bf16[256]{0:T(256)(128)(2,1)} %param.7) | data formatting | bytes 1024 | tf_op jit(solution)/shard_map/reshape | solution.py:323
  7.8 0.2 shard_map.56
  8.0 0.5 %collective-permute-start.1 = (bf16[64,128]{1,0:T(8,128)(2,1)S(1)}, bf16[64,128]{1,0:T(8,128)(2,1)S(1)}, u32[]{:S(2)}, u32[]{:S(2)}) collective-permute-start(bf16[64,128]{1,0:T(8,128)(2,1)S(1)} %get-tuple-element.19), channel_id=1, source_target_pairs={{0,6},{2,4},{1,14},{3,12},{4,2},{6,0},{5,10},{7,8},{9,15},{11,13},... | collective-permute-start | bytes 49160 | tf_op jit(solution)/shard_map/ppermute | solution.py:343
  8.5 1.0 %collective-permute-start.3 = (bf16[64,128]{1,0:T(8,128)(2,1)S(1)}, bf16[64,128]{1,0:T(8,128)(2,1)S(1)}, u32[]{:S(2)}, u32[]{:S(2)}) collective-permute-start(bf16[64,128]{1,0:T(8,128)(2,1)S(1)} %get-tuple-element.20), channel_id=1, source_target_pairs={{0,3},{2,1},{1,11},{3,9},{4,7},{6,5},{5,15},{7,13},{9,10},{11,8},{... | collective-permute-start | bytes 49160 | tf_op jit(solution)/shard_map/ppermute | solution.py:342
  9.5 3.2 %collective-permute-done.1.refs_1_.edge_a_ref = bf16[64,128]{1,0:T(8,128)(2,1)S(1)} collective-permute-done((bf16[64,128]{1,0:T(8,128)(2,1)S(1)}, bf16[64,128]{1,0:T(8,128)(2,1)S(1)}, u32[]{:S(2)}, u32[]{:S(2)}) %collective-permute-start.1) | collective-permute-done | bytes 16416 | tf_op jit(solution)/shard_map/ppermute | solution.py:343
  12.8 4.3 %collective-permute-done.3.refs_3_.edge_b_ref = bf16[64,128]{1,0:T(8,128)(2,1)S(1)} collective-permute-done((bf16[64,128]{1,0:T(8,128)(2,1)S(1)}, bf16[64,128]{1,0:T(8,128)(2,1)S(1)}, u32[]{:S(2)}, u32[]{:S(2)}) %collective-permute-start.3) | collective-permute-done | bytes 16416 | tf_op jit(solution)/shard_map/ppermute | solution.py:342
  17.2 1.8 %collective-permute-done.4.swapped_ref = bf16[1696,128]{1,0:T(8,128)(2,1)S(1)} collective-permute-done((bf16[1696,128]{1,0:T(8,128)(2,1)S(1)}, bf16[1696,128]{1,0:T(8,128)(2,1)S(1)}, u32[]{:S(2)}, u32[]{:S(2)}) %collective-permute-start.4) | collective-permute-done | bytes 434208 | tf_op jit(solution)/shard_map/ppermute | solution.py:351
  19.0 0.7 %shard_map.58.spread_ref = bf16[3,4,26,16,128]{4,3,2,1,0:T(8,128)(2,1)S(1)} custom-call(bf16[784,128]{1,0:T(8,128)(2,1)S(1)} %get-tuple-element.21.same_ref, bf16[784,128]{1,0:T(8,128)(2,1)S(1)} %collective-permute-done.refs_0_.a_ref, bf16[64,128]{1,0:T(8,128)(2,1)S(1)} %collective-permute-done.1.refs_1_.edge_a_ref, ...), custom_call_target="tpu_custom_call" | custom-call | tf_op jit(solution)/shard_map/pallas_call | solution.py:355
  19.7 0.9 %shard_map.59 = bf16[384,256]{1,0:T(8,128)(2,1)S(1)} custom-call(bf16[3,4,26,16,128]{4,3,2,1,0:T(8,128)(2,1)S(1)} %shard_map.58.spread_ref, bf16[3456,256]{1,0:T(8,128)(2,1)S(1)} %bitcast.3), custom_call_target="tpu_custom_call" | custom-call | flops 4294967296 | bytes 1 | tf_op jit(solution)/shard_map/pallas_call | solution.py:371
  20.6 1.6 %collective-permute-start.5 = (bf16[384,256]{1,0:T(8,128)(2,1)S(1)}, bf16[384,256]{1,0:T(8,128)(2,1)S(1)}, u32[]{:S(2)}, u32[]{:S(2)}) collective-permute-start(bf16[384,256]{1,0:T(8,128)(2,1)S(1)} %shard_map.59), channel_id=1, source_target_pairs={{0,12},{1,5},{4,8},{5,1},{8,4},{9,13},{12,0},{13,9},{2,14},{3,7},{... | collective-permute-start | bytes 589832 | tf_op jit(solution)/shard_map/ppermute | solution.py:406
  22.3 1.5 %shard_map.60.spread_ref = bf16[3,10,26,16,128]{4,3,2,1,0:T(8,128)(2,1)S(1)} custom-call(bf16[784,128]{1,0:T(8,128)(2,1)S(1)} %get-tuple-element.21.same_ref, bf16[784,128]{1,0:T(8,128)(2,1)S(1)} %collective-permute-done.refs_0_.a_ref, bf16[64,128]{1,0:T(8,128)(2,1)S(1)} %collective-permute-done.1.refs_1_.edge_a_ref, ...), custom_call_target="tpu_custom_call" | custom-call | tf_op jit(solution)/shard_map/pallas_call | solution.py:355
  23.8 0.9 %shard_map.61 = bf16[384,256]{1,0:T(8,128)(2,1)S(1)} custom-call(bf16[3,10,26,16,128]{4,3,2,1,0:T(8,128)(2,1)S(1)} %shard_map.60.spread_ref, bf16[3456,256]{1,0:T(8,128)(2,1)S(1)} %bitcast.4), custom_call_target="tpu_custom_call" | custom-call | flops 4294967296 | bytes 1 | tf_op jit(solution)/shard_map/pallas_call | solution.py:371
  24.7 0.4 collective-permute-start.6
  25.1 1.6 %shard_map.62 = (bf16[384,256]{1,0:T(8,128)(2,1)S(1)}, bf16[384,256]{1,0:T(8,128)(2,1)S(1)}) custom-call(bf16[3,10,26,16,128]{4,3,2,1,0:T(8,128)(2,1)S(1)} %shard_map.60.spread_ref, bf16[3456,256]{1,0:T(8,128)(2,1)S(1)} %bitcast.5), custom_call_target="tpu_custom_call" | custom-call | flops 4294967296 | bytes 1 | tf_op jit(solution)/shard_map/pallas_call | solution.py:371
  26.7 2.6 %collective-permute-start.7 = (bf16[384,256]{1,0:T(8,128)(2,1)S(1)}, bf16[384,256]{1,0:T(8,128)(2,1)S(1)}, u32[]{:S(2)}, u32[]{:S(2)}) collective-permute-start(bf16[384,256]{1,0:T(8,128)(2,1)S(1)} %get-tuple-element.24), channel_id=1, source_target_pairs={{0,8},{1,5},{4,12},{5,1},{8,0},{9,13},{12,4},{13,9},{2,10},{3,7},{... | collective-permute-start | bytes 589832 | tf_op jit(solution)/shard_map/ppermute | solution.py:408
  29.3 7.1 %collective-permute-done.6.rest_1_.rest_0_ = bf16[384,256]{1,0:T(8,128)(2,1)S(1)} collective-permute-done((bf16[384,256]{1,0:T(8,128)(2,1)S(1)}, bf16[384,256]{1,0:T(8,128)(2,1)S(1)}, u32[]{:S(2)}, u32[]{:S(2)}) %collective-permute-start.6) | collective-permute-done | bytes 196640 | tf_op jit(solution)/shard_map/ppermute | solution.py:407
  36.4 0.9 %shard_map.67 = bf16[384,256]{1,0:T(8,128)(2,1)S(1)} custom-call(bf16[3,10,26,16,128]{4,3,2,1,0:T(8,128)(2,1)S(1)} %shard_map.60.spread_ref, bf16[3456,256]{1,0:T(8,128)(2,1)S(1)} %bitcast.6, bf16[384,256]{1,0:T(8,128)(2,1)S(1)} %collective-permute-done.6.rest_1_.rest_0_), custom_call_target="tpu_custom_call" | custom-call | flops 1 | bytes 1 | tf_op jit(solution)/shard_map/pallas_call | solution.py:371
  37.3 1.1 %collective-permute-start.10 = (bf16[384,256]{1,0:T(8,128)(2,1)S(1)}, bf16[384,256]{1,0:T(8,128)(2,1)S(1)}, u32[]{:S(2)}, u32[]{:S(2)}) collective-permute-start(bf16[384,256]{1,0:T(8,128)(2,1)S(1)} %shard_map.67), channel_id=1, source_target_pairs={{0,12},{1,5},{4,8},{5,1},{8,4},{9,13},{12,0},{13,9},{2,14},{3,7},{... | collective-permute-start | bytes 589832 | tf_op jit(solution)/shard_map/ppermute | solution.py:416
  38.4 0.9 %shard_map.66 = bf16[384,256]{1,0:T(8,128)(2,1)S(1)} custom-call(bf16[3,10,26,16,128]{4,3,2,1,0:T(8,128)(2,1)S(1)} %shard_map.60.spread_ref, bf16[3456,256]{1,0:T(8,128)(2,1)S(1)} %bitcast.7, bf16[384,256]{1,0:T(8,128)(2,1)S(1)} %collective-permute-done.5.rest_0_), custom_call_target="tpu_custom_call" | custom-call | flops 1 | bytes 1 | tf_op jit(solution)/shard_map/pallas_call | solution.py:371
  39.4 0.4 collective-permute-done.7.rest_2_
  39.8 2.9 %collective-permute-done.8.rest_3_ = bf16[384,256]{1,0:T(8,128)(2,1)S(1)} collective-permute-done((bf16[384,256]{1,0:T(8,128)(2,1)S(1)}, bf16[384,256]{1,0:T(8,128)(2,1)S(1)}, u32[]{:S(2)}, u32[]{:S(2)}) %collective-permute-start.8) | collective-permute-done | bytes 196640 | tf_op jit(solution)/shard_map/ppermute | solution.py:409
  42.6 0.9 %shard_map.63.first_ref = f32[384,256]{1,0:T(8,128)S(1)} custom-call(bf16[3,10,26,16,128]{4,3,2,1,0:T(8,128)(2,1)S(1)} %shard_map.60.spread_ref, bf16[3456,256]{1,0:T(8,128)(2,1)S(1)} %bitcast.8, bf16[384,256]{1,0:T(8,128)(2,1)S(1)} %collective-permute-done.5.rest_0_, bf16[384,256]{1,0:T(8,128)(2,1)S(1)} %collective-permute-done.6.rest_1_.rest_0_, ...), custom_call_target="tpu_custom_call" | custom-call | flops 34359738368 | bytes 1 | tf_op jit(solution)/shard_map/pallas_call | solution.py:371
  43.5 0.9 %shard_map.65.second_ref = f32[384,256]{1,0:T(8,128)S(1)} custom-call(bf16[3,10,26,16,128]{4,3,2,1,0:T(8,128)(2,1)S(1)} %shard_map.60.spread_ref, bf16[3456,256]{1,0:T(8,128)(2,1)S(1)} %bitcast.9, bf16[1,256]{1,0:T(2,128)(2,1)S(1)} %reshape.22.rest_4_.rest_0_), custom_call_target="tpu_custom_call" | custom-call | flops 34359738368 | bytes 1 | tf_op jit(solution)/shard_map/pallas_call | solution.py:371
  44.4 0.7 %shard_map.64.whole_ref = bf16[768,256]{1,0:T(8,128)(2,1)} custom-call(f32[384,256]{1,0:T(8,128)S(1)} %shard_map.63.first_ref), custom_call_target="tpu_custom_call" | custom-call | tf_op jit(solution)/shard_map/pallas_call | solution.py:426
  45.1 2.1 %collective-permute-done.10.other_ref = bf16[384,256]{1,0:T(8,128)(2,1)S(1)} collective-permute-done((bf16[384,256]{1,0:T(8,128)(2,1)S(1)}, bf16[384,256]{1,0:T(8,128)(2,1)S(1)}, u32[]{:S(2)}, u32[]{:S(2)}) %collective-permute-start.10) | collective-permute-done | bytes 196640 | tf_op jit(solution)/shard_map/ppermute | solution.py:416
  47.2 2.2 %collective-permute-done.9.one_ref = bf16[384,256]{1,0:T(8,128)(2,1)S(1)} collective-permute-done((bf16[384,256]{1,0:T(8,128)(2,1)S(1)}, bf16[384,256]{1,0:T(8,128)(2,1)S(1)}, u32[]{:S(2)}, u32[]{:S(2)}) %collective-permute-start.9) | collective-permute-done | bytes 196640 | tf_op jit(solution)/shard_map/ppermute | solution.py:416
  49.4 0.7 %shard_map.68 = bf16[768,256]{1,0:T(8,128)(2,1)} custom-call(bf16[768,256]{1,0:T(8,128)(2,1)} %shard_map.64.whole_ref, f32[384,256]{1,0:T(8,128)S(1)} %shard_map.65.second_ref, bf16[384,256]{1,0:T(8,128)(2,1)S(1)} %collective-permute-done.9.one_ref, bf16[384,256]{1,0:T(8,128)(2,1)S(1)} %collective-permute-done.10.other_ref), custom_call_target="tpu_custom_call", output_to_operand_aliasing={{}: (0, {})} | custom-call | tf_op jit(solution)/shard_map/pallas_call | solution.py:434
  (13 shorter events, 0.2 us)
Async XLA Ops:
  0.0 1.0 %copy-start.1 = (bf16[2,24,16,256]{3,2,1,0:T(8,128)(2,1)S(1)}, bf16[2,24,16,256]{3,2,1,0:T(8,128)(2,1)}, u32[]{:S(2)}) copy-start(bf16[2,24,16,256]{3,2,1,0:T(8,128)(2,1)} %param.5) | copy-start | bytes 1179652
  1.2 15.9 %collective-permute-start = (bf16[784,128]{1,0:T(8,128)(2,1)S(1)}, bf16[784,128]{1,0:T(8,128)(2,1)S(1)}, u32[]{:S(2)}, u32[]{:S(2)}) collective-permute-start(bf16[784,128]{1,0:T(8,128)(2,1)S(1)} %get-tuple-element.18), channel_id=1, source_target_pairs={{0,4},{1,12},{4,0},{5,8},{9,13},{8,5},{13,9},{12,1},{2,6},{3,14},{... | collective-permute-start | bytes 602120 | tf_op jit(solution)/shard_map/ppermute | solution.py:341
  4.3 12.8 %collective-permute-start.2 = (bf16[784,128]{1,0:T(8,128)(2,1)S(1)}, bf16[784,128]{1,0:T(8,128)(2,1)S(1)}, u32[]{:S(2)}, u32[]{:S(2)}) collective-permute-start(bf16[784,128]{1,0:T(8,128)(2,1)S(1)} %get-tuple-element.21.same_ref), channel_id=1, source_target_pairs={{0,1},{1,9},{4,5},{5,13},{9,8},{8,0},{13,12},{12,4},{2,3},{3,11},{... | collective-permute-start | bytes 602120 | tf_op jit(solution)/shard_map/ppermute | solution.py:340
  7.8 12.0 %copy-start = (bf16[27,128,256]{2,1,0:T(8,128)(2,1)S(1)}, bf16[27,128,256]{2,1,0:T(8,128)(2,1)}, u32[]{:S(2)}) copy-start(bf16[27,128,256]{2,1,0:T(8,128)(2,1)} %param.8) | copy-start | bytes 5308420
  8.0 4.8 %collective-permute-start.1 = (bf16[64,128]{1,0:T(8,128)(2,1)S(1)}, bf16[64,128]{1,0:T(8,128)(2,1)S(1)}, u32[]{:S(2)}, u32[]{:S(2)}) collective-permute-start(bf16[64,128]{1,0:T(8,128)(2,1)S(1)} %get-tuple-element.19), channel_id=1, source_target_pairs={{0,6},{2,4},{1,14},{3,12},{4,2},{6,0},{5,10},{7,8},{9,15},{11,13},... | collective-permute-start | bytes 49160 | tf_op jit(solution)/shard_map/ppermute | solution.py:343
  8.5 8.6 %collective-permute-start.3 = (bf16[64,128]{1,0:T(8,128)(2,1)S(1)}, bf16[64,128]{1,0:T(8,128)(2,1)S(1)}, u32[]{:S(2)}, u32[]{:S(2)}) collective-permute-start(bf16[64,128]{1,0:T(8,128)(2,1)S(1)} %get-tuple-element.20), channel_id=1, source_target_pairs={{0,3},{2,1},{1,11},{3,9},{4,7},{6,5},{5,15},{7,13},{9,10},{11,8},{... | collective-permute-start | bytes 49160 | tf_op jit(solution)/shard_map/ppermute | solution.py:342
  17.1 1.8 %collective-permute-start.4 = (bf16[1696,128]{1,0:T(8,128)(2,1)S(1)}, bf16[1696,128]{1,0:T(8,128)(2,1)S(1)}, u32[]{:S(2)}, u32[]{:S(2)}) collective-permute-start(bf16[1696,128]{1,0:T(8,128)(2,1)S(1)} %shard_map.57), channel_id=1, source_target_pairs={{0,1},{1,0},{2,3},{3,2},{4,5},{5,4},{6,7},{7,6},{8,9},{9,8},{10,11... | collective-permute-start | bytes 1302536 | tf_op jit(solution)/shard_map/ppermute | solution.py:351
  20.6 8.7 %collective-permute-start.5 = (bf16[384,256]{1,0:T(8,128)(2,1)S(1)}, bf16[384,256]{1,0:T(8,128)(2,1)S(1)}, u32[]{:S(2)}, u32[]{:S(2)}) collective-permute-start(bf16[384,256]{1,0:T(8,128)(2,1)S(1)} %shard_map.59), channel_id=1, source_target_pairs={{0,12},{1,5},{4,8},{5,1},{8,4},{9,13},{12,0},{13,9},{2,14},{3,7},{... | collective-permute-start | bytes 589832 | tf_op jit(solution)/shard_map/ppermute | solution.py:406
  24.7 4.6 %copy-start.2 = (bf16[256]{0:T(256)(128)(2,1)S(1)}, bf16[256]{0:T(256)(128)(2,1)}, u32[]{:S(2)}) copy-start(bf16[256]{0:T(256)(128)(2,1)} %param.9) | copy-start | bytes 1540
  24.7 11.7 %collective-permute-start.6 = (bf16[384,256]{1,0:T(8,128)(2,1)S(1)}, bf16[384,256]{1,0:T(8,128)(2,1)S(1)}, u32[]{:S(2)}, u32[]{:S(2)}) collective-permute-start(bf16[384,256]{1,0:T(8,128)(2,1)S(1)} %shard_map.61), channel_id=1, source_target_pairs={{0,4},{1,13},{4,0},{5,9},{8,12},{9,5},{12,8},{13,1},{2,6},{3,15},{... | collective-permute-start | bytes 589832 | tf_op jit(solution)/shard_map/ppermute | solution.py:407
  26.7 13.1 %collective-permute-start.7 = (bf16[384,256]{1,0:T(8,128)(2,1)S(1)}, bf16[384,256]{1,0:T(8,128)(2,1)S(1)}, u32[]{:S(2)}, u32[]{:S(2)}) collective-permute-start(bf16[384,256]{1,0:T(8,128)(2,1)S(1)} %get-tuple-element.24), channel_id=1, source_target_pairs={{0,8},{1,5},{4,12},{5,1},{8,0},{9,13},{12,4},{13,9},{2,10},{3,7},{... | collective-permute-start | bytes 589832 | tf_op jit(solution)/shard_map/ppermute | solution.py:408
  29.3 13.4 %collective-permute-start.8 = (bf16[384,256]{1,0:T(8,128)(2,1)S(1)}, bf16[384,256]{1,0:T(8,128)(2,1)S(1)}, u32[]{:S(2)}, u32[]{:S(2)}) collective-permute-start(bf16[384,256]{1,0:T(8,128)(2,1)S(1)} %get-tuple-element.25), channel_id=1, source_target_pairs={{0,4},{1,9},{4,0},{5,13},{8,12},{9,1},{12,8},{13,5},{2,6},{3,11},{... | collective-permute-start | bytes 589832 | tf_op jit(solution)/shard_map/ppermute | solution.py:409
  37.3 9.9 %collective-permute-start.10 = (bf16[384,256]{1,0:T(8,128)(2,1)S(1)}, bf16[384,256]{1,0:T(8,128)(2,1)S(1)}, u32[]{:S(2)}, u32[]{:S(2)}) collective-permute-start(bf16[384,256]{1,0:T(8,128)(2,1)S(1)} %shard_map.67), channel_id=1, source_target_pairs={{0,12},{1,5},{4,8},{5,1},{8,4},{9,13},{12,0},{13,9},{2,14},{3,7},{... | collective-permute-start | bytes 589832 | tf_op jit(solution)/shard_map/ppermute | solution.py:416
  39.3 10.1 %collective-permute-start.9 = (bf16[384,256]{1,0:T(8,128)(2,1)S(1)}, bf16[384,256]{1,0:T(8,128)(2,1)S(1)}, u32[]{:S(2)}, u32[]{:S(2)}) collective-permute-start(bf16[384,256]{1,0:T(8,128)(2,1)S(1)} %shard_map.66), channel_id=1, source_target_pairs={{0,4},{1,13},{4,0},{5,9},{8,12},{9,5},{12,8},{13,1},{2,6},{3,15},{... | collective-permute-start | bytes 589832 | tf_op jit(solution)/shard_map/ppermute | solution.py:416

commit v9 on v7

--- a/solution.py
+++ b/solution.py
@@ -211,7 +211,8 @@
 
     def normed(raw):
         value = (raw.astype(jnp.float32) - total) * scale + shift
-        return value / (1.0 + jnp.exp(-value))
+        half = 0.5 * value
+        return half + half * jnp.tanh(half)
 
     n_all = out_ref.shape[1]
     zero_row = jnp.zeros((cols, LANES), jnp.bfloat16)
@@ -401,12 +402,12 @@
     spread = spread_out(2 + n_blocks * frames, False, lead[0])
     second = mixed(1, frame(far_of, 0), frame(mid_of, 1))
     second = partial_sums(spread, [(second, 0, 0, ())], [1], after=lead, cost=1 << 32)
-    jobs = [(mixed(core, frame(mid_of, 0), frame(near_of, 0)), core, 0, ()) for core in range(2)]
+    jobs = [(mixed(core, frame(mid_of, 0), frame(near_of, 0)), 1 - core, 0, ()) for core in range(2)]
     straight = partial_sums(spread, jobs, [1, 1], after=second, cost=1 << 32)
     got_1 = lax.ppermute(lead[0], both, route(0, far_of))
     got_2 = lax.ppermute(second[0], both, route(1, far_of))
-    got_3 = lax.ppermute(straight[0], both, route(0, mid_of))
-    got_4 = lax.ppermute(straight[1], both, route(1, mid_of))
+    got_3 = lax.ppermute(straight[0], both, route(1, mid_of))
+    got_4 = lax.ppermute(straight[1], both, route(0, mid_of))
     last = [
         partial_sums(
             spread, [(mixed(core, frame(far_of, 1), frame(near_of, 1)), 0, 0, ((0, core),))], [1], (got,), after=after

time: 50.3 us -> 50.3 us (level)
    ppermute x2, waiting for transfers between devices: 2.84 us -> 6.55 us  [the longest x1 6.55 us: split_body(): got_3 = lax.ppermute(straight[0], both, route(1, mid_of))]
    ppermute x2, waiting for transfers between devices: 4.68 us -> 2.7 us  [split_body(): lax.ppermute(sent, both, route(core, far_of))]
    ppermute x1, waiting for transfers between devices: 7.08 us -> 5.64 us  [split_body(): got_2 = lax.ppermute(second[0], both, route(1, far_of))]
  transfers between devices with their start and end apart: 11 -> 11, of which waited for: 8 -> 7; matrix products, arithmetic and copies ran while one was open for 3% -> 3% of each run, Pallas kernels for 17% -> 17%
where the time goes in v9:
time: 50.3 us; the launch traced here: 50.1 us
  waiting for transfers between devices  24.2 us (48%)
  starting transfers between devices  12.4 us (25%)
  Pallas kernels  11.1 us (22%)
  local copies, waits for them, and re-layouts  2.33 us (5%)
    pallas_call x7, Pallas kernels, partial_sums(): pl.pallas_call(functools.partial(partial_kernel, jobs=jobs, n_adds=len(ad...  6.91 us
    ppermute x1, waiting for transfers between devices, split_body(): got_3 = lax.ppermute(straight[0], both, route(1, mid_of))  6.55 us
    ppermute x1, waiting for transfers between devices, split_body(): got_2 = lax.ppermute(second[0], both, route(1, far_of))  5.64 us
    ppermute x1, waiting for transfers between devices, split_body(): got_edge_b = lax.ppermute(edge_same, ('tm', 'tile', 'chan'), edge_b)  4.33 us
    ppermute x1, waiting for transfers between devices, split_body(): got_edge_a = lax.ppermute(edge_following, ('tm', 'tile', 'chan'), edge_a)  3.23 us
    ppermute x1, starting transfers between devices, split_body(): got_a = lax.ppermute(following, both, route_a)  3.08 us
    ppermute x2, waiting for transfers between devices, split_body(): lax.ppermute(sent, both, route(core, far_of))  2.7 us
    pallas_call x2, Pallas kernels, spread_out(): pl.pallas_call(functools.partial(spread_kernel, frames=frames, rows=rows,...  2.23 us
  transfers between devices with their start and end apart: 11, of which 7 were waited for; matrix products, arithmetic and copies ran while one was open for 3% of the time, Pallas kernels for 17%

profile of v9, /device:TPU:0, one launch (start us, length us, event | category | flops | bytes accessed | tf_op | source)
XLA Modules:
  0.0 50.1 jit_solution(8862207040042488449)
XLA Ops:
  0.0 1.0 %copy-done.1 = bf16[2,24,16,256]{3,2,1,0:T(8,128)(2,1)S(1)} copy-done((bf16[2,24,16,256]{3,2,1,0:T(8,128)(2,1)S(1)}, bf16[2,24,16,256]{3,2,1,0:T(8,128)(2,1)}, u32[]{:S(2)}) %copy-start.1) | copy-done | bytes 393240
  1.0 0.2 shard_map.55
  1.2 3.1 %collective-permute-start = (bf16[784,128]{1,0:T(8,128)(2,1)S(1)}, bf16[784,128]{1,0:T(8,128)(2,1)S(1)}, u32[]{:S(2)}, u32[]{:S(2)}) collective-permute-start(bf16[784,128]{1,0:T(8,128)(2,1)S(1)} %get-tuple-element.18), channel_id=1, source_target_pairs={{0,4},{1,12},{4,0},{5,8},{9,13},{8,5},{13,9},{12,1},{2,6},{3,14},{... | collective-permute-start | bytes 602120 | tf_op jit(solution)/shard_map/ppermute | solution.py:342
  4.3 2.1 %collective-permute-start.2 = (bf16[784,128]{1,0:T(8,128)(2,1)S(1)}, bf16[784,128]{1,0:T(8,128)(2,1)S(1)}, u32[]{:S(2)}, u32[]{:S(2)}) collective-permute-start(bf16[784,128]{1,0:T(8,128)(2,1)S(1)} %get-tuple-element.21.same_ref), channel_id=1, source_target_pairs={{0,1},{1,9},{4,5},{5,13},{9,8},{8,0},{13,12},{12,4},{2,3},{3,11},{... | collective-permute-start | bytes 602120 | tf_op jit(solution)/shard_map/ppermute | solution.py:341
  6.4 0.7 %reshape.19.gain_ref = bf16[1,256]{1,0:T(2,128)(2,1)S(1)} reshape(bf16[256]{0:T(256)(128)(2,1)} %param.6) | data formatting | bytes 1024 | tf_op jit(solution)/shard_map/reshape | solution.py:324
  7.1 0.7 %reshape.20.bias_ref = bf16[1,256]{1,0:T(2,128)(2,1)S(1)} reshape(bf16[256]{0:T(256)(128)(2,1)} %param.7) | data formatting | bytes 1024 | tf_op jit(solution)/shard_map/reshape | solution.py:324
  7.8 0.2 shard_map.56
  8.0 0.5 %collective-permute-start.1 = (bf16[64,128]{1,0:T(8,128)(2,1)S(1)}, bf16[64,128]{1,0:T(8,128)(2,1)S(1)}, u32[]{:S(2)}, u32[]{:S(2)}) collective-permute-start(bf16[64,128]{1,0:T(8,128)(2,1)S(1)} %get-tuple-element.19), channel_id=1, source_target_pairs={{0,6},{2,4},{1,14},{3,12},{4,2},{6,0},{5,10},{7,8},{9,15},{11,13},... | collective-permute-start | bytes 49160 | tf_op jit(solution)/shard_map/ppermute | solution.py:344
  8.5 1.0 %collective-permute-start.3 = (bf16[64,128]{1,0:T(8,128)(2,1)S(1)}, bf16[64,128]{1,0:T(8,128)(2,1)S(1)}, u32[]{:S(2)}, u32[]{:S(2)}) collective-permute-start(bf16[64,128]{1,0:T(8,128)(2,1)S(1)} %get-tuple-element.20), channel_id=1, source_target_pairs={{0,3},{2,1},{1,11},{3,9},{4,7},{6,5},{5,15},{7,13},{9,10},{11,8},{... | collective-permute-start | bytes 49160 | tf_op jit(solution)/shard_map/ppermute | solution.py:343
  9.5 3.2 %collective-permute-done.1.refs_1_.edge_a_ref = bf16[64,128]{1,0:T(8,128)(2,1)S(1)} collective-permute-done((bf16[64,128]{1,0:T(8,128)(2,1)S(1)}, bf16[64,128]{1,0:T(8,128)(2,1)S(1)}, u32[]{:S(2)}, u32[]{:S(2)}) %collective-permute-start.1) | collective-permute-done | bytes 16416 | tf_op jit(solution)/shard_map/ppermute | solution.py:344
  12.8 4.3 %collective-permute-done.3.refs_3_.edge_b_ref = bf16[64,128]{1,0:T(8,128)(2,1)S(1)} collective-permute-done((bf16[64,128]{1,0:T(8,128)(2,1)S(1)}, bf16[64,128]{1,0:T(8,128)(2,1)S(1)}, u32[]{:S(2)}, u32[]{:S(2)}) %collective-permute-start.3) | collective-permute-done | bytes 16416 | tf_op jit(solution)/shard_map/ppermute | solution.py:343
  17.2 1.8 %collective-permute-done.4.swapped_ref = bf16[1696,128]{1,0:T(8,128)(2,1)S(1)} collective-permute-done((bf16[1696,128]{1,0:T(8,128)(2,1)S(1)}, bf16[1696,128]{1,0:T(8,128)(2,1)S(1)}, u32[]{:S(2)}, u32[]{:S(2)}) %collective-permute-start.4) | collective-permute-done | bytes 434208 | tf_op jit(solution)/shard_map/ppermute | solution.py:352
  19.0 0.7 %shard_map.58.spread_ref = bf16[3,4,26,16,128]{4,3,2,1,0:T(8,128)(2,1)S(1)} custom-call(bf16[784,128]{1,0:T(8,128)(2,1)S(1)} %get-tuple-element.21.same_ref, bf16[784,128]{1,0:T(8,128)(2,1)S(1)} %collective-permute-done.refs_0_.a_ref, bf16[64,128]{1,0:T(8,128)(2,1)S(1)} %collective-permute-done.1.refs_1_.edge_a_ref, ...), custom_call_target="tpu_custom_call" | custom-call | tf_op jit(solution)/shard_map/pallas_call | solution.py:356
  19.7 0.9 %shard_map.59 = bf16[384,256]{1,0:T(8,128)(2,1)S(1)} custom-call(bf16[3,4,26,16,128]{4,3,2,1,0:T(8,128)(2,1)S(1)} %shard_map.58.spread_ref, bf16[3456,256]{1,0:T(8,128)(2,1)S(1)} %bitcast.3), custom_call_target="tpu_custom_call" | custom-call | flops 4294967296 | bytes 1 | tf_op jit(solution)/shard_map/pallas_call | solution.py:372
  20.6 1.6 %collective-permute-start.5 = (bf16[384,256]{1,0:T(8,128)(2,1)S(1)}, bf16[384,256]{1,0:T(8,128)(2,1)S(1)}, u32[]{:S(2)}, u32[]{:S(2)}) collective-permute-start(bf16[384,256]{1,0:T(8,128)(2,1)S(1)} %shard_map.59), channel_id=1, source_target_pairs={{0,12},{1,5},{4,8},{5,1},{8,4},{9,13},{12,0},{13,9},{2,14},{3,7},{... | collective-permute-start | bytes 589832 | tf_op jit(solution)/shard_map/ppermute | solution.py:407
  22.3 1.5 %shard_map.60.spread_ref = bf16[3,10,26,16,128]{4,3,2,1,0:T(8,128)(2,1)S(1)} custom-call(bf16[784,128]{1,0:T(8,128)(2,1)S(1)} %get-tuple-element.21.same_ref, bf16[784,128]{1,0:T(8,128)(2,1)S(1)} %collective-permute-done.refs_0_.a_ref, bf16[64,128]{1,0:T(8,128)(2,1)S(1)} %collective-permute-done.1.refs_1_.edge_a_ref, ...), custom_call_target="tpu_custom_call" | custom-call | tf_op jit(solution)/shard_map/pallas_call | solution.py:356
  23.8 0.9 %shard_map.61 = bf16[384,256]{1,0:T(8,128)(2,1)S(1)} custom-call(bf16[3,10,26,16,128]{4,3,2,1,0:T(8,128)(2,1)S(1)} %shard_map.60.spread_ref, bf16[3456,256]{1,0:T(8,128)(2,1)S(1)} %bitcast.4), custom_call_target="tpu_custom_call" | custom-call | flops 4294967296 | bytes 1 | tf_op jit(solution)/shard_map/pallas_call | solution.py:372
  24.7 0.4 collective-permute-start.6
  25.1 1.6 %shard_map.62 = (bf16[384,256]{1,0:T(8,128)(2,1)S(1)}, bf16[384,256]{1,0:T(8,128)(2,1)S(1)}) custom-call(bf16[3,10,26,16,128]{4,3,2,1,0:T(8,128)(2,1)S(1)} %shard_map.60.spread_ref, bf16[3456,256]{1,0:T(8,128)(2,1)S(1)} %bitcast.5), custom_call_target="tpu_custom_call" | custom-call | flops 4294967296 | bytes 1 | tf_op jit(solution)/shard_map/pallas_call | solution.py:372
  26.6 1.8 %collective-permute-start.7 = (bf16[384,256]{1,0:T(8,128)(2,1)S(1)}, bf16[384,256]{1,0:T(8,128)(2,1)S(1)}, u32[]{:S(2)}, u32[]{:S(2)}) collective-permute-start(bf16[384,256]{1,0:T(8,128)(2,1)S(1)} %get-tuple-element.24), channel_id=1, source_target_pairs={{0,4},{1,9},{4,0},{5,13},{8,12},{9,1},{12,8},{13,5},{2,6},{3,11},{... | collective-permute-start | bytes 589832 | tf_op jit(solution)/shard_map/ppermute | solution.py:409
  28.5 0.8 %collective-permute-start.8 = (bf16[384,256]{1,0:T(8,128)(2,1)S(1)}, bf16[384,256]{1,0:T(8,128)(2,1)S(1)}, u32[]{:S(2)}, u32[]{:S(2)}) collective-permute-start(bf16[384,256]{1,0:T(8,128)(2,1)S(1)} %get-tuple-element.25), channel_id=1, source_target_pairs={{0,8},{1,5},{4,12},{5,1},{8,0},{9,13},{12,4},{13,9},{2,10},{3,7},{... | collective-permute-start | bytes 589832 | tf_op jit(solution)/shard_map/ppermute | solution.py:410
  29.3 5.6 %collective-permute-done.6.rest_1_.rest_0_ = bf16[384,256]{1,0:T(8,128)(2,1)S(1)} collective-permute-done((bf16[384,256]{1,0:T(8,128)(2,1)S(1)}, bf16[384,256]{1,0:T(8,128)(2,1)S(1)}, u32[]{:S(2)}, u32[]{:S(2)}) %collective-permute-start.6) | collective-permute-done | bytes 196640 | tf_op jit(solution)/shard_map/ppermute | solution.py:408
  34.9 0.9 %shard_map.67 = bf16[384,256]{1,0:T(8,128)(2,1)S(1)} custom-call(bf16[3,10,26,16,128]{4,3,2,1,0:T(8,128)(2,1)S(1)} %shard_map.60.spread_ref, bf16[3456,256]{1,0:T(8,128)(2,1)S(1)} %bitcast.6, bf16[384,256]{1,0:T(8,128)(2,1)S(1)} %collective-permute-done.5.rest_0_), custom_call_target="tpu_custom_call" | custom-call | flops 1 | bytes 1 | tf_op jit(solution)/shard_map/pallas_call | solution.py:372
  35.9 0.9 %shard_map.66 = bf16[384,256]{1,0:T(8,128)(2,1)S(1)} custom-call(bf16[3,10,26,16,128]{4,3,2,1,0:T(8,128)(2,1)S(1)} %shard_map.60.spread_ref, bf16[3456,256]{1,0:T(8,128)(2,1)S(1)} %bitcast.7, bf16[384,256]{1,0:T(8,128)(2,1)S(1)} %collective-permute-done.6.rest_1_.rest_0_), custom_call_target="tpu_custom_call" | custom-call | flops 1 | bytes 1 | tf_op jit(solution)/shard_map/pallas_call | solution.py:372
  36.8 0.8 %collective-permute-start.9 = (bf16[384,256]{1,0:T(8,128)(2,1)S(1)}, bf16[384,256]{1,0:T(8,128)(2,1)S(1)}, u32[]{:S(2)}, u32[]{:S(2)}) collective-permute-start(bf16[384,256]{1,0:T(8,128)(2,1)S(1)} %shard_map.66), channel_id=1, source_target_pairs={{0,12},{1,5},{4,8},{5,1},{8,4},{9,13},{12,0},{13,9},{2,14},{3,7},{... | collective-permute-start | bytes 589832 | tf_op jit(solution)/shard_map/ppermute | solution.py:417
  37.6 6.5 %collective-permute-done.7.rest_2_ = bf16[384,256]{1,0:T(8,128)(2,1)S(1)} collective-permute-done((bf16[384,256]{1,0:T(8,128)(2,1)S(1)}, bf16[384,256]{1,0:T(8,128)(2,1)S(1)}, u32[]{:S(2)}, u32[]{:S(2)}) %collective-permute-start.7) | collective-permute-done | bytes 196640 | tf_op jit(solution)/shard_map/ppermute | solution.py:409
  44.2 0.9 %shard_map.63.first_ref = f32[384,256]{1,0:T(8,128)S(1)} custom-call(bf16[3,10,26,16,128]{4,3,2,1,0:T(8,128)(2,1)S(1)} %shard_map.60.spread_ref, bf16[3456,256]{1,0:T(8,128)(2,1)S(1)} %bitcast.8, bf16[384,256]{1,0:T(8,128)(2,1)S(1)} %collective-permute-done.5.rest_0_, bf16[384,256]{1,0:T(8,128)(2,1)S(1)} %collective-permute-done.6.rest_1_.rest_0_, ...), custom_call_target="tpu_custom_call" | custom-call | flops 34359738368 | bytes 1 | tf_op jit(solution)/shard_map/pallas_call | solution.py:372
  45.1 0.9 %shard_map.65.second_ref = f32[384,256]{1,0:T(8,128)S(1)} custom-call(bf16[3,10,26,16,128]{4,3,2,1,0:T(8,128)(2,1)S(1)} %shard_map.60.spread_ref, bf16[3456,256]{1,0:T(8,128)(2,1)S(1)} %bitcast.9, bf16[1,256]{1,0:T(2,128)(2,1)S(1)} %reshape.22.rest_4_.rest_0_), custom_call_target="tpu_custom_call" | custom-call | flops 34359738368 | bytes 1 | tf_op jit(solution)/shard_map/pallas_call | solution.py:372
  46.0 0.7 %shard_map.64.whole_ref = bf16[768,256]{1,0:T(8,128)(2,1)} custom-call(f32[384,256]{1,0:T(8,128)S(1)} %shard_map.63.first_ref), custom_call_target="tpu_custom_call" | custom-call | tf_op jit(solution)/shard_map/pallas_call | solution.py:427
  46.7 2.3 %collective-permute-done.10.other_ref = bf16[384,256]{1,0:T(8,128)(2,1)S(1)} collective-permute-done((bf16[384,256]{1,0:T(8,128)(2,1)S(1)}, bf16[384,256]{1,0:T(8,128)(2,1)S(1)}, u32[]{:S(2)}, u32[]{:S(2)}) %collective-permute-start.10) | collective-permute-done | bytes 196640 | tf_op jit(solution)/shard_map/ppermute | solution.py:417
  49.0 0.4 collective-permute-done.9.one_ref
  49.4 0.7 %shard_map.68 = bf16[768,256]{1,0:T(8,128)(2,1)} custom-call(bf16[768,256]{1,0:T(8,128)(2,1)} %shard_map.64.whole_ref, f32[384,256]{1,0:T(8,128)S(1)} %shard_map.65.second_ref, bf16[384,256]{1,0:T(8,128)(2,1)S(1)} %collective-permute-done.9.one_ref, bf16[384,256]{1,0:T(8,128)(2,1)S(1)} %collective-permute-done.10.other_ref), custom_call_target="tpu_custom_call", output_to_operand_aliasing={{}: (0, {})} | custom-call | tf_op jit(solution)/shard_map/pallas_call | solution.py:435
  (13 shorter events, 0.2 us)
Async XLA Ops:
  0.0 1.0 %copy-start.1 = (bf16[2,24,16,256]{3,2,1,0:T(8,128)(2,1)S(1)}, bf16[2,24,16,256]{3,2,1,0:T(8,128)(2,1)}, u32[]{:S(2)}) copy-start(bf16[2,24,16,256]{3,2,1,0:T(8,128)(2,1)} %param.5) | copy-start | bytes 1179652
  1.2 15.9 %collective-permute-start = (bf16[784,128]{1,0:T(8,128)(2,1)S(1)}, bf16[784,128]{1,0:T(8,128)(2,1)S(1)}, u32[]{:S(2)}, u32[]{:S(2)}) collective-permute-start(bf16[784,128]{1,0:T(8,128)(2,1)S(1)} %get-tuple-element.18), channel_id=1, source_target_pairs={{0,4},{1,12},{4,0},{5,8},{9,13},{8,5},{13,9},{12,1},{2,6},{3,14},{... | collective-permute-start | bytes 602120 | tf_op jit(solution)/shard_map/ppermute | solution.py:342
  4.3 12.8 %collective-permute-start.2 = (bf16[784,128]{1,0:T(8,128)(2,1)S(1)}, bf16[784,128]{1,0:T(8,128)(2,1)S(1)}, u32[]{:S(2)}, u32[]{:S(2)}) collective-permute-start(bf16[784,128]{1,0:T(8,128)(2,1)S(1)} %get-tuple-element.21.same_ref), channel_id=1, source_target_pairs={{0,1},{1,9},{4,5},{5,13},{9,8},{8,0},{13,12},{12,4},{2,3},{3,11},{... | collective-permute-start | bytes 602120 | tf_op jit(solution)/shard_map/ppermute | solution.py:341
  7.8 11.9 %copy-start = (bf16[27,128,256]{2,1,0:T(8,128)(2,1)S(1)}, bf16[27,128,256]{2,1,0:T(8,128)(2,1)}, u32[]{:S(2)}) copy-start(bf16[27,128,256]{2,1,0:T(8,128)(2,1)} %param.8) | copy-start | bytes 5308420
  8.0 4.8 %collective-permute-start.1 = (bf16[64,128]{1,0:T(8,128)(2,1)S(1)}, bf16[64,128]{1,0:T(8,128)(2,1)S(1)}, u32[]{:S(2)}, u32[]{:S(2)}) collective-permute-start(bf16[64,128]{1,0:T(8,128)(2,1)S(1)} %get-tuple-element.19), channel_id=1, source_target_pairs={{0,6},{2,4},{1,14},{3,12},{4,2},{6,0},{5,10},{7,8},{9,15},{11,13},... | collective-permute-start | bytes 49160 | tf_op jit(solution)/shard_map/ppermute | solution.py:344
  8.5 8.6 %collective-permute-start.3 = (bf16[64,128]{1,0:T(8,128)(2,1)S(1)}, bf16[64,128]{1,0:T(8,128)(2,1)S(1)}, u32[]{:S(2)}, u32[]{:S(2)}) collective-permute-start(bf16[64,128]{1,0:T(8,128)(2,1)S(1)} %get-tuple-element.20), channel_id=1, source_target_pairs={{0,3},{2,1},{1,11},{3,9},{4,7},{6,5},{5,15},{7,13},{9,10},{11,8},{... | collective-permute-start | bytes 49160 | tf_op jit(solution)/shard_map/ppermute | solution.py:343
  17.1 1.8 %collective-permute-start.4 = (bf16[1696,128]{1,0:T(8,128)(2,1)S(1)}, bf16[1696,128]{1,0:T(8,128)(2,1)S(1)}, u32[]{:S(2)}, u32[]{:S(2)}) collective-permute-start(bf16[1696,128]{1,0:T(8,128)(2,1)S(1)} %shard_map.57), channel_id=1, source_target_pairs={{0,1},{1,0},{2,3},{3,2},{4,5},{5,4},{6,7},{7,6},{8,9},{9,8},{10,11... | collective-permute-start | bytes 1302536 | tf_op jit(solution)/shard_map/ppermute | solution.py:352
  20.6 14.3 %collective-permute-start.5 = (bf16[384,256]{1,0:T(8,128)(2,1)S(1)}, bf16[384,256]{1,0:T(8,128)(2,1)S(1)}, u32[]{:S(2)}, u32[]{:S(2)}) collective-permute-start(bf16[384,256]{1,0:T(8,128)(2,1)S(1)} %shard_map.59), channel_id=1, source_target_pairs={{0,12},{1,5},{4,8},{5,1},{8,4},{9,13},{12,0},{13,9},{2,14},{3,7},{... | collective-permute-start | bytes 589832 | tf_op jit(solution)/shard_map/ppermute | solution.py:407
  24.7 4.6 %copy-start.2 = (bf16[256]{0:T(256)(128)(2,1)S(1)}, bf16[256]{0:T(256)(128)(2,1)}, u32[]{:S(2)}) copy-start(bf16[256]{0:T(256)(128)(2,1)} %param.9) | copy-start | bytes 1540
  24.7 10.3 %collective-permute-start.6 = (bf16[384,256]{1,0:T(8,128)(2,1)S(1)}, bf16[384,256]{1,0:T(8,128)(2,1)S(1)}, u32[]{:S(2)}, u32[]{:S(2)}) collective-permute-start(bf16[384,256]{1,0:T(8,128)(2,1)S(1)} %shard_map.61), channel_id=1, source_target_pairs={{0,4},{1,13},{4,0},{5,9},{8,12},{9,5},{12,8},{13,1},{2,6},{3,15},{... | collective-permute-start | bytes 589832 | tf_op jit(solution)/shard_map/ppermute | solution.py:408
  26.6 17.6 %collective-permute-start.7 = (bf16[384,256]{1,0:T(8,128)(2,1)S(1)}, bf16[384,256]{1,0:T(8,128)(2,1)S(1)}, u32[]{:S(2)}, u32[]{:S(2)}) collective-permute-start(bf16[384,256]{1,0:T(8,128)(2,1)S(1)} %get-tuple-element.24), channel_id=1, source_target_pairs={{0,4},{1,9},{4,0},{5,13},{8,12},{9,1},{12,8},{13,5},{2,6},{3,11},{... | collective-permute-start | bytes 589832 | tf_op jit(solution)/shard_map/ppermute | solution.py:409
  28.5 15.7 %collective-permute-start.8 = (bf16[384,256]{1,0:T(8,128)(2,1)S(1)}, bf16[384,256]{1,0:T(8,128)(2,1)S(1)}, u32[]{:S(2)}, u32[]{:S(2)}) collective-permute-start(bf16[384,256]{1,0:T(8,128)(2,1)S(1)} %get-tuple-element.25), channel_id=1, source_target_pairs={{0,8},{1,5},{4,12},{5,1},{8,0},{9,13},{12,4},{13,9},{2,10},{3,7},{... | collective-permute-start | bytes 589832 | tf_op jit(solution)/shard_map/ppermute | solution.py:410
  35.8 13.1 %collective-permute-start.10 = (bf16[384,256]{1,0:T(8,128)(2,1)S(1)}, bf16[384,256]{1,0:T(8,128)(2,1)S(1)}, u32[]{:S(2)}, u32[]{:S(2)}) collective-permute-start(bf16[384,256]{1,0:T(8,128)(2,1)S(1)} %shard_map.67), channel_id=1, source_target_pairs={{0,4},{1,13},{4,0},{5,9},{8,12},{9,5},{12,8},{13,1},{2,6},{3,15},{... | collective-permute-start | bytes 589832 | tf_op jit(solution)/shard_map/ppermute | solution.py:417
  36.8 12.6 %collective-permute-start.9 = (bf16[384,256]{1,0:T(8,128)(2,1)S(1)}, bf16[384,256]{1,0:T(8,128)(2,1)S(1)}, u32[]{:S(2)}, u32[]{:S(2)}) collective-permute-start(bf16[384,256]{1,0:T(8,128)(2,1)S(1)} %shard_map.66), channel_id=1, source_target_pairs={{0,12},{1,5},{4,8},{5,1},{8,4},{9,13},{12,0},{13,9},{2,14},{3,7},{... | collective-permute-start | bytes 589832 | tf_op jit(solution)/shard_map/ppermute | solution.py:417
